TPU v7x, 32 devices: a whole 2x2x4 slice. The times are simulated.
32 devices in a mesh: dp: 8 (over z, y), fsdp: 4 (over x, core).
Axes of the slice: x: 2, y: 2, z: 4, core: 2. Of those that a mesh axis runs over, the one named last changes fastest.
Arguments:
- inputs: bfloat16 [32, 1024, 768], P(('dp', 'fsdp')), may hold values from -6 to 6
- encoded: bfloat16 [32, 512, 768], P(('dp', 'fsdp')), may hold values from -6 to 6
- out_grad: bfloat16 [32, 1024, 768], P(('dp', 'fsdp')), may hold values from -6 to 6
- prefix: int32 [32], P(('dp', 'fsdp')), may hold values from 102 to 512
- bucket_map: int32 [2, 1024], replicated, may hold values from 0 to 31, as said below
- bias_table: bfloat16 [32, 12], replicated, may hold values from -4 to 4
- norm_self: bfloat16 [768], P(('dp', 'fsdp')), may hold values from 0.099609375 to 1.8984375
- self_query: bfloat16 [768, 768], P(('dp', 'fsdp')), may hold values from -0.02734375 to 0.02734375
- self_key: bfloat16 [768, 768], P(('dp', 'fsdp')), may hold values from -0.21875 to 0.21875
- self_value: bfloat16 [768, 768], P(('dp', 'fsdp')), may hold values from -0.21875 to 0.21875
- self_out: bfloat16 [768, 768], P(('dp', 'fsdp')), may hold values from -1 to 1
- norm_cross: bfloat16 [768], P(('dp', 'fsdp')), may hold values from 0.099609375 to 1.8984375
- cross_query: bfloat16 [768, 768], P(('dp', 'fsdp')), may hold values from -0.02734375 to 0.02734375
- cross_key: bfloat16 [768, 768], P(('dp', 'fsdp')), may hold values from -0.21875 to 0.21875
- cross_value: bfloat16 [768, 768], P(('dp', 'fsdp')), may hold values from -0.21875 to 0.21875
- cross_out: bfloat16 [768, 768], P(('dp', 'fsdp')), may hold values from -1 to 1
- norm_feed: bfloat16 [768], P(('dp', 'fsdp')), may hold values from 0.099609375 to 1.8984375
- feed_gate: bfloat16 [768, 2048], P(('dp', 'fsdp')), may hold values from -0.21875 to 0.21875
- feed_up: bfloat16 [768, 2048], P(('dp', 'fsdp')), may hold values from -0.21875 to 0.21875
- feed_down: bfloat16 [2048, 768], P(('dp', 'fsdp')), may hold values from -0.125 to 0.125
Outputs:
- output: bfloat16 [32, 1024, 768], P(('dp', 'fsdp'))
- inputs_grad: float32 [32, 1024, 768], P(('dp', 'fsdp'))
- encoded_grad: float32 [32, 512, 768], P(('dp', 'fsdp'))
- table_grad: float32 [32, 12], replicated
- norm_self_grad: float32 [768], P(('dp', 'fsdp'))
- self_query_grad: float32 [768, 768], P(('dp', 'fsdp'))
- self_key_grad: float32 [768, 768], P(('dp', 'fsdp'))
- self_value_grad: float32 [768, 768], P(('dp', 'fsdp'))
- self_out_grad: float32 [768, 768], P(('dp', 'fsdp'))
- norm_cross_grad: float32 [768], P(('dp', 'fsdp'))
- cross_query_grad: float32 [768, 768], P(('dp', 'fsdp'))
- cross_key_grad: float32 [768, 768], P(('dp', 'fsdp'))
- cross_value_grad: float32 [768, 768], P(('dp', 'fsdp'))
- cross_out_grad: float32 [768, 768], P(('dp', 'fsdp'))
- norm_feed_grad: float32 [768], P(('dp', 'fsdp'))
- feed_gate_grad: float32 [768, 2048], P(('dp', 'fsdp'))
- feed_up_grad: float32 [768, 2048], P(('dp', 'fsdp'))
- feed_down_grad: float32 [2048, 768], P(('dp', 'fsdp'))
Inputs may be any that keep to these rules, and one draw needn't show every extreme that they name: bucket_map[0, d] is the bucket of a key d positions before its query; bucket_map[1, a] is the bucket within one half of a key a positions away; both rows never fall as the distance grows, equal the distance for the nearest 32/2 and 8 distances, and end at 31 and 15.
All inputs are finite; a program needn't handle non-finite values.
Results may differ from a plain program's by a relative error of at most 0.023.
Values may be sent and summed in bfloat16 or wider, within the bound.
A program may use at most 320 MiB of HBM per device.

v0:
```python
import jax
import jax.numpy as jnp
from jax import lax
from jax.sharding import PartitionSpec as P

DH = 64
NB = 32


negative = -1e30
lane_span = 128


def normalize(value, gain):
    scale = lax.rsqrt(jnp.mean(value * value, axis=-1, keepdims=True) + 1e-06)
    return value * scale * gain.astype(jnp.float32)


def norm_back(value, gain, grad):
    unused, pull = jax.vjp(normalize, value, gain.astype(jnp.float32))
    return pull(grad)


def activate(gate, upward):
    return jax.nn.gelu(gate, approximate=True) * upward


def project(left, right):
    return jnp.dot(left, right, preferred_element_type=jnp.float32)


def contract(left, right):
    return jnp.einsum("ta,tb->ab", left, right, preferred_element_type=jnp.float32)


def back_project(grad, weight):
    return jnp.einsum("tb,ab->ta", grad, weight, preferred_element_type=jnp.float32)


def bucket_ids(first_row, count, length, limit, marks):
    causal_marks, two_way_marks = marks
    query_place = first_row + lax.broadcasted_iota(jnp.int32, (count, length), 0)
    key_place = lax.broadcasted_iota(jnp.int32, (count, length), 1)
    offset = key_place - query_place
    behind = jnp.maximum(-offset, 0)
    apart = jnp.abs(offset)
    causal = jnp.zeros((count, length), jnp.int32)
    for number in range(NB - 1):
        causal = causal + (behind >= causal_marks[number]).astype(jnp.int32)
    two_way = NB // 2 * (offset > 0).astype(jnp.int32)
    for number in range(NB // 2 - 1):
        two_way = two_way + (apart >= two_way_marks[number]).astype(jnp.int32)
    inside = (query_place < limit) & (key_place < limit)
    allowed = (key_place <= query_place) | (key_place < limit)
    return (jnp.where(inside, two_way, causal), allowed)


def head_bias(ids, column):
    bucket_range = jnp.arange(NB, dtype=jnp.int32)
    return jnp.sum(jnp.where(ids[:, :, None] == bucket_range, column[None, None, :], 0.0), axis=-1)


def head_scores(rows, keys, ids, allowed, column):
    scores = jnp.einsum("rd,kd->rk", rows, keys, preferred_element_type=jnp.float32)
    if ids is None:
        return scores
    return jnp.where(allowed, scores + head_bias(ids, column), negative)


def attend_forward(query, keys, values, limit, marks, table, row_block):
    length = query.shape[0]
    groups = query.shape[1] // lane_span
    per_group = lane_span // DH
    lane = lax.broadcasted_iota(jnp.int32, (1, lane_span), 1) // DH
    zero = jnp.zeros((), jnp.bfloat16)
    columns = []
    lse_all = []
    for group in range(groups):
        query_group = query[:, group * lane_span : (group + 1) * lane_span]
        key_group = keys[:, group * lane_span : (group + 1) * lane_span]
        value_group = values[:, group * lane_span : (group + 1) * lane_span]
        mixed_rows = []
        lse_group = []
        for first_row in range(0, length, row_block):
            count = min(row_block, length - first_row)
            rows = query_group[first_row : first_row + count]
            ids, allowed = (None, None)
            if marks is not None:
                ids, allowed = bucket_ids(first_row, count, key_group.shape[0], limit, marks)
            mixed = jnp.zeros((count, lane_span), jnp.float32)
            lse_block = []
            for head in range(per_group):
                pick = lane == head
                column = None if marks is None else table[:, group * per_group + head]
                scores = head_scores(jnp.where(pick, rows, zero), key_group, ids, allowed, column)
                highest_score = jnp.max(scores, axis=-1, keepdims=True)
                weights = jnp.exp(scores - highest_score)
                total = jnp.sum(weights, axis=-1, keepdims=True)
                probs = (weights / total).astype(jnp.bfloat16)
                mixed = mixed + jnp.where(
                    pick, jnp.dot(probs, value_group, preferred_element_type=jnp.float32), 0.0
                )
                lse_block.append(highest_score + jnp.log(total))
            mixed_rows.append(mixed)
            lse_group.append(lse_block)
        columns.append(jnp.concatenate(mixed_rows, axis=0))
        lse_all.append(lse_group)
    return (jnp.concatenate(columns, axis=1).astype(jnp.bfloat16), lse_all)


def attend_backward(query, keys, values, grad_mixed, lse_all, limit, marks, table, row_block):
    length = query.shape[0]
    groups = query.shape[1] // lane_span
    per_group = lane_span // DH
    lane = lax.broadcasted_iota(jnp.int32, (1, lane_span), 1) // DH
    zero = jnp.zeros((), jnp.bfloat16)
    bucket_range = jnp.arange(NB, dtype=jnp.int32)
    query_columns = []
    key_columns = []
    value_columns = []
    table_columns = []
    for group in range(groups):
        query_group = query[:, group * lane_span : (group + 1) * lane_span]
        key_group = keys[:, group * lane_span : (group + 1) * lane_span]
        value_group = values[:, group * lane_span : (group + 1) * lane_span]
        grad_group = grad_mixed[:, group * lane_span : (group + 1) * lane_span]
        key_grad = jnp.zeros(key_group.shape, jnp.float32)
        value_grad = jnp.zeros(value_group.shape, jnp.float32)
        table_heads = [jnp.zeros((NB,), jnp.float32) for head in range(per_group)]
        query_rows = []
        for block, first_row in enumerate(range(0, length, row_block)):
            count = min(row_block, length - first_row)
            rows = query_group[first_row : first_row + count]
            grad_rows = grad_group[first_row : first_row + count]
            ids, allowed = (None, None)
            if marks is not None:
                ids, allowed = bucket_ids(first_row, count, key_group.shape[0], limit, marks)
            query_part = jnp.zeros((count, lane_span), jnp.float32)
            for head in range(per_group):
                pick = lane == head
                column = None if marks is None else table[:, group * per_group + head]
                head_rows = jnp.where(pick, rows, zero)
                head_grads = jnp.where(pick, grad_rows, zero)
                scores = head_scores(head_rows, key_group, ids, allowed, column)
                probs = jnp.exp(scores - lse_all[group][block][head])
                value_grad = value_grad + jnp.einsum(
                    "rk,rd->kd",
                    probs.astype(jnp.bfloat16),
                    head_grads,
                    preferred_element_type=jnp.float32,
                )
                grad_probs = jnp.einsum(
                    "rd,kd->rk", head_grads, value_group, preferred_element_type=jnp.float32
                )
                delta = jnp.sum(probs * grad_probs, axis=-1, keepdims=True)
                grad_scores = (probs * (grad_probs - delta)).astype(jnp.bfloat16)
                query_part = query_part + jnp.where(
                    pick, jnp.dot(grad_scores, key_group, preferred_element_type=jnp.float32), 0.0
                )
                key_grad = key_grad + jnp.einsum(
                    "rk,rd->kd", grad_scores, head_rows, preferred_element_type=jnp.float32
                )
                if marks is not None:
                    widened = grad_scores.astype(jnp.float32)
                    table_heads[head] = table_heads[head] + jnp.sum(
                        jnp.where(ids[:, :, None] == bucket_range, widened[:, :, None], 0.0),
                        axis=(0, 1),
                    )
            query_rows.append(query_part)
        query_columns.append(jnp.concatenate(query_rows, axis=0))
        key_columns.append(key_grad)
        value_columns.append(value_grad)
        table_columns.extend(table_heads)
    grads = (
        jnp.concatenate(query_columns, axis=1).astype(jnp.bfloat16),
        jnp.concatenate(key_columns, axis=1).astype(jnp.bfloat16),
        jnp.concatenate(value_columns, axis=1).astype(jnp.bfloat16),
    )
    if marks is None:
        return grads + (None,)
    return grads + (jnp.stack(table_columns, axis=1),)


def attend_all(query, keys, values, limits, marks, table, row_block):
    mixed_parts = []
    lse_parts = []
    for number, limit in enumerate(limits):
        mixed, lse = attend_forward(query, keys, values, limit, marks, table, row_block)
        mixed_parts.append(mixed)
        lse_parts.append(lse)
    return (mixed_parts[0], lse_parts)


def attend_back_all(query, keys, values, grad_mixed, lse_parts, limits, marks, table, row_block):
    query_parts = []
    key_parts = []
    value_parts = []
    table_total = None
    for number, limit in enumerate(limits):
        outcome = attend_backward(
            query, keys, values, grad_mixed, lse_parts[number], limit, marks, table, row_block
        )
        query_parts.append(outcome[0])
        key_parts.append(outcome[1])
        value_parts.append(outcome[2])
        if outcome[3] is not None:
            table_total = outcome[3]
    return (query_parts[0], key_parts[0], value_parts[0], table_total)


def per_device(
    inputs,
    encoded,
    out_grad,
    prefix,
    bucket_map,
    bias_table,
    norm_self,
    self_query,
    self_key,
    self_value,
    self_out,
    norm_cross,
    cross_query,
    cross_key,
    cross_value,
    cross_out,
    norm_feed,
    feed_gate,
    feed_up,
    feed_down,
):
    attention_full = (
        lax.all_gather(norm_self, ("dp", "fsdp"), axis=0, tiled=True),
        lax.all_gather(self_query, ("dp", "fsdp"), axis=0, tiled=True),
        lax.all_gather(self_key, ("dp", "fsdp"), axis=0, tiled=True),
        lax.all_gather(self_value, ("dp", "fsdp"), axis=0, tiled=True),
        lax.all_gather(self_out, ("dp", "fsdp"), axis=0, tiled=True),
        lax.all_gather(norm_cross, ("dp", "fsdp"), axis=0, tiled=True),
        lax.all_gather(cross_query, ("dp", "fsdp"), axis=0, tiled=True),
        lax.all_gather(cross_key, ("dp", "fsdp"), axis=0, tiled=True),
        lax.all_gather(cross_value, ("dp", "fsdp"), axis=0, tiled=True),
        lax.all_gather(cross_out, ("dp", "fsdp"), axis=0, tiled=True),
    )
    (
        gain_self,
        query_weight,
        key_weight,
        value_weight,
        out_weight,
        gain_cross,
        cross_query_full,
        cross_key_full,
        cross_value_full,
        cross_out_full,
    ) = attention_full
    seqs, length, width = inputs.shape
    source = encoded.shape[1]
    row_block = min(512, length)
    causal_marks = jnp.sum(
        (bucket_map[0][None, :] < jnp.arange(1, NB, dtype=jnp.int32)[:, None]).astype(jnp.int32),
        axis=1,
    )
    two_way_marks = jnp.sum(
        (bucket_map[1][None, :] < jnp.arange(1, NB // 2, dtype=jnp.int32)[:, None]).astype(
            jnp.int32
        ),
        axis=1,
    )
    marks = (causal_marks, two_way_marks)
    table = bias_table.astype(jnp.float32)
    limits = [prefix[0]]
    tokens = inputs.reshape(seqs * length, width).astype(jnp.float32)
    memory = encoded.reshape(seqs * source, width)
    normed_one = normalize(tokens, gain_self).astype(jnp.bfloat16)
    query_one = project(normed_one, query_weight).astype(jnp.bfloat16)
    key_one = project(normed_one, key_weight).astype(jnp.bfloat16)
    value_one = project(normed_one, value_weight).astype(jnp.bfloat16)
    mixed_one, sums_one = attend_all(query_one, key_one, value_one, limits, marks, table, row_block)
    first = tokens + project(mixed_one, out_weight)
    normed_two = normalize(first, gain_cross).astype(jnp.bfloat16)
    query_two = project(normed_two, cross_query_full).astype(jnp.bfloat16)
    key_two = project(memory, cross_key_full).astype(jnp.bfloat16)
    value_two = project(memory, cross_value_full).astype(jnp.bfloat16)
    mixed_two, sums_two = attend_all(query_two, key_two, value_two, limits, None, None, row_block)
    second = first + project(mixed_two, cross_out_full)
    feed_full = (
        lax.all_gather(norm_feed, ("dp", "fsdp"), axis=0, tiled=True),
        lax.all_gather(feed_gate, ("dp", "fsdp"), axis=0, tiled=True),
        lax.all_gather(feed_up, ("dp", "fsdp"), axis=0, tiled=True),
        lax.all_gather(feed_down, ("dp", "fsdp"), axis=0, tiled=True),
    )
    gain_feed, gate_weight, up_weight, down_weight = feed_full
    normed_three = normalize(second, gain_feed).astype(jnp.bfloat16)
    gate = project(normed_three, gate_weight)
    upward = project(normed_three, up_weight)
    hidden = activate(gate, upward).astype(jnp.bfloat16)
    result = second + project(hidden, down_weight)
    output = result.astype(jnp.bfloat16).reshape(seqs, length, width)
    feed_full = (
        lax.all_gather(norm_feed, ("dp", "fsdp"), axis=0, tiled=True),
        lax.all_gather(feed_gate, ("dp", "fsdp"), axis=0, tiled=True),
        lax.all_gather(feed_up, ("dp", "fsdp"), axis=0, tiled=True),
        lax.all_gather(feed_down, ("dp", "fsdp"), axis=0, tiled=True),
    )
    gain_feed, gate_weight, up_weight, down_weight = feed_full
    grad_out = out_grad.reshape(seqs * length, width)
    grad_down = contract(hidden, grad_out)
    grad_hidden = back_project(grad_out, down_weight)
    unused, pull = jax.vjp(activate, gate, upward)
    grad_gate, grad_up = pull(grad_hidden)
    grad_gate = grad_gate.astype(jnp.bfloat16)
    grad_up = grad_up.astype(jnp.bfloat16)
    grad_gate_weight = contract(normed_three, grad_gate)
    grad_up_weight = contract(normed_three, grad_up)
    grad_normed_three = back_project(grad_gate, gate_weight) + back_project(grad_up, up_weight)
    grad_second, grad_gain_feed = norm_back(second, gain_feed, grad_normed_three)
    grad_second = grad_second + grad_out.astype(jnp.float32)
    attention_full = (
        lax.all_gather(norm_self, ("dp", "fsdp"), axis=0, tiled=True),
        lax.all_gather(self_query, ("dp", "fsdp"), axis=0, tiled=True),
        lax.all_gather(self_key, ("dp", "fsdp"), axis=0, tiled=True),
        lax.all_gather(self_value, ("dp", "fsdp"), axis=0, tiled=True),
        lax.all_gather(self_out, ("dp", "fsdp"), axis=0, tiled=True),
        lax.all_gather(norm_cross, ("dp", "fsdp"), axis=0, tiled=True),
        lax.all_gather(cross_query, ("dp", "fsdp"), axis=0, tiled=True),
        lax.all_gather(cross_key, ("dp", "fsdp"), axis=0, tiled=True),
        lax.all_gather(cross_value, ("dp", "fsdp"), axis=0, tiled=True),
        lax.all_gather(cross_out, ("dp", "fsdp"), axis=0, tiled=True),
    )
    (
        gain_self,
        query_weight,
        key_weight,
        value_weight,
        out_weight,
        gain_cross,
        cross_query_full,
        cross_key_full,
        cross_value_full,
        cross_out_full,
    ) = attention_full
    branch_two = grad_second.astype(jnp.bfloat16)
    grad_cross_out = contract(mixed_two, branch_two)
    grad_mixed_two = back_project(branch_two, cross_out_full).astype(jnp.bfloat16)
    grad_query_two, grad_key_two, grad_value_two, unused_table = attend_back_all(
        query_two, key_two, value_two, grad_mixed_two, sums_two, limits, None, None, row_block
    )
    grad_cross_query = contract(normed_two, grad_query_two)
    grad_cross_key = contract(memory, grad_key_two)
    grad_cross_value = contract(memory, grad_value_two)
    encoded_grad = (
        back_project(grad_key_two, cross_key_full) + back_project(grad_value_two, cross_value_full)
    ).reshape(seqs, source, width)
    grad_first, grad_gain_cross = norm_back(
        first, gain_cross, back_project(grad_query_two, cross_query_full)
    )
    grad_first = grad_first + grad_second
    branch_one = grad_first.astype(jnp.bfloat16)
    grad_self_out = contract(mixed_one, branch_one)
    grad_mixed_one = back_project(branch_one, out_weight).astype(jnp.bfloat16)
    grad_query_one, grad_key_one, grad_value_one, table_part = attend_back_all(
        query_one, key_one, value_one, grad_mixed_one, sums_one, limits, marks, table, row_block
    )
    grad_self_query = contract(normed_one, grad_query_one)
    grad_self_key = contract(normed_one, grad_key_one)
    grad_self_value = contract(normed_one, grad_value_one)
    grad_normed_one = (
        back_project(grad_query_one, query_weight)
        + back_project(grad_key_one, key_weight)
        + back_project(grad_value_one, value_weight)
    )
    grad_tokens, grad_gain_self = norm_back(tokens, gain_self, grad_normed_one)
    inputs_grad = (grad_tokens + grad_first).reshape(seqs, length, width)
    table_grad = lax.psum(table_part, ("dp", "fsdp"))
    shares = (
        lax.psum_scatter(grad_gain_self, ("dp", "fsdp"), scatter_dimension=0, tiled=True),
        lax.psum_scatter(grad_self_query, ("dp", "fsdp"), scatter_dimension=0, tiled=True),
        lax.psum_scatter(grad_self_key, ("dp", "fsdp"), scatter_dimension=0, tiled=True),
        lax.psum_scatter(grad_self_value, ("dp", "fsdp"), scatter_dimension=0, tiled=True),
        lax.psum_scatter(grad_self_out, ("dp", "fsdp"), scatter_dimension=0, tiled=True),
        lax.psum_scatter(grad_gain_cross, ("dp", "fsdp"), scatter_dimension=0, tiled=True),
        lax.psum_scatter(grad_cross_query, ("dp", "fsdp"), scatter_dimension=0, tiled=True),
        lax.psum_scatter(grad_cross_key, ("dp", "fsdp"), scatter_dimension=0, tiled=True),
        lax.psum_scatter(grad_cross_value, ("dp", "fsdp"), scatter_dimension=0, tiled=True),
        lax.psum_scatter(grad_cross_out, ("dp", "fsdp"), scatter_dimension=0, tiled=True),
        lax.psum_scatter(grad_gain_feed, ("dp", "fsdp"), scatter_dimension=0, tiled=True),
        lax.psum_scatter(grad_gate_weight, ("dp", "fsdp"), scatter_dimension=0, tiled=True),
        lax.psum_scatter(grad_up_weight, ("dp", "fsdp"), scatter_dimension=0, tiled=True),
        lax.psum_scatter(grad_down, ("dp", "fsdp"), scatter_dimension=0, tiled=True),
    )
    attention_shares = shares[:10]
    feed_shares = shares[10:]
    return (
        output,
        inputs_grad,
        encoded_grad,
        table_grad,
        attention_shares[0],
        attention_shares[1],
        attention_shares[2],
        attention_shares[3],
        attention_shares[4],
        attention_shares[5],
        attention_shares[6],
        attention_shares[7],
        attention_shares[8],
        attention_shares[9],
        feed_shares[0],
        feed_shares[1],
        feed_shares[2],
        feed_shares[3],
    )


def solution(mesh):
    placed = (
        P(("dp", "fsdp"), None, None),
        P(("dp", "fsdp"), None, None),
        P(("dp", "fsdp"), None, None),
        P(("dp", "fsdp")),
        P(),
        P(),
        P(("dp", "fsdp")),
        P(("dp", "fsdp"), None),
        P(("dp", "fsdp"), None),
        P(("dp", "fsdp"), None),
        P(("dp", "fsdp"), None),
        P(("dp", "fsdp")),
        P(("dp", "fsdp"), None),
        P(("dp", "fsdp"), None),
        P(("dp", "fsdp"), None),
        P(("dp", "fsdp"), None),
        P(("dp", "fsdp")),
        P(("dp", "fsdp"), None),
        P(("dp", "fsdp"), None),
        P(("dp", "fsdp"), None),
    )
    return jax.shard_map(
        per_device,
        mesh=mesh,
        in_specs=placed,
        out_specs=(
            P(("dp", "fsdp"), None, None),
            P(("dp", "fsdp"), None, None),
            P(("dp", "fsdp"), None, None),
            P(),
            P(("dp", "fsdp")),
            P(("dp", "fsdp"), None),
            P(("dp", "fsdp"), None),
            P(("dp", "fsdp"), None),
            P(("dp", "fsdp"), None),
            P(("dp", "fsdp")),
            P(("dp", "fsdp"), None),
            P(("dp", "fsdp"), None),
            P(("dp", "fsdp"), None),
            P(("dp", "fsdp"), None),
            P(("dp", "fsdp")),
            P(("dp", "fsdp"), None),
            P(("dp", "fsdp"), None),
            P(("dp", "fsdp"), None),
        ),
        check_vma=False,
    )
```

profile of v0, /device:TPU:0, one launch (start us, length us, event | category | flops | bytes accessed | tf_op | source)
XLA Modules:
  0.0 1933.9 jit_solution(13731412751931353577)
XLA Ops:
  20.4 42.1 %all-reduce.7 = (bf16[768]{0:T(1024)(128)(2,1)S(1)}, bf16[768]{0:T(1024)(128)(2,1)S(1)}, bf16[768]{0:T(1024)(128)(2,1)S(1)}) all-reduce(bf16[768]{0:T(1024)(128)(2,1)S(1)} %dynamic-update-slice, bf16[768]{0:T(1024)(128)(2,1)S(1)} %dynamic-update-slice.1, ...), channel_id=1, replica_groups=mesh['dp'=8,'fsdp'=4] {'dp','fsdp'}, use_global_device_ids=true, to_apply=%add | all-reduce | flops 2304 | bytes 9216
  66.8 2.8 copy.68
  69.6 40.2 %add_select_fusion.25 = s32[512,1024]{1,0:T(8,128)} fusion(s32[]{:T(128)} %bitcast.50, s32[]{:T(128)} %bitcast.49, s32[]{:T(128)} %bitcast.48, s32[]{:T(128)} %bitcast.47, s32[]{:T(128)} %bitcast.46, s32[]{:T(128)} %bitcast.45, s32[]{:T(128)} %bitcast.44, s32[]{:T(128)} %bitcast.43, s32[]{:T(128)} %bitcast.42, s32[]{:T(128)} %bitcast.41, s32[]{:T(128)} %bitcast.40, ...), kind=kLoop, calls=%fused_computation.286 | loop fusion | flops 76021760 | bytes 2098872 | tf_op jit(solution)/shard_map/jit(_where)/select_n | solution.py:55
  109.8 39.1 %add_select_fusion.22 = s32[512,1024]{1,0:T(8,128)S(1)} fusion(s32[512]{0:T(512)S(1)} %iota_add_fusion, s32[]{:T(128)} %bitcast.50, s32[]{:T(128)} %bitcast.49, s32[]{:T(128)} %bitcast.48, s32[]{:T(128)} %bitcast.47, s32[]{:T(128)} %bitcast.46, s32[]{:T(128)} %bitcast.45, s32[]{:T(128)} %bitcast.44, s32[]{:T(128)} %bitcast.43, s32[]{:T(128)} %bitcast.42, ...), kind=kLoop, calls=%fused_computation.228 | loop fusion | flops 76021760 | bytes 2100920 | tf_op jit(solution)/shard_map/jit(_where)/select_n | solution.py:55
  148.9 299.9 %select_reduce_fusion.24 = (f32[512,1024]{1,0:T(8,128)}, f32[512,1024]{1,0:T(8,128)}, f32[512,1024]{1,0:T(8,128)}, f32[512,1024]{1,0:T(8,128)}, f32[512,1024]{1,...) fusion(f32[32]{0:T(128)S(1)} %get-tuple-element.197, ...), kind=kLoop, calls=%fused_computation.24 | loop fusion | flops 826277888 | bytes 54527488 | tf_op jit(solution)/shard_map/reduce_sum | solution.py:60
  448.8 3.3 convolution_convert_fusion.4
  452.2 3.9 convolution_convert_fusion.5
  459.7 3.4 convolution_convert_fusion.3
  559.9 5.0 multiply_reduce_fusion.5
  567.0 4.0 convolution_convert_fusion.2
  617.2 4.3 multiply_reduce_fusion.4
  624.8 9.2 fusion.1228
  634.1 9.4 fusion.1227
  643.5 16.9 multiply_convert_fusion
  660.4 6.8 fusion.1229
  667.3 4.6 multiply_reduce_fusion
  674.3 4.3 fusion.421
  678.6 3.8 convolution_convert_fusion.1
  791.5 5.0 multiply_reduce_fusion.1
  841.6 4.2 fusion.1151
  863.5 4.3 fusion.1152
  888.7 3.8 multiply_reduce_fusion.24
  892.5 3.5 multiply_reduce_fusion.23
  896.0 2.8 fusion.1141
  899.0 4.3 fusion.1166
  910.9 2.5 multiply_reduce_fusion.22
  925.7 4.3 fusion.418
  930.5 4.2 fusion.1154
  970.8 2.9 fusion.1146
  991.4 2.9 fusion.1144
  1012.7 2.9 fusion.1142
  1015.8 8.7 fusion.1233
  1024.6 8.8 fusion.1232
  1033.5 8.9 fusion.163
  1042.4 67.7 %select_reduce_fusion.1 = (f32[32]{0:T(128)S(1)}, f32[32]{0:T(128)S(1)}, f32[32]{0:T(128)S(1)}, f32[32]{0:T(128)S(1)}, f32[32]{0:T(128)S(1)}, /*index=5*/f32[32]...) fusion(f32[512,1024]{1,0:T(8,128)} %get-tuple-element.191, ...), kind=kLoop, calls=%fused_computation.1 | loop fusion | flops 419430016 | bytes 27264512 | tf_op jit(solution)/shard_map/reduce_sum | solution.py:165
  1110.1 67.5 %select_reduce_fusion = (f32[32]{0:T(128)S(1)}, f32[32]{0:T(128)S(1)}, f32[32]{0:T(128)S(1)}, f32[32]{0:T(128)S(1)}, f32[32]{0:T(128)S(1)}, /*index=5*/f32[32]{0...) fusion(f32[512,1024]{1,0:T(8,128)} %get-tuple-element.167, ...), kind=kLoop, calls=%fused_computation | loop fusion | flops 419430016 | bytes 27264512 | tf_op jit(solution)/shard_map/reduce_sum | solution.py:165
  1177.6 7.9 fusion.167
  1185.6 2.7 copy.76
  1188.3 3.0 fusion.1230
  1197.7 3.6 copy.77
  1201.5 40.4 %all-reduce.6 = (f32[32,12]{0,1:T(8,128)}, f32[768]{0:T(1024)S(1)}, f32[768]{0:T(1024)S(1)}, f32[768]{0:T(1024)S(1)}) all-reduce(f32[32,12]{0,1:T(8,128)S(1)} %stack.2, f32[768]{0:T(1024)S(1)} %get-tuple-element.76, f32[768]{0:T(1024)S(1)} %copy-done.442, f32[768]{0:T(1024)S(1)} %copy-done.441), channel_id=1, replica_groups=mesh['dp'=8,'fsdp'=4] {'dp','fsdp'}, use_global_device_ids=true, to_apply=%region_200.201 | all-reduce | flops 2688 | bytes 21504 | tf_op jit(solution)/shard_map/psum | solution.py:375
  1247.8 5.1 reduce-scatter.22.cloned.1.call-done
  1252.9 104.6 %reduce-scatter.16.cloned.1.call-done = f32[24,768]{1,0:T(8,128)} async-done(((f32[768,768]{1,0:T(8,128)}), f32[24,768]{1,0:T(8,128)}) %reduce-scatter.16.cloned.1.call-update) | async-done | bytes 73744 | tf_op jit(solution)/shard_map/reduce_scatter | solution.py:378
  1357.5 103.8 %reduce-scatter.18.cloned.1.call-done = f32[24,768]{1,0:T(8,128)} async-done(((f32[768,768]{1,0:T(8,128)}), f32[24,768]{1,0:T(8,128)}) %reduce-scatter.18.cloned.1.call-update) | async-done | bytes 73744 | tf_op jit(solution)/shard_map/reduce_scatter | solution.py:379
  1461.4 104.8 %reduce-scatter.20.cloned.1.call-done = f32[24,768]{1,0:T(8,128)} async-done(((f32[768,768]{1,0:T(8,128)}), f32[24,768]{1,0:T(8,128)}) %reduce-scatter.20.cloned.1.call-update) | async-done | bytes 73744 | tf_op jit(solution)/shard_map/reduce_scatter | solution.py:380
  1566.2 119.6 %reduce-scatter.30.cloned.1.call-done = f32[24,2048]{1,0:T(8,128)} async-done(((f32[768,2048]{1,0:T(8,128)}), f32[24,2048]{1,0:T(8,128)}) %reduce-scatter.30.cloned.1.call-update) | async-done | bytes 196624 | tf_op jit(solution)/shard_map/reduce_scatter | solution.py:389
  1685.7 120.9 %reduce-scatter.28.cloned.1.call-done = f32[24,2048]{1,0:T(8,128)} async-done(((f32[768,2048]{1,0:T(8,128)}), f32[24,2048]{1,0:T(8,128)}) %reduce-scatter.28.cloned.1.call-update) | async-done | bytes 196624 | tf_op jit(solution)/shard_map/reduce_scatter | solution.py:388
  1806.6 119.9 %reduce-scatter.32.cloned.1.call-done = f32[64,768]{1,0:T(8,128)} async-done(((f32[2048,768]{1,0:T(8,128)}), f32[64,768]{1,0:T(8,128)}) %reduce-scatter.32.cloned.1.call-update) | async-done | bytes 196624 | tf_op jit(solution)/shard_map/reduce_scatter | solution.py:390
  (1471 shorter events, 464.2 us)
Async XLA Ops:
  7.2 557.7 %copy-start = (bf16[1,512,768]{2,1,0:T(8,128)(2,1)S(1)}, bf16[1,512,768]{2,1,0:T(8,128)(2,1)}, u32[]{:S(2)}) copy-start(bf16[1,512,768]{2,1,0:T(8,128)(2,1)} %param.21) | copy-start | bytes 2359300
  7.2 441.6 %all-gather.14.cloned.1.call-start = ((), (), s32[]{:S(2)}) async-start(), calls=%async_computation.12 | async-start | bytes 1216512 | tf_op jit(solution)/shard_map/all_gather | solution.py:236
  7.9 444.2 %all-gather.12.cloned.1.call-start = ((), (), s32[]{:S(2)}) async-start(), calls=%async_computation.11 | async-start | bytes 1216512 | tf_op jit(solution)/shard_map/all_gather | solution.py:235
  8.7 451.0 %all-gather.16.cloned.1.call-start = ((), (), s32[]{:S(2)}) async-start(), calls=%async_computation.13 | async-start | bytes 1216512 | tf_op jit(solution)/shard_map/all_gather | solution.py:237
  9.4 550.5 %all-gather.18.cloned.1.call-start = ((), (), s32[]{:S(2)}) async-start(), calls=%async_computation.14 | async-start | bytes 1216512 | tf_op jit(solution)/shard_map/all_gather | solution.py:238
  10.0 554.9 %all-gather.22.cloned.1.call-start = ((), (), s32[]{:S(2)}) async-start(), calls=%async_computation.16 | async-start | bytes 1216512 | tf_op jit(solution)/shard_map/all_gather | solution.py:241
  10.6 556.4 %all-gather.20.cloned.1.call-start = ((), (), s32[]{:S(2)}) async-start(), calls=%async_computation.15 | async-start | bytes 1216512 | tf_op jit(solution)/shard_map/all_gather | solution.py:240
  11.2 561.7 %all-gather.24.cloned.1.call-start = ((), (), s32[]{:S(2)}) async-start(), calls=%async_computation.17 | async-start | bytes 1216512 | tf_op jit(solution)/shard_map/all_gather | solution.py:242
  11.9 605.3 %all-gather.26.cloned.1.call-start = ((), (), s32[]{:S(2)}) async-start(), calls=%async_computation.18 | async-start | bytes 1216512 | tf_op jit(solution)/shard_map/all_gather | solution.py:243
  12.7 612.2 %all-gather.30.cloned.1.call-start = ((), (), s32[]{:S(2)}) async-start(), calls=%async_computation.20 | async-start | bytes 3244032 | tf_op jit(solution)/shard_map/all_gather | solution.py:290
  13.4 620.7 %all-gather.28.cloned.1.call-start = ((), (), s32[]{:S(2)}) async-start(), calls=%async_computation.19 | async-start | bytes 3244032 | tf_op jit(solution)/shard_map/all_gather | solution.py:289
  14.0 629.5 %all-gather.32.cloned.1.call-start = ((), (), s32[]{:S(2)}) async-start(), calls=%async_computation.21 | async-start | bytes 3244032 | tf_op jit(solution)/shard_map/all_gather | solution.py:291
  14.7 1233.1 %reduce-scatter.26.cloned.1.call-start = ((), (), s32[]{:S(2)}) async-start(), calls=%async_computation.27 | async-start | bytes 2433024 | tf_op jit(solution)/shard_map/reduce_scatter | solution.py:386
  62.5 397.1 %copy-start.321 = (f32[768]{0:T(1024)}, f32[768]{0:T(1024)S(1)}, u32[]{:S(2)}) copy-start(f32[768]{0:T(1024)S(1)} %convert_element_type.943) | copy-start | bytes 9220
  62.5 504.5 %copy-start.412 = (f32[768]{0:T(1024)}, f32[768]{0:T(1024)S(1)}, u32[]{:S(2)}) copy-start(f32[768]{0:T(1024)S(1)} %convert_element_type.1067) | copy-start | bytes 9220
  66.8 43.0 %copy-start.326 = (f32[1024]{0:T(1024)}, f32[1024]{0:T(1024)S(1)}, u32[]{:S(2)}) copy-start(f32[1024]{0:T(1024)S(1)} %fusion.15) | copy-start | bytes 12292
  66.8 392.8 %copy-start.323 = (f32[1024]{0:T(1024)}, f32[1024]{0:T(1024)S(1)}, u32[]{:S(2)}) copy-start(f32[1024]{0:T(1024)S(1)} %fusion.946) | copy-start | bytes 12292
  148.9 299.9 %copy-start.183 = (s32[512,1024]{1,0:T(8,128)}, s32[512,1024]{1,0:T(8,128)S(1)}, u32[]{:S(2)}) copy-start(s32[512,1024]{1,0:T(8,128)S(1)} %add_select_fusion.22) | copy-start | bytes 6291460
  594.1 141.2 %copy-start.384 = (f32[512]{0:T(512)}, f32[512]{0:T(512)S(1)}, u32[]{:S(2)}) copy-start(f32[512]{0:T(512)S(1)} %log_add_fusion.31) | copy-start | bytes 6148
  616.8 121.2 %copy-start.386 = (f32[512]{0:T(512)}, f32[512]{0:T(512)S(1)}, u32[]{:S(2)}) copy-start(f32[512]{0:T(512)S(1)} %log_add_fusion.27) | copy-start | bytes 6148
  616.9 123.8 %copy-start.388 = (f32[512]{0:T(512)}, f32[512]{0:T(512)S(1)}, u32[]{:S(2)}) copy-start(f32[512]{0:T(512)S(1)} %log_add_fusion.23) | copy-start | bytes 6148
  616.9 82.2 %copy-start.410 = (f32[512]{0:T(512)}, f32[512]{0:T(512)S(1)}, u32[]{:S(2)}) copy-start(f32[512]{0:T(512)S(1)} %log_add_fusion.24) | copy-start | bytes 6148
  616.9 86.7 %copy-start.406 = (f32[512]{0:T(512)}, f32[512]{0:T(512)S(1)}, u32[]{:S(2)}) copy-start(f32[512]{0:T(512)S(1)} %log_add_fusion.28) | copy-start | bytes 6148
  617.0 67.8 %copy-start.408 = (f32[512]{0:T(512)}, f32[512]{0:T(512)S(1)}, u32[]{:S(2)}) copy-start(f32[512]{0:T(512)S(1)} %log_add_fusion.30) | copy-start | bytes 6148
  617.0 91.7 %copy-start.402 = (f32[512]{0:T(512)}, f32[512]{0:T(512)S(1)}, u32[]{:S(2)}) copy-start(f32[512]{0:T(512)S(1)} %log_add_fusion.32) | copy-start | bytes 6148
  617.0 70.0 %copy-start.404 = (f32[512]{0:T(512)}, f32[512]{0:T(512)S(1)}, u32[]{:S(2)}) copy-start(f32[512]{0:T(512)S(1)} %log_add_fusion.34) | copy-start | bytes 6148
  617.0 96.3 %copy-start.398 = (f32[512]{0:T(512)}, f32[512]{0:T(512)S(1)}, u32[]{:S(2)}) copy-start(f32[512]{0:T(512)S(1)} %log_add_fusion.36) | copy-start | bytes 6148
  617.1 72.1 %copy-start.400 = (f32[512]{0:T(512)}, f32[512]{0:T(512)S(1)}, u32[]{:S(2)}) copy-start(f32[512]{0:T(512)S(1)} %log_add_fusion.38) | copy-start | bytes 6148
  617.1 100.8 %copy-start.394 = (f32[512]{0:T(512)}, f32[512]{0:T(512)S(1)}, u32[]{:S(2)}) copy-start(f32[512]{0:T(512)S(1)} %log_add_fusion.40) | copy-start | bytes 6148
  617.1 74.3 %copy-start.396 = (f32[512]{0:T(512)}, f32[512]{0:T(512)S(1)}, u32[]{:S(2)}) copy-start(f32[512]{0:T(512)S(1)} %log_add_fusion.42) | copy-start | bytes 6148
  617.1 105.3 %copy-start.390 = (f32[512]{0:T(512)}, f32[512]{0:T(512)S(1)}, u32[]{:S(2)}) copy-start(f32[512]{0:T(512)S(1)} %log_add_fusion.44) | copy-start | bytes 6148
  617.1 76.5 %copy-start.392 = (f32[512]{0:T(512)}, f32[512]{0:T(512)S(1)}, u32[]{:S(2)}) copy-start(f32[512]{0:T(512)S(1)} %log_add_fusion.46) | copy-start | bytes 6148
  682.4 41.7 %copy-start.181 = (bf16[1024,768]{1,0:T(8,128)(2,1)}, bf16[1024,768]{1,0:T(8,128)(2,1)S(1)}, u32[]{:S(2)}) copy-start(bf16[1024,768]{1,0:T(8,128)(2,1)S(1)} %convolution_convert_fusion.1) | copy-start | bytes 4718596
  725.2 522.6 %reduce-scatter.36.cloned.1.call-start = ((), (), s32[]{:S(2)}) async-start(), calls=%async_computation.32 | async-start | bytes 2433024
  841.5 406.3 %reduce-scatter.34.cloned.1.call-start = ((), (), s32[]{:S(2)}) async-start(), calls=%async_computation.31 | async-start | bytes 2433024
  863.3 384.5 %reduce-scatter.24.cloned.1.call-start = ((), (), s32[]{:S(2)}) async-start(), calls=%async_computation.26 | async-start | bytes 2433024 | tf_op jit(solution)/shard_map/reduce_scatter | solution.py:383
  898.9 354.1 %reduce-scatter.22.cloned.1.call-start = ((), (), s32[]{:S(2)}) async-start(), calls=%async_computation.25 | async-start | bytes 2433024 | tf_op jit(solution)/shard_map/reduce_scatter | solution.py:381
  930.0 427.5 %reduce-scatter.16.cloned.1.call-start = ((), (), s32[]{:S(2)}) async-start(), calls=%async_computation.22 | async-start | bytes 2433024 | tf_op jit(solution)/shard_map/reduce_scatter | solution.py:378
  973.7 487.7 %reduce-scatter.18.cloned.1.call-start = ((), (), s32[]{:S(2)}) async-start(), calls=%async_computation.23 | async-start | bytes 2433024 | tf_op jit(solution)/shard_map/reduce_scatter | solution.py:379
  994.3 571.8 %reduce-scatter.20.cloned.1.call-start = ((), (), s32[]{:S(2)}) async-start(), calls=%async_computation.24 | async-start | bytes 2433024 | tf_op jit(solution)/shard_map/reduce_scatter | solution.py:380
  1015.6 670.1 %reduce-scatter.30.cloned.1.call-start = ((), (), s32[]{:S(2)}) async-start(), calls=%async_computation.29 | async-start | bytes 6488064 | tf_op jit(solution)/shard_map/reduce_scatter | solution.py:389
  1024.6 782.1 %reduce-scatter.28.cloned.1.call-start = ((), (), s32[]{:S(2)}) async-start(), calls=%async_computation.28 | async-start | bytes 6488064 | tf_op jit(solution)/shard_map/reduce_scatter | solution.py:388
  1033.4 893.1 %reduce-scatter.32.cloned.1.call-start = ((), (), s32[]{:S(2)}) async-start(), calls=%async_computation.30 | async-start | bytes 6488064 | tf_op jit(solution)/shard_map/reduce_scatter | solution.py:390
  1110.1 67.6 %copy-start.92 = (f32[1024,768]{0,1:T(8,128)S(1)}, f32[1024,768]{0,1:T(8,128)}, u32[]{:S(2)}) copy-start(f32[1024,768]{0,1:T(8,128)} %copy-done.90) | copy-start | bytes 9437188
  1197.7 45.9 %copy-start.283 = (bf16[512,768]{0,1:T(8,128)(2,1)S(1)}, bf16[512,768]{0,1:T(8,128)(2,1)}, u32[]{:S(2)}) copy-start(bf16[512,768]{0,1:T(8,128)(2,1)} %fusion.251) | copy-start | bytes 2359300
  1201.3 44.5 %copy-start.263 = (bf16[512,768]{0,1:T(8,128)(2,1)S(1)}, bf16[512,768]{0,1:T(8,128)(2,1)}, u32[]{:S(2)}) copy-start(bf16[512,768]{0,1:T(8,128)(2,1)} %copy-done.262) | copy-start | bytes 2359300
  1201.3 44.5 %copy-start.281 = (bf16[768,768]{1,0:T(8,128)(2,1)S(1)}, bf16[768,768]{1,0:T(8,128)(2,1)}, u32[]{:S(2)}) copy-start(bf16[768,768]{1,0:T(8,128)(2,1)} %all-gather.24.cloned.1.call-done) | copy-start | bytes 3538948
  1243.6 683.0 %copy-start.1 = (bf16[1,512,768]{2,1,0:T(8,128)(2,1)S(1)}, bf16[1,512,768]{2,1,0:T(8,128)(2,1)}, u32[]{:S(2)}) copy-start(bf16[1,512,768]{2,1,0:T(8,128)(2,1)} %param.21) | copy-start | bytes 2359300
  (424 other events, 1328.9 us)
Sparse Core Ops, SparseCore 0:
  10.9 56.8 all-gather.13
  70.7 52.9 all-gather.11
  126.6 52.9 all-gather.15
  182.3 52.9 all-gather.17
  238.1 52.9 all-gather.21
  293.8 52.9 all-gather.19
  349.7 52.9 all-gather.23
  405.6 52.9 all-gather.25
  461.5 57.8 all-gather.29
  522.1 57.7 all-gather.27
  582.8 57.7 all-gather.31
  725.3 98.7 reduce-scatter.25
  841.6 98.8 reduce-scatter.35
  946.2 98.0 reduce-scatter.33
  1050.8 97.9 reduce-scatter.23
  1154.5 98.3 reduce-scatter.21
  1259.5 97.9 reduce-scatter.15
  1363.2 98.0 reduce-scatter.17
  1468.1 98.0 reduce-scatter.19
  1572.2 113.4 reduce-scatter.29
  1692.9 113.7 reduce-scatter.27
  1812.8 113.6 reduce-scatter.31
where the time goes:
time: 1940 us; the launch traced here: 1930 us
  waiting for transfers between devices  686 us (35%)
  other arithmetic  630 us (32%)
  matrix products  427 us (22%)
  local copies, waits for them, and re-layouts  84.4 us (4%)
  blocking collectives  82.5 us (4%)
  between operations  21.3 us (1%)
    reduce_sum x1, other arithmetic, head_bias(): jnp.sum(jnp.where(ids[:, :, None] == bucket_range, column[None, None, :],...  300 us
    reduce_sum x2, other arithmetic, attend_backward(): jnp.sum(jnp.where(ids[:, :, None] == bucket_range, widened[:, :, None], 0...  135 us
    reduce_scatter x1, waiting for transfers between devices, per_device(): lax.psum_scatter(grad_gate_weight, ('dp', 'fsdp'), scatter_dimension=0, t...  121 us
    reduce_scatter x1, waiting for transfers between devices, per_device(): lax.psum_scatter(grad_down, ('dp', 'fsdp'), scatter_dimension=0, tiled=True)  120 us
    reduce_scatter x1, waiting for transfers between devices, per_device(): lax.psum_scatter(grad_up_weight, ('dp', 'fsdp'), scatter_dimension=0, til...  120 us
    reduce_scatter x1, waiting for transfers between devices, per_device(): lax.psum_scatter(grad_self_value, ('dp', 'fsdp'), scatter_dimension=0, ti...  105 us
    reduce_scatter x1, waiting for transfers between devices, per_device(): lax.psum_scatter(grad_self_query, ('dp', 'fsdp'), scatter_dimension=0, ti...  105 us
    reduce_scatter x1, waiting for transfers between devices, per_device(): lax.psum_scatter(grad_self_key, ('dp', 'fsdp'), scatter_dimension=0, tile...  104 us
  transfers between devices with their start and end apart: 22, of which 7 were waited for; matrix products, arithmetic and copies ran while one was open for 52% of the time, Pallas kernels for 0%

commit v1 on v0

v1 whole, which is shorter than its diff:
```python
import functools

import jax
import jax.numpy as jnp
import numpy as np
from jax import lax
from jax.experimental import pallas as pl
from jax.experimental.pallas import tpu as pltpu
from jax.sharding import PartitionSpec as P

DH = 64
NB = 32
PAIR = 2 * DH
SUB = 128
NEG = -1e30
F32 = jnp.float32
BF16 = jnp.bfloat16
AXES = ("dp", "fsdp")


def dot(a, b, ca=1, cb=0):
    return lax.dot_general(a, b, (((ca,), (cb,)), ((), ())), preferred_element_type=F32)


def exact_dot(a, b, ca=1, cb=0):
    return lax.dot_general(
        a,
        b,
        (((ca,), (cb,)), ((), ())),
        preferred_element_type=F32,
        precision=lax.Precision.HIGHEST,
    )


def rms(value):
    return lax.rsqrt(jnp.mean(value * value, axis=-1, keepdims=True) + 1e-06)


class Band:
    def __init__(self, length, reach):
        self.far = length
        self.reach = reach
        self.causal = length + reach
        self.two_way = 2 * reach
        self.width = self.causal + self.two_way
        self.query_zero = length - SUB
        self.query_zero_two = reach - SUB
        self.key_zero = reach - SUB
        self.key_zero_two = reach - SUB

    def distances(self, rows):
        lanes = np.arange(self.causal)
        lanes_two = np.arange(self.two_way)
        if rows == "queries":
            causal = self.query_zero - lanes
            two_way = self.query_zero_two - lanes_two
        else:
            causal = lanes - self.key_zero
            two_way = lanes_two - self.key_zero_two
        causal = (causal + self.reach - 1) % self.causal - (self.reach - 1) if rows == "queries" else (
            causal + self.reach
        ) % self.causal - self.reach
        two_way = (two_way + self.reach - 1) % self.two_way - (self.reach - 1) if rows == "queries" else (
            two_way + self.reach
        ) % self.two_way - self.reach
        return causal, two_way


def lane_buckets(bucket_map, band, rows):
    causal, two_way = band.distances(rows)
    top = bucket_map.shape[1] - 1
    one = bucket_map[0][np.clip(causal, 0, top)]
    one = jnp.where(causal < 0, -1, one)
    two = bucket_map[1][np.clip(np.abs(two_way), 0, top)] + (NB // 2) * (two_way < 0).astype(np.int32)
    return jnp.concatenate([one, two]).reshape(1, -1)


def one_hot(buckets_ref):
    width = buckets_ref.shape[1]
    return buckets_ref[...] == lax.broadcasted_iota(jnp.int32, (NB, width), 0)


def spread(row, width):
    return pltpu.roll(jnp.broadcast_to(row, (SUB, width)), 0, 1, stride=1, stride_axis=0)


def fold(band):
    width = band.shape[1]
    half = SUB // 2
    while half >= 8:
        band = band[:half] + pltpu.roll(band[half:], width - half, 1)
        half //= 2
    row = lax.broadcasted_iota(jnp.int32, band.shape, 0)
    for bit in (4, 2, 1):
        band = jnp.where((row & bit) != 0, pltpu.roll(band, width - bit, 1), band)
    return jnp.sum(band, axis=0, keepdims=True)


def fill_bands(head, bias_ref, band, causal_ref, two_ref):
    row = bias_ref[pl.ds(head, 1), :]
    causal_ref[...] = spread(row[:, : band.causal], band.causal)
    two_ref[...] = spread(row[:, band.causal :], band.two_way)


def bias_rows(table_ref, buckets_ref):
    hot = one_hot(buckets_ref)
    bias = dot(table_ref[...], jnp.where(hot, 1.0, 0.0).astype(BF16))
    return jnp.where(buckets_ref[...] < 0, NEG, bias)


def head_cols(head):
    group = head // 2
    return pl.ds(pl.multiple_of(group * PAIR, PAIR), PAIR), head % 2


def pick_lanes(half):
    return lax.broadcasted_iota(jnp.int32, (1, PAIR), 1) // DH == half


def soft_rows(scores):
    high = jnp.max(scores, axis=-1, keepdims=True)
    weights = jnp.exp(scores - high)
    total = jnp.sum(weights, axis=-1, keepdims=True)
    return weights.astype(BF16), total, high + jnp.log(total)


def store_head(mixed_ref, lse_ref, rows, cols, head, half, out, total, lse):
    pick = pick_lanes(half)
    mixed_ref[rows, cols] = jnp.where(pick, (out / total).astype(BF16), mixed_ref[rows, cols])
    lane = lax.broadcasted_iota(jnp.int32, (1, lse_ref.shape[1]), 1)
    lse_ref[rows, :] = jnp.where(lane == head, lse, lse_ref[rows, :])


def self_forward_head(head, limit, q_ref, k_ref, v_ref, causal_ref, two_ref, band, mixed_ref, lse_ref):
    length = q_ref.shape[0]
    cols, half = head_cols(head)
    pick = pick_lanes(half)
    block = 256
    for start in range(0, length, block):
        keys = max(start + block, band.reach)
        rows = pl.ds(start, block)
        query = jnp.where(pick, q_ref[rows, cols], 0)
        scores = dot(query, k_ref[pl.ds(0, keys), cols], 1, 1)
        parts = []
        for first in range(start, start + block, SUB):
            at = band.query_zero - first
            bias = causal_ref[:, at : at + keys]
            if start < band.reach:
                at = band.query_zero_two - first
                two = two_ref[:, at : at + keys]
                inside = (first + lax.broadcasted_iota(jnp.int32, (SUB, keys), 0) < limit) & (
                    lax.broadcasted_iota(jnp.int32, (SUB, keys), 1) < limit
                )
                bias = jnp.where(inside, two, bias)
            parts.append(bias)
        weights, total, lse = soft_rows(scores + jnp.concatenate(parts, axis=0))
        out = dot(weights, v_ref[pl.ds(0, keys), cols])
        store_head(mixed_ref, lse_ref, rows, cols, head, half, out, total, lse)


def cross_forward_head(head, q_ref, k_ref, v_ref, mixed_ref, lse_ref):
    length = q_ref.shape[0]
    cols, half = head_cols(head)
    pick = pick_lanes(half)
    block = 256
    for start in range(0, length, block):
        rows = pl.ds(start, block)
        query = jnp.where(pick, q_ref[rows, cols], 0)
        weights, total, lse = soft_rows(dot(query, k_ref[:, cols], 1, 1))
        out = dot(weights, v_ref[:, cols])
        store_head(mixed_ref, lse_ref, rows, cols, head, half, out, total, lse)


def row_blocks(count, block, step):
    @pl.loop(0, count // block)
    def _(index):
        step(pl.ds(pl.multiple_of(index * block, block), block))


def forward_kernel(
    limit_ref, tokens_ref, memory_ref, gains_ref, table_ref, buckets_ref,
    wq_ref, wk_ref, wv_ref, wo_ref, cq_ref, ck_ref, cv_ref, co_ref,
    q1_ref, k1_ref, v1_ref, mixed1_ref, lse1_ref, first_ref,
    q2_ref, k2_ref, v2_ref, mixed2_ref, lse2_ref, second_ref,
    bias_ref, causal_ref, two_ref,
    *, band, heads,
):
    length = tokens_ref.shape[0]
    bias_ref[...] = bias_rows(table_ref, buckets_ref)

    def project_self(rows):
        value = tokens_ref[rows, :].astype(F32)
        normed = (value * rms(value) * gains_ref[0:1, :]).astype(BF16)
        q1_ref[rows, :] = dot(normed, wq_ref[...]).astype(BF16)
        k1_ref[rows, :] = dot(normed, wk_ref[...]).astype(BF16)
        v1_ref[rows, :] = dot(normed, wv_ref[...]).astype(BF16)

    row_blocks(length, 256, project_self)
    lse1_ref[...] = jnp.zeros_like(lse1_ref)
    lse2_ref[...] = jnp.zeros_like(lse2_ref)
    mixed1_ref[...] = jnp.zeros_like(mixed1_ref)
    mixed2_ref[...] = jnp.zeros_like(mixed2_ref)

    @pl.loop(0, heads)
    def _(head):
        fill_bands(head, bias_ref, band, causal_ref, two_ref)
        self_forward_head(head, limit_ref[0], q1_ref, k1_ref, v1_ref, causal_ref, two_ref, band, mixed1_ref, lse1_ref)

    def project_memory(rows):
        k2_ref[rows, :] = dot(memory_ref[rows, :], ck_ref[...]).astype(BF16)
        v2_ref[rows, :] = dot(memory_ref[rows, :], cv_ref[...]).astype(BF16)

    row_blocks(memory_ref.shape[0], 256, project_memory)

    def project_cross(rows):
        value = tokens_ref[rows, :].astype(F32) + dot(mixed1_ref[rows, :], wo_ref[...])
        first_ref[rows, :] = value
        normed = (value * rms(value) * gains_ref[1:2, :]).astype(BF16)
        q2_ref[rows, :] = dot(normed, cq_ref[...]).astype(BF16)

    row_blocks(length, 256, project_cross)

    @pl.loop(0, heads)
    def _(head):
        cross_forward_head(head, q2_ref, k2_ref, v2_ref, mixed2_ref, lse2_ref)

    def project_second(rows):
        second_ref[rows, :] = first_ref[rows, :] + dot(mixed2_ref[rows, :], co_ref[...])

    row_blocks(length, 256, project_second)


def norm_back_rows(value, gain, grad):
    scale = rms(value)
    unit = value * scale
    scaled = grad * gain
    back = scale * (scaled - unit * jnp.mean(scaled * unit, axis=-1, keepdims=True))
    return back, jnp.sum(grad * unit, axis=0, keepdims=True)


GELU_A = 0.7978845608028654
GELU_B = 0.044715


def feed_kernel(
    second_ref, gout_ref, gains_ref, gate_ref, up_ref, down_ref,
    output_ref, gsecond_ref, ggain_ref, dgate_ref, dup_ref, ddown_ref,
    normed_ref, flipped_ref, out_ref, back_ref, hidden_ref, ggate_ref, gup_ref,
):
    step = pl.program_id(0)
    length = second_ref.shape[0]
    block = 256

    @pl.when(step == 0)
    def _():
        def prepare(rows):
            value = second_ref[rows, :]
            normed = (value * rms(value) * gains_ref[2:3, :]).astype(BF16)
            normed_ref[rows, :] = normed
            flipped_ref[:, rows] = normed.T
            out_ref[rows, :] = value
            back_ref[rows, :] = jnp.zeros_like(value)

        row_blocks(length, block, prepare)

    def rows_step(rows):
        normed = normed_ref[rows, :]
        gate = dot(normed, gate_ref[...])
        upward = dot(normed, up_ref[...])
        square = gate * gate
        bend = jnp.tanh(GELU_A * gate * (1.0 + GELU_B * square))
        half = 0.5 * (1.0 + bend)
        active = gate * half
        hidden = (active * upward).astype(BF16)
        hidden_ref[rows, :] = hidden
        out_ref[rows, :] += dot(hidden, down_ref[...])
        ghidden = dot(gout_ref[rows, :], down_ref[...], 1, 1)
        slope = half + 0.5 * gate * (1.0 - bend * bend) * (GELU_A * (1.0 + 3.0 * GELU_B * square))
        ggate = (ghidden * upward * slope).astype(BF16)
        gup = (ghidden * active).astype(BF16)
        ggate_ref[rows, :] = ggate
        gup_ref[rows, :] = gup
        back_ref[rows, :] += dot(ggate, gate_ref[...], 1, 1) + dot(gup, up_ref[...], 1, 1)

    row_blocks(length, block, rows_step)
    ddown_ref[...] = dot(hidden_ref[...].T, gout_ref[...]).astype(BF16)
    dgate_ref[...] = dot(flipped_ref[...], ggate_ref[...]).astype(BF16)
    dup_ref[...] = dot(flipped_ref[...], gup_ref[...]).astype(BF16)

    @pl.when(step == pl.num_programs(0) - 1)
    def _():
        ggain_ref[...] = jnp.zeros_like(ggain_ref)

        def finish(rows):
            output_ref[rows, :] = out_ref[rows, :].astype(BF16)
            back, ggain = norm_back_rows(second_ref[rows, :], gains_ref[2:3, :], back_ref[rows, :])
            gsecond_ref[rows, :] = back + gout_ref[rows, :].astype(F32)
            ggain_ref[0:1, :] += ggain

        row_blocks(length, block, finish)


def backward_head_prepare(group_cols, gm_ref, mixed_ref, delta_ref):
    product = (gm_ref[:, group_cols].astype(F32) * mixed_ref[:, group_cols].astype(F32)).T
    delta_ref[0:1, :] = jnp.sum(product[:DH], axis=0, keepdims=True)
    delta_ref[1:2, :] = jnp.sum(product[DH:], axis=0, keepdims=True)


def backward_block(key_rows, cols, half, start, bias, q_ref, k_ref, v_ref, gm_ref, lse, delta, gk_ref, gv_ref, gqt_ref):
    length = q_ref.shape[0]
    pick = pick_lanes(half)
    queries = pl.ds(start, length - start)
    query = jnp.where(pick, q_ref[queries, cols], 0)
    grad = jnp.where(pick, gm_ref[queries, cols], 0)
    keys = k_ref[key_rows, cols]
    scores = dot(keys, query, 1, 1)
    if bias is not None:
        scores = scores + bias
    probs = jnp.exp(scores - lse[:, start:])
    gv = dot(probs.astype(BF16), grad)
    gprobs = dot(v_ref[key_rows, cols], grad, 1, 1)
    gscores = probs * (gprobs - delta[:, start:])
    low = gscores.astype(BF16)
    gk = dot(low, query)
    gk_ref[key_rows, cols] = jnp.where(pick, gk.astype(BF16), gk_ref[key_rows, cols])
    gv_ref[key_rows, cols] = jnp.where(pick, gv.astype(BF16), gv_ref[key_rows, cols])
    gqt_ref[:, queries] += dot(jnp.where(pick, keys, 0).T, low)
    return gscores


def self_backward_head(
    head, limit, q_ref, k_ref, v_ref, gm_ref, mixed_ref, lse_ref, delta_ref, causal_ref, two_ref, band,
    gk_ref, gv_ref, gqt_ref, causal_sum_ref, two_sum_ref,
):
    length = q_ref.shape[0]
    cols, half = head_cols(head)
    lse = lse_ref[pl.ds(head, 1), :]
    delta = delta_ref[pl.ds(half, 1), :]
    reach = band.reach
    block = 256
    for first in range(0, length, block):
        start = 0 if first < reach else first
        count = length - start
        parts = []
        for key in range(first, first + block, SUB):
            at = band.key_zero - key + start
            bias = causal_ref[:, at : at + count]
            if first < reach:
                at = band.key_zero_two - key
                two = two_ref[:, at : at + reach]
                inside = (key + lax.broadcasted_iota(jnp.int32, (SUB, reach), 0) < limit) & (
                    lax.broadcasted_iota(jnp.int32, (SUB, reach), 1) < limit
                )
                bias = jnp.concatenate([jnp.where(inside, two, bias[:, :reach]), bias[:, reach:]], axis=1)
            parts.append(bias)
        gscores = backward_block(
            pl.ds(first, block), cols, half, start, jnp.concatenate(parts, axis=0),
            q_ref, k_ref, v_ref, gm_ref, lse, delta, gk_ref, gv_ref, gqt_ref,
        )
        for key in range(first, first + block, SUB):
            part = gscores[key - first : key - first + SUB]
            at = band.key_zero - key + start
            if first < reach:
                inside = (key + lax.broadcasted_iota(jnp.int32, (SUB, reach), 0) < limit) & (
                    lax.broadcasted_iota(jnp.int32, (SUB, reach), 1) < limit
                )
                head_part = part[:, :reach]
                at_two = band.key_zero_two - key
                two_sum_ref[:, at_two : at_two + reach] += jnp.where(inside, head_part, 0.0)
                causal_sum_ref[:, at : at + reach] += jnp.where(inside, 0.0, head_part)
                causal_sum_ref[:, at + reach : at + count] += part[:, reach:]
            else:
                causal_sum_ref[:, at : at + count] += part


def cross_backward_kernel(
    gsecond_ref, first_ref, memory_ref, gains_ref, q_ref, k_ref, v_ref, mixed1_ref, mixed2_ref, lse_ref,
    wo_ref, cq_ref, ck_ref, cv_ref, co_ref,
    gmem_ref, gfirst_ref, gm1_ref, ggain_ref, dwo_ref, dcq_ref, dck_ref, dcv_ref, dco_ref,
    gm_ref, branch_ref, flipped_ref, lse_rows_ref, delta_ref, gq_ref, gk_ref, gv_ref, gqt_ref,
    *, heads,
):
    length, width = first_ref.shape
    source = memory_ref.shape[0]
    block = 256

    def prepare(rows):
        branch = gsecond_ref[rows, :].astype(BF16)
        branch_ref[rows, :] = branch
        gm_ref[rows, :] = dot(branch, co_ref[...], 1, 1).astype(BF16)
        flipped_ref[:, rows] = mixed2_ref[rows, :].T

    row_blocks(length, block, prepare)

    def out_grad(rows):
        dco_ref[rows, :] = dot(flipped_ref[rows, :], branch_ref[...]).astype(BF16)

    row_blocks(width, block, out_grad)
    lse_rows_ref[...] = lse_ref[...].T
    gk_ref[...] = jnp.zeros_like(gk_ref)
    gv_ref[...] = jnp.zeros_like(gv_ref)

    @pl.loop(0, heads // 2)
    def _(group):
        cols = pl.ds(pl.multiple_of(group * PAIR, PAIR), PAIR)
        backward_head_prepare(cols, gm_ref, mixed2_ref, delta_ref)
        gqt_ref[...] = jnp.zeros_like(gqt_ref)

        @pl.loop(0, 2)
        def _(half):
            head = group * 2 + half
            for first in range(0, source, block):
                backward_block(
                    pl.ds(first, block), cols, half, 0, None, q_ref, k_ref, v_ref, gm_ref,
                    lse_rows_ref[pl.ds(head, 1), :], delta_ref[pl.ds(half, 1), :], gk_ref, gv_ref, gqt_ref,
                )

        gq_ref[:, cols] = gqt_ref[...].T.astype(BF16)

    def memory_grad(rows):
        gmem_ref[rows, :] = dot(gk_ref[rows, :], ck_ref[...], 1, 1) + dot(gv_ref[rows, :], cv_ref[...], 1, 1)
        flipped_ref[:, rows] = memory_ref[rows, :].T

    row_blocks(source, block, memory_grad)

    def memory_weights(rows):
        flipped = flipped_ref[rows, :source]
        dck_ref[rows, :] = dot(flipped, gk_ref[...]).astype(BF16)
        dcv_ref[rows, :] = dot(flipped, gv_ref[...]).astype(BF16)

    row_blocks(width, block, memory_weights)
    ggain_ref[...] = jnp.zeros_like(ggain_ref)

    def first_grad(rows):
        value = first_ref[rows, :]
        flipped_ref[:, rows] = (value * rms(value) * gains_ref[1:2, :]).astype(BF16).T
        back, ggain = norm_back_rows(value, gains_ref[1:2, :], dot(gq_ref[rows, :], cq_ref[...], 1, 1))
        ggain_ref[0:1, :] += ggain
        gfirst = back + gsecond_ref[rows, :]
        gfirst_ref[rows, :] = gfirst
        branch = gfirst.astype(BF16)
        branch_ref[rows, :] = branch
        gm1_ref[rows, :] = dot(branch, wo_ref[...], 1, 1).astype(BF16)

    row_blocks(length, block, first_grad)

    def query_weights(rows):
        dcq_ref[rows, :] = dot(flipped_ref[rows, :], gq_ref[...]).astype(BF16)

    row_blocks(width, block, query_weights)

    def flip_mixed(rows):
        flipped_ref[:, rows] = mixed1_ref[rows, :].T

    row_blocks(length, block, flip_mixed)

    def out_weights(rows):
        dwo_ref[rows, :] = dot(flipped_ref[rows, :], branch_ref[...]).astype(BF16)

    row_blocks(width, block, out_weights)


def self_backward_kernel(
    limit_ref, tokens_ref, gains_ref, table_ref, buckets_ref, q_ref, k_ref, v_ref, mixed_ref, lse_ref, gm_ref, gfirst_ref,
    wq_ref, wk_ref, wv_ref,
    gtokens_ref, ggain_ref, gtable_ref, dwq_ref, dwk_ref, dwv_ref,
    bias_ref, causal_ref, two_ref, flipped_ref, lse_rows_ref, delta_ref, gq_ref, gk_ref, gv_ref, gqt_ref,
    causal_sum_ref, two_sum_ref, sums_ref,
    *, band, heads,
):
    length, width = tokens_ref.shape
    block = 256
    bias_ref[...] = bias_rows(table_ref, buckets_ref)
    lse_rows_ref[...] = lse_ref[...].T
    gk_ref[...] = jnp.zeros_like(gk_ref)
    gv_ref[...] = jnp.zeros_like(gv_ref)
    sums_ref[...] = jnp.zeros_like(sums_ref)

    @pl.loop(0, heads // 2)
    def _(group):
        cols = pl.ds(pl.multiple_of(group * PAIR, PAIR), PAIR)
        backward_head_prepare(cols, gm_ref, mixed_ref, delta_ref)
        gqt_ref[...] = jnp.zeros_like(gqt_ref)

        @pl.loop(0, 2)
        def _(half):
            head = group * 2 + half
            fill_bands(head, bias_ref, band, causal_ref, two_ref)
            causal_sum_ref[...] = jnp.zeros_like(causal_sum_ref)
            two_sum_ref[...] = jnp.zeros_like(two_sum_ref)
            self_backward_head(
                head, limit_ref[0], q_ref, k_ref, v_ref, gm_ref, mixed_ref, lse_rows_ref, delta_ref,
                causal_ref, two_ref, band, gk_ref, gv_ref, gqt_ref, causal_sum_ref, two_sum_ref,
            )
            sums_ref[pl.ds(head, 1), : band.causal] = fold(causal_sum_ref[...])
            sums_ref[pl.ds(head, 1), band.causal :] = fold(two_sum_ref[...])

        gq_ref[:, cols] = gqt_ref[...].T.astype(BF16)

    hot = jnp.where(one_hot(buckets_ref), 1.0, 0.0)
    gtable_ref[...] = exact_dot(sums_ref[...], hot, 1, 1)
    ggain_ref[...] = jnp.zeros_like(ggain_ref)

    def tokens_grad(rows):
        value = tokens_ref[rows, :].astype(F32)
        flipped_ref[:, rows] = (value * rms(value) * gains_ref[0:1, :]).astype(BF16).T
        grad = dot(gq_ref[rows, :], wq_ref[...], 1, 1)
        grad += dot(gk_ref[rows, :], wk_ref[...], 1, 1)
        grad += dot(gv_ref[rows, :], wv_ref[...], 1, 1)
        back, ggain = norm_back_rows(value, gains_ref[0:1, :], grad)
        ggain_ref[0:1, :] += ggain
        gtokens_ref[rows, :] = back + gfirst_ref[rows, :]

    row_blocks(length, block, tokens_grad)

    def weights(rows):
        flipped = flipped_ref[rows, :]
        dwq_ref[rows, :] = dot(flipped, gq_ref[...]).astype(BF16)
        dwk_ref[rows, :] = dot(flipped, gk_ref[...]).astype(BF16)
        dwv_ref[rows, :] = dot(flipped, gv_ref[...]).astype(BF16)

    row_blocks(width, block, weights)


def vmem(*shapes):
    return [pltpu.VMEM(shape, dtype) for shape, dtype in shapes]


def params(**kw):
    return pltpu.CompilerParams(vmem_limit_bytes=60 * 1024 * 1024, **kw)


def weight_block(number, width):
    return pl.BlockSpec((width, width), lambda *_: (0, number))


def per_device(
    inputs, encoded, out_grad, prefix, bucket_map, bias_table,
    norm_self, self_query, self_key, self_value, self_out,
    norm_cross, cross_query, cross_key, cross_value, cross_out,
    norm_feed, feed_gate, feed_up, feed_down,
):
    seqs, length, width = inputs.shape
    source = encoded.shape[1]
    heads = bias_table.shape[1]
    ff = feed_gate.shape[1]
    band = Band(length, length // 2)
    tokens = inputs.reshape(length, width)
    memory = encoded.reshape(source, width)
    gout = out_grad.reshape(length, width)
    lanes = 16
    table = jnp.pad(bias_table.T, ((0, lanes - heads), (0, 0)))
    query_buckets = lane_buckets(bucket_map, band, "queries")
    key_buckets = lane_buckets(bucket_map, band, "keys")

    attention = lax.all_gather(
        jnp.concatenate(
            [self_query, self_key, self_value, self_out, cross_query, cross_key, cross_value, cross_out], axis=1
        ),
        AXES, axis=0, tiled=True,
    )
    feed = lax.all_gather(jnp.concatenate([feed_gate, feed_up], axis=1), AXES, axis=0, tiled=True)
    down = lax.all_gather(feed_down, AXES, axis=0, tiled=True)
    gains = lax.all_gather(jnp.stack([norm_self, norm_cross, norm_feed]), AXES, axis=1, tiled=True)
    gains = jnp.pad(gains.astype(F32), ((0, 5), (0, 0)))

    whole = pl.BlockSpec(memory_space=pltpu.VMEM)
    scalar = pl.BlockSpec(memory_space=pltpu.SMEM)

    def weights(*numbers):
        return [weight_block(number, width) for number in numbers]

    def full(shape):
        return pl.BlockSpec(shape, lambda *_: (0,) * len(shape))

    def like(shape, dtype):
        return jax.ShapeDtypeStruct(shape, dtype)

    act = like((length, width), BF16)
    mem = like((source, width), BF16)
    act32 = like((length, width), F32)
    lse_shape = like((length, SUB), F32)
    outs = [act, act, act, act, lse_shape, act32, act, mem, mem, act, lse_shape, act32]
    q1, k1, v1, mixed1, lse1, first, q2, k2, v2, mixed2, lse2, second = pl.pallas_call(
        functools.partial(forward_kernel, band=band, heads=heads),
        out_shape=outs,
        grid=(1,),
        in_specs=[scalar] + [full(a.shape) for a in (tokens, memory, gains, table, query_buckets)] + weights(*range(8)),
        out_specs=[full(o.shape) for o in outs],
        scratch_shapes=vmem(
            ((lanes, band.width), F32), ((SUB, band.causal), F32), ((SUB, band.two_way), F32)
        ),
        compiler_params=params(),
        name="forward",
    )(prefix, tokens, memory, gains, table, query_buckets, *([attention] * 8))

    fblock = 256
    ggain_shape = like((8, width), F32)
    feed_out = [
        act, act32, ggain_shape, like((width, ff), BF16), like((width, ff), BF16), like((ff, width), BF16)
    ]
    output, gsecond, ggain_feed, dgate, dup, ddown = pl.pallas_call(
        feed_kernel,
        out_shape=feed_out,
        grid=(ff // fblock,),
        in_specs=[full(second.shape), full(gout.shape), full(gains.shape)]
        + [
            pl.BlockSpec((width, fblock), lambda i: (0, i)),
            pl.BlockSpec((width, fblock), lambda i: (0, i + ff // fblock)),
            pl.BlockSpec((fblock, width), lambda i: (i, 0)),
        ],
        out_specs=[full(o.shape) for o in feed_out[:3]]
        + [
            pl.BlockSpec((width, fblock), lambda i: (0, i)),
            pl.BlockSpec((width, fblock), lambda i: (0, i)),
            pl.BlockSpec((fblock, width), lambda i: (i, 0)),
        ],
        scratch_shapes=vmem(
            ((length, width), BF16), ((width, length), BF16), ((length, width), F32), ((length, width), F32),
            ((length, fblock), BF16), ((length, fblock), BF16), ((length, fblock), BF16),
        ),
        compiler_params=params(),
        name="feed",
    )(second, gout, gains, feed, feed, down)

    square = like((width, width), BF16)
    cross_out_shapes = [like((source, width), F32), act32, act, ggain_shape] + [square] * 5
    cross_in = (gsecond, first, memory, gains, q2, k2, v2, mixed1, mixed2, lse2)
    gmem, gfirst, gm1, ggain_cross, dwo, dcq, dck, dcv, dco = pl.pallas_call(
        functools.partial(cross_backward_kernel, heads=heads),
        out_shape=cross_out_shapes,
        grid=(1,),
        in_specs=[full(a.shape) for a in cross_in] + weights(3, 4, 5, 6, 7),
        out_specs=[full(o.shape) for o in cross_out_shapes],
        scratch_shapes=vmem(
            ((length, width), BF16), ((length, width), BF16), ((width, length), BF16), ((SUB, length), F32),
            ((8, length), F32), ((length, width), BF16), ((source, width), BF16), ((source, width), BF16),
            ((PAIR, length), F32),
        ),
        compiler_params=params(),
        name="cross_backward",
    )(*cross_in, *([attention] * 5))

    self_out_shapes = [act32, ggain_shape, like((lanes, NB), F32)] + [square] * 3
    self_in = (tokens, gains, table, key_buckets, q1, k1, v1, mixed1, lse1, gm1, gfirst)
    gtokens, ggain_self, gtable, dwq, dwk, dwv = pl.pallas_call(
        functools.partial(self_backward_kernel, band=band, heads=heads),
        out_shape=self_out_shapes,
        grid=(1,),
        in_specs=[scalar] + [full(a.shape) for a in self_in] + weights(0, 1, 2),
        out_specs=[full(o.shape) for o in self_out_shapes],
        scratch_shapes=vmem(
            ((lanes, band.width), F32), ((SUB, band.causal), F32), ((SUB, band.two_way), F32), ((width, length), BF16),
            ((SUB, length), F32), ((8, length), F32), ((length, width), BF16), ((length, width), BF16),
            ((length, width), BF16), ((PAIR, length), F32), ((SUB, band.causal), F32), ((SUB, band.two_way), F32),
            ((lanes, band.width), F32),
        ),
        compiler_params=params(),
        name="self_backward",
    )(prefix, *self_in, *([attention] * 3))

    table_grad = lax.psum(gtable[:heads].T, AXES)
    ggains = lax.psum_scatter(
        jnp.stack([ggain_self[0], ggain_cross[0], ggain_feed[0]]), AXES, scatter_dimension=1, tiled=True
    )

    def scatter(parts):
        return lax.psum_scatter(jnp.concatenate(parts, axis=1), AXES, scatter_dimension=0, tiled=True).astype(F32)

    feed_grads = scatter([dgate, dup])
    down_grad = lax.psum_scatter(ddown, AXES, scatter_dimension=0, tiled=True).astype(F32)
    squares = scatter([dwq, dwk, dwv, dwo, dcq, dck, dcv, dco])
    pieces = [squares[:, i * width : (i + 1) * width] for i in range(8)]
    return (
        output.reshape(inputs.shape),
        gtokens.reshape(inputs.shape),
        gmem.reshape(encoded.shape),
        table_grad,
        ggains[0], pieces[0], pieces[1], pieces[2], pieces[3],
        ggains[1], pieces[4], pieces[5], pieces[6], pieces[7],
        ggains[2], feed_grads[:, :ff], feed_grads[:, ff:], down_grad,
    )


def solution(mesh):
    rows = P(AXES, None)
    gain = P(AXES)
    block = P(AXES, None, None)
    return jax.shard_map(
        per_device,
        mesh=mesh,
        in_specs=(block, block, block, gain, P(), P())
        + (gain, rows, rows, rows, rows)
        + (gain, rows, rows, rows, rows)
        + (gain, rows, rows, rows),
        out_specs=(block, block, block, P())
        + (gain, rows, rows, rows, rows)
        + (gain, rows, rows, rows, rows)
        + (gain, rows, rows, rows),
        check_vma=False,
    )
```

time: 1940 us -> 665 us (0.34)
  other arithmetic: 630 us -> 9.72 us
  matrix products: 427 us -> 0 us
  waiting for transfers between devices: 686 us -> 278 us
  Pallas kernels: 0 us -> 232 us
  local copies, waits for them, and re-layouts: 84.4 us -> 44.9 us
    reduce_scatter x9 -> x3, waiting for transfers between devices: 679 us -> 189 us  [the longest x2 189 us: scatter(): lax.psum_scatter(jnp.concatenate(parts, axis=1), AXES, scatter_dimension=...]
    reduce_sum x54 -> x0, other arithmetic: 454 us -> none  [the longest x1 300 us: head_bias(): jnp.sum(jnp.where(ids[:, :, None] == bucket_range, column[None, None, :],...]
    dot_general x321 -> x0, matrix products: 427 us -> none  [the longest x48 74.2 us: attend_backward(): jnp.einsum('rd,kd->rk', head_grads, value_group, preferred_element_type=j...]
    pallas_call x0 -> x4, Pallas kernels: none -> 232 us  [the longest x1 68.5 us: per_device(): pl.pallas_call(functools.partial(forward_kernel, band=band, heads=heads),...]
    all_gather x11 -> x3, waiting for transfers between devices: 0.12 us -> 88.2 us  [the longest x1 63.7 us: per_device(): lax.all_gather(jnp.concatenate([feed_gate, feed_up], axis=1), AXES, axis=...]
    select_n x2, other arithmetic: 79.3 us -> 0.01 us  [lane_buckets(): one = jnp.where(causal < 0, -1, one)]
    unnamed x915 -> x56, local copies, waits for them, and re-layouts: 81.5 us -> 17.9 us
    convert_element_type x53 -> x1, other arithmetic: 64.4 us -> 1.58 us  [per_device(): lax.psum_scatter(ddown, AXES, scatter_dimension=0, tiled=True).astype(F32)]
  transfers between devices with their start and end apart: 22 -> 6, of which waited for: 7 -> 4; matrix products, arithmetic and copies ran while one was open for 52% -> 7% of each run, Pallas kernels for 0% -> 26%
where the time goes in v1:
time: 665 us; the launch traced here: 664 us
  waiting for transfers between devices  278 us (42%)
  Pallas kernels  232 us (35%)
  blocking collectives  83.7 us (13%)
  local copies, waits for them, and re-layouts  44.9 us (7%)
  between operations  15.1 us (2%)
  other arithmetic  9.72 us (1%)
    reduce_scatter x2, waiting for transfers between devices, scatter(): lax.psum_scatter(jnp.concatenate(parts, axis=1), AXES, scatter_dimension=...  189 us
    pallas_call x1, Pallas kernels, per_device(): pl.pallas_call(functools.partial(forward_kernel, band=band, heads=heads),...  68.5 us
    all_gather x1, waiting for transfers between devices, per_device(): lax.all_gather(jnp.concatenate([feed_gate, feed_up], axis=1), AXES, axis=...  63.7 us
    pallas_call x1, Pallas kernels, per_device(): pl.pallas_call(feed_kernel, out_shape=feed_out, grid=(ff // fblock,), in_...  62.4 us
    pallas_call x1, Pallas kernels, per_device(): pl.pallas_call(functools.partial(self_backward_kernel, band=band, heads=h...  53.9 us
    pallas_call x1, Pallas kernels, per_device(): pl.pallas_call(functools.partial(cross_backward_kernel, heads=heads), out...  47 us
    all_gather x1, blocking collectives, per_device(): lax.all_gather(jnp.stack([norm_self, norm_cross, norm_feed]), AXES, axis=...  43.4 us
    psum x1, blocking collectives, per_device(): table_grad = lax.psum(gtable[:heads].T, AXES)  40.3 us
  transfers between devices with their start and end apart: 6, of which 4 were waited for; matrix products, arithmetic and copies ran while one was open for 7% of the time, Pallas kernels for 26%

profile of v1, /device:TPU:0, one launch (start us, length us, event | category | flops | bytes accessed | tf_op | source)
XLA Modules:
  0.0 663.9 jit_solution(16721330703283443221)
XLA Ops:
  7.3 0.8 constant_dynamic-update-slice_fusion.7
  8.0 0.8 constant_dynamic-update-slice_fusion.6
  8.8 0.8 constant_dynamic-update-slice_fusion.5
  9.6 0.8 constant_dynamic-update-slice_fusion.4
  10.3 0.8 constant_dynamic-update-slice_fusion.3
  11.1 0.8 constant_dynamic-update-slice_fusion.2
  11.9 0.8 constant_dynamic-update-slice_fusion.1
  12.7 0.8 constant_dynamic-update-slice_fusion
  13.4 0.7 copy-done.8
  14.2 0.7 all-gather.9.cloned.1.call-update
  15.0 1.6 pad_maximum_fusion.1
  17.3 0.7 broadcast_clamp_fusion
  18.0 0.8 fusion.2
  18.8 4.5 gather_fusion.1
  23.5 5.9 gather_fusion
  29.4 0.6 reshape.62.buckets_ref
  30.0 43.4 %all-gather = bf16[32,24,3]{1,2,0:T(4,128)(2,1)S(1)} all-gather(bf16[1,24,3]{1,2,0:T(4,128)(2,1)S(1)} %maximum_bitcast_fusion), channel_id=1, replica_groups=mesh['dp'=8,'fsdp'=4] {'dp','fsdp'}, dimensions={0}, use_global_device_ids=true | all-gather | bytes 4752 | tf_op jit(solution)/shard_map/all_gather | solution.py:564
  73.5 0.6 pad.12.table_ref
  74.1 0.6 pad_convert_fusion.gains_ref
  74.8 24.4 %all-gather.5.cloned.1.call-done.wq_ref.wk_ref.wv_ref.wo_ref.cq_ref.ck_ref.cv_ref.co_ref = bf16[768,6144]{1,0:T(8,128)(2,1)} async-done(((bf16[24,6144]{1,0:T(8,128)(2,1)}), bf16[768,6144]{1,0:T(8,128)(2,1)}) %all-gather.5.cloned.1.call-update) | async-done | bytes 9437200 | tf_op jit(solution)/shard_map/all_gather | solution.py:556
  99.2 68.5 %forward.1 = (bf16[1024,768]{1,0:T(8,128)(2,1)}, bf16[1024,768]{1,0:T(8,128)(2,1)}, bf16[1024,768]{1,0:T(8,128)(2,1)}, bf16[1024,768]{1,0:T(8,128)(2,1)}, f32[10...) custom-call(s32[1]{0:T(128)S(6)} %copy.69.limit_ref, ...), custom_call_target="tpu_custom_call" | custom-call | tf_op jit(solution)/shard_map/forward/pallas_call | solution.py:584
  167.7 63.7 %all-gather.7.cloned.1.call-done.gate_ref.up_ref = bf16[768,4096]{1,0:T(8,128)(2,1)} async-done(((bf16[24,4096]{1,0:T(8,128)(2,1)}), bf16[768,4096]{1,0:T(8,128)(2,1)}) %all-gather.7.cloned.1.call-update) | async-done | bytes 6291472 | tf_op jit(solution)/shard_map/all_gather | solution.py:562
  231.4 62.4 %feed.1 = (bf16[1024,768]{1,0:T(8,128)(2,1)}, f32[1024,768]{1,0:T(8,128)}, f32[8,768]{1,0:T(8,128)}, bf16[768,2048]{1,0:T(8,128)(2,1)}, bf16[768,2048]{1,0:T(8,128)(2,1)}, /*index=5*/bf16[2048,768]{1,0:T(8,128)(2,1)}) custom-call(f32[1024,768]{1,0:T(8,128)} %get-tuple-element.51.second_ref, bf16[1024,768]{1,0:T(8,128)(2,1)} %bitcast.36, ...), custom_call_target="tpu_custom_call" | custom-call | tf_op jit(solution)/shard_map/feed/pallas_call | solution.py:602
  293.9 1.8 copy-done
  295.7 5.1 pad_maximum_fusion
  300.9 0.2 reduce-scatter.5.cloned.1.call-start
  301.1 5.9 gather_fusion.2
  307.0 0.6 reshape.65.buckets_ref
  307.6 47.0 %cross_backward.1 = (f32[512,768]{1,0:T(8,128)}, f32[1024,768]{1,0:T(8,128)}, bf16[1024,768]{1,0:T(8,128)(2,1)}, f32[8,768]{1,0:T(8,128)}, bf16[768,768]{1,0:T(8...) custom-call(f32[1024,768]{1,0:T(8,128)} %get-tuple-element.58.gsecon, ...), custom_call_target="tpu_custom_call" | custom-call | tf_op jit(solution)/shard_map/cross_backward/pallas_call | solution.py:629
  354.6 53.9 %self_backward.1 = (f32[1024,768]{1,0:T(8,128)}, f32[8,768]{1,0:T(8,128)}, f32[16,32]{1,0:T(8,128)}, bf16[768,768]{1,0:T(8,128)(2,1)}, bf16[768,768]{1,0:T(8,128)(2,1)}, /*index=5*/bf16[768,768]{1,0:T(8,128)(2,1)}) custom-call(s32[1]{0:T(128)S(6)} %copy.69.limit_ref, bf16[1024,768]{1,0:T(8,128)(2,1)} %bitcast.33, f32[8,768]{1,0:T(8,128)} %pad_convert_fusion.gains_ref, ...), custom_call_target="tpu_custom_call" | custom-call | tf_op jit(solution)/shard_map/self_backward/pallas_call | solution.py:646
  408.6 2.6 constant_dynamic-update-slice_fusion.15
  411.2 1.1 constant_dynamic-update-slice_fusion.14
  412.3 1.2 constant_dynamic-update-slice_fusion.13
  413.5 1.3 constant_dynamic-update-slice_fusion.12
  414.8 1.2 constant_dynamic-update-slice_fusion.11
  416.0 1.2 constant_dynamic-update-slice_fusion.10
  417.2 1.1 constant_dynamic-update-slice_fusion.9
  418.3 1.2 constant_dynamic-update-slice_fusion.8
  419.6 0.7 slice.64
  420.3 0.7 slice.62
  421.1 0.7 slice.63
  421.8 40.3 %all-reduce.3 = (f32[32,12]{0,1:T(8,128)}, f32[3,768]{1,0:T(4,128)S(1)}) all-reduce(f32[32,12]{0,1:T(8,128)S(1)} %slice_bitcast_fusion, f32[3,768]{1,0:T(4,128)S(1)} %pad_maximum_fusion.2), channel_id=1, replica_groups=mesh['dp'=8,'fsdp'=4] {'dp','fsdp'}, use_global_device_ids=true, to_apply=%region_0.1 | all-reduce | flops 2688 | bytes 21504 | tf_op jit(solution)/shard_map/psum | solution.py:662
  462.2 0.5 slice_bitcast_fusion.1
  462.7 1.6 convert_element_type.16
  464.3 49.5 %reduce-scatter.7.cloned.1.call-done = bf16[24,4096]{1,0:T(8,128)(2,1)} async-done(((bf16[768,4096]{1,0:T(8,128)(2,1)}), bf16[24,4096]{1,0:T(8,128)(2,1)}) %reduce-scatter.7.cloned.1.call-update) | async-done | bytes 196624 | tf_op jit(solution)/shard_map/reduce_scatter | solution.py:668
  513.8 1.7 fusion.1
  515.5 139.8 %reduce-scatter.5.cloned.1.call-done = bf16[24,6144]{1,0:T(8,128)(2,1)} async-done(((bf16[768,6144]{1,0:T(8,128)(2,1)}), bf16[24,6144]{1,0:T(8,128)(2,1)}) %reduce-scatter.5.cloned.1.call-update) | async-done | bytes 294928 | tf_op jit(solution)/shard_map/reduce_scatter | solution.py:668
  655.3 1.7 fusion
  (62 shorter events, 0.6 us)
Async XLA Ops:
  7.2 16.1 %copy-start.10 = (s32[1536]{0:T(1024)S(1)}, s32[1536]{0:T(1024)}, u32[]{:S(2)}) copy-start(s32[1536]{0:T(1024)} %constant.62) | copy-start | bytes 18436
  7.2 16.1 %copy-start.11 = (s32[1536]{0:T(1024)S(1)}, s32[1536]{0:T(1024)}, u32[]{:S(2)}) copy-start(s32[1536]{0:T(1024)} %constant.60) | copy-start | bytes 18436
  7.2 92.0 %all-gather.5.cloned.1.call-start = ((), (), s32[]{:S(2)}) async-start(), calls=%async_computation.3 | async-start | bytes 9732096 | tf_op jit(solution)/shard_map/all_gather | solution.py:556
  13.4 0.7 copy-start.8
  14.2 153.6 %all-gather.9.cloned.1.call-start = ((), (), s32[]{:S(2)}) async-start(), calls=%async_computation.5 | async-start | bytes 3244032 | tf_op jit(solution)/shard_map/all_gather | solution.py:563
  14.9 216.5 %all-gather.7.cloned.1.call-start = ((), (), s32[]{:S(2)}) async-start(), calls=%async_computation.4 | async-start | bytes 6488064 | tf_op jit(solution)/shard_map/all_gather | solution.py:562
  16.6 446.1 %reduce-scatter.9.cloned.1.call-start = ((), (), s32[]{:S(2)}) async-start(), calls=%async_computation.8 | async-start | bytes 3244032 | tf_op jit(solution)/shard_map/reduce_scatter | solution.py:671
  23.4 5.9 copy-start.16
  23.4 6.0 copy-start.12
  23.4 6.0 copy-start.13
  23.4 6.6 copy-start.17
  23.4 6.6 copy-start.18
  23.4 6.6 copy-start.19
  23.4 50.1 %copy-start.14 = (bf16[32,12]{0,1:T(8,128)(2,1)S(1)}, bf16[32,12]{0,1:T(8,128)(2,1)}, u32[]{:S(2)}) copy-start(bf16[32,12]{0,1:T(8,128)(2,1)} %param.37) | copy-start | bytes 2308
  293.8 1.9 copy-start
  293.9 219.9 %reduce-scatter.7.cloned.1.call-start = ((), (), s32[]{:S(2)}) async-start(), calls=%async_computation.7 | async-start | bytes 6488064 | tf_op jit(solution)/shard_map/reduce_scatter | solution.py:668
  300.9 354.4 %reduce-scatter.5.cloned.1.call-start = ((), (), s32[]{:S(2)}) async-start(), calls=%async_computation.6 | async-start | bytes 9732096 | tf_op jit(solution)/shard_map/reduce_scatter | solution.py:668
  301.1 5.9 copy-start.15
  408.6 2.6 copy-start.7
  408.6 3.7 copy-start.6
  408.6 4.9 copy-start.5
  411.2 3.6 copy-start.4
  412.3 3.7 copy-start.3
  413.5 3.7 copy-start.2
  414.8 3.6 copy-start.1
  419.5 2.3 copy-start.9
Sparse Core Ops, SparseCore 0:
  14.3 84.8 all-gather.4
  102.1 57.5 all-gather.8
  163.1 68.3 all-gather.6
  294.0 100.0 reduce-scatter.8
  399.5 114.1 reduce-scatter.6
  520.5 134.7 reduce-scatter.4

commit v2 on v1

--- a/solution.py
+++ b/solution.py
@@ -2,7 +2,6 @@
 
 import jax
 import jax.numpy as jnp
-import numpy as np
 from jax import lax
 from jax.experimental import pallas as pl
 from jax.experimental.pallas import tpu as pltpu
@@ -36,9 +35,116 @@
     return lax.rsqrt(jnp.mean(value * value, axis=-1, keepdims=True) + 1e-06)
 
 
+MESH = pl.DeviceIdType.MESH
+EVERY = slice(None)
+
+
+class Place:
+    def __init__(self, sizes):
+        self.sizes = grid_of(sizes)
+        across, inner = lax.axis_index("dp"), lax.axis_index("fsdp")
+        deep, high, wide, cores = self.sizes
+        self.at = {
+            "z": lax.div(across, high),
+            "y": lax.rem(across, high),
+            "x": lax.div(inner, cores),
+            "c": lax.rem(inner, cores),
+        }
+
+    def device(self, **moved):
+        at = {**self.at, **moved}
+        deep, high, wide, cores = self.sizes
+        return (at["z"] * high + at["y"], at["x"] * cores + at["c"])
+
+    def size(self, axis):
+        return self.sizes["zyxc".index(axis)]
+
+    def others(self, axis):
+        size = self.size(axis)
+        return [lax.rem(self.at[axis] + step, size) for step in range(1, size)]
+
+    def meet(self):
+        barrier = pltpu.get_barrier_semaphore()
+        peers = [self.device(**{axis: other}) for axis in "zyxc" for other in self.others(axis)]
+        for peer in peers:
+            pl.semaphore_signal(barrier, inc=1, device_id=peer, device_id_type=MESH)
+        pl.semaphore_wait(barrier, len(peers))
+
+
+def grid_of(sizes):
+    wide = sizes["fsdp"] // 2
+    return (sizes["dp"] // wide, wide, wide, 2)
+
+
+class Gather:
+    PHASES = 4
+
+    def __init__(self, place, pieces, shards, outs, local_sem, send_sem, recv_sem):
+        self.place, self.pieces, self.shards, self.outs = place, pieces, shards, outs
+        self.local_sem, self.send_sem, self.recv_sem = local_sem, send_sem, recv_sem
+
+    @staticmethod
+    def copies(sizes, pieces):
+        return len(pieces) * sum(size - 1 for size in grid_of(sizes))
+
+    def view(self, piece, *index):
+        array, first, rows, order = piece
+        start = self.place.at["c"] * self.shards[array].shape[0] + first
+        return self.outs[array].at[(*index, pl.ds(pl.multiple_of(start, 8), rows), EVERY)]
+
+    def phase(self, number, phase):
+        piece = self.pieces[number]
+        place = self.place
+        at = place.at
+        deep, high, wide, cores = place.sizes
+        array, first, rows, order = piece
+        base = number * sum(size - 1 for size in place.sizes)
+        if phase == 0:
+            axis, skip = "z", 0
+            source = self.shards[array].at[pl.ds(first, rows), :]
+            target = self.view(piece, at["z"], at["y"], at["x"])
+        elif phase == 3:
+            axis, skip = "c", deep + high + wide - 3
+            source = target = self.view(piece, EVERY, EVERY, EVERY)
+        else:
+            axis = order[phase - 1]
+            skip = deep - 1 + (phase - 1) * (high - 1)
+            if phase == 1:
+                source = self.view(piece, EVERY, at["y"], at["x"])
+            elif axis == "y":
+                source = self.view(piece, EVERY, at["y"], EVERY)
+            else:
+                source = self.view(piece, EVERY, EVERY, at["x"])
+            target = source
+        copies = []
+        for step, other in enumerate(place.others(axis)):
+            slot = base + skip + step
+            copies.append(
+                pltpu.make_async_remote_copy(
+                    source,
+                    target,
+                    self.send_sem.at[slot],
+                    self.recv_sem.at[slot],
+                    device_id=place.device(**{axis: other}),
+                    device_id_type=MESH,
+                )
+            )
+        if phase == 0:
+            copies.append(pltpu.make_async_copy(source, target, self.local_sem.at[number]))
+        return copies
+
+    def advance(self, numbers, phase):
+        for number in numbers:
+            if phase > 0:
+                for copy in self.phase(number, phase - 1):
+                    copy.wait()
+            if phase < self.PHASES:
+                for copy in self.phase(number, phase):
+                    copy.start()
+
+
 class Band:
     def __init__(self, length, reach):
-        self.far = length
         self.reach = reach
         self.causal = length + reach
         self.two_way = 2 * reach
@@ -46,38 +152,39 @@
         self.query_zero = length - SUB
         self.query_zero_two = reach - SUB
         self.key_zero = reach - SUB
-        self.key_zero_two = reach - SUB
 
     def distances(self, rows):
-        lanes = np.arange(self.causal)
-        lanes_two = np.arange(self.two_way)
+        causal = lax.broadcasted_iota(jnp.int32, (1, self.causal), 1)
+        two_way = lax.broadcasted_iota(jnp.int32, (1, self.two_way), 1)
         if rows == "queries":
-            causal = self.query_zero - lanes
-            two_way = self.query_zero_two - lanes_two
-        else:
-            causal = lanes - self.key_zero
-            two_way = lanes_two - self.key_zero_two
-        causal = (causal + self.reach - 1) % self.causal - (self.reach - 1) if rows == "queries" else (
-            causal + self.reach
-        ) % self.causal - self.reach
-        two_way = (two_way + self.reach - 1) % self.two_way - (self.reach - 1) if rows == "queries" else (
-            two_way + self.reach
-        ) % self.two_way - self.reach
-        return causal, two_way
-
-
-def lane_buckets(bucket_map, band, rows):
+            causal, two_way = self.query_zero - causal, self.query_zero_two - two_way
+            return (
+                jnp.where(causal <= -self.reach, causal + self.causal, causal),
+                jnp.where(two_way <= -self.reach, two_way + self.two_way, two_way),
+            )
+        causal, two_way = causal - self.key_zero, two_way - self.key_zero
+        return (
+            jnp.where(causal >= self.causal - self.reach, causal - self.causal, causal),
+            jnp.where(two_way >= self.reach, two_way - self.two_way, two_way),
+        )
+
+
+def one_hot(map_ref, band, rows):
+    bucket = lax.broadcasted_iota(jnp.int32, (NB, 1), 0)
+
+    def edges(row, number):
+        entries = map_ref[row : row + 1, :]
+        below = jnp.sum((entries < number).astype(jnp.int32), axis=1, keepdims=True)
+        return below, below + jnp.sum((entries == number).astype(jnp.int32), axis=1, keepdims=True)
+
     causal, two_way = band.distances(rows)
-    top = bucket_map.shape[1] - 1
-    one = bucket_map[0][np.clip(causal, 0, top)]
-    one = jnp.where(causal < 0, -1, one)
-    two = bucket_map[1][np.clip(np.abs(two_way), 0, top)] + (NB // 2) * (two_way < 0).astype(np.int32)
-    return jnp.concatenate([one, two]).reshape(1, -1)
-
-
-def one_hot(buckets_ref):
-    width = buckets_ref.shape[1]
-    return buckets_ref[...] == lax.broadcasted_iota(jnp.int32, (NB, width), 0)
+    low, high = edges(0, bucket)
+    one = (causal >= low) & (causal < high)
+    ahead = bucket >= NB // 2
+    low, high = edges(1, jnp.where(ahead, bucket - NB // 2, bucket))
+    apart = jnp.abs(two_way)
+    two = (apart >= low) & (apart < high) & ((two_way < 0) == ahead)
+    return jnp.concatenate([jnp.where(one, 1.0, 0.0), jnp.where(two, 1.0, 0.0)], axis=1), causal
 
 
 def spread(row, width):
@@ -102,10 +209,10 @@
     two_ref[...] = spread(row[:, band.causal :], band.two_way)
 
 
-def bias_rows(table_ref, buckets_ref):
-    hot = one_hot(buckets_ref)
-    bias = dot(table_ref[...], jnp.where(hot, 1.0, 0.0).astype(BF16))
-    return jnp.where(buckets_ref[...] < 0, NEG, bias)
+def bias_rows(table_ref, map_ref, band, rows):
+    hot, causal = one_hot(map_ref, band, rows)
+    bias = dot(table_ref[...], hot.astype(BF16), 0, 0)
+    return jnp.concatenate([jnp.where(causal < 0, NEG, bias[:, : band.causal]), bias[:, band.causal :]], axis=1)
 
 
 def head_cols(head):
@@ -177,57 +284,148 @@
         step(pl.ds(pl.multiple_of(index * block, block), block))
 
 
+def gain_rows(gathered, width):
+    devices = gathered.shape[0]
+    share = width // devices
+    lane = lax.broadcasted_iota(jnp.int32, (SUB, width), 1)
+    select = jnp.where(lax.rem(lane, share) == lax.broadcasted_iota(jnp.int32, (SUB, width), 0), 1.0, 0.0)
+    first = share * lax.broadcasted_iota(jnp.int32, (devices, width), 0)
+    lane = lax.broadcasted_iota(jnp.int32, (devices, width), 1)
+    own = (lane >= first) & (lane < first + share)
+    rows = []
+    for number in range(8):
+        spread_out = exact_dot(gathered[:, number, :], select)
+        rows.append(jnp.sum(jnp.where(own, spread_out, 0.0), axis=0, keepdims=True))
+    return jnp.concatenate(rows, axis=0)
+
+
+ATTENTION = 8
+SHARDS = 12
+
+
+def gather_pieces(rows, down_rows):
+    head, tail = rows // 3 // 8 * 8, rows - rows // 3 // 8 * 8
+    first = [(0, 0, rows, "xy"), (1, 0, rows, "yx"), (2, 0, head, "xy"), (2, head, tail, "yx"), (11, 0, 8, "xy")]
+    rest = [(3, 0, rows, "xy"), (4, 0, rows, "yx"), (5, 0, rows, "xy"), (6, 0, rows, "yx")]
+    rest += [(7, 0, tail, "xy"), (7, tail, head, "yx")]
+    feed = [(8, 0, rows, "xy"), (9, 0, rows, "yx")]
+    feed += [(10, 0, down_rows // 2, "xy"), (10, down_rows // 2, down_rows // 2, "yx")]
+    pieces = first + rest + feed
+    numbers = list(range(len(pieces)))
+    groups = numbers[: len(first)], numbers[len(first) : len(first) + len(rest)], numbers[len(first) + len(rest) :]
+    return pieces, groups
+
+
 def forward_kernel(
-    limit_ref, tokens_ref, memory_ref, gains_ref, table_ref, buckets_ref,
-    wq_ref, wk_ref, wv_ref, wo_ref, cq_ref, ck_ref, cv_ref, co_ref,
-    q1_ref, k1_ref, v1_ref, mixed1_ref, lse1_ref, first_ref,
-    q2_ref, k2_ref, v2_ref, mixed2_ref, lse2_ref, second_ref,
-    bias_ref, causal_ref, two_ref,
-    *, band, heads,
+    limit_ref, tokens_ref, memory_ref, table_ref, map_ref, gain1_ref, gain2_ref, gain3_ref, *refs, band, heads, plan,
 ):
-    length = tokens_ref.shape[0]
-    bias_ref[...] = bias_rows(table_ref, buckets_ref)
-
-    def project_self(rows):
-        value = tokens_ref[rows, :].astype(F32)
-        normed = (value * rms(value) * gains_ref[0:1, :]).astype(BF16)
-        q1_ref[rows, :] = dot(normed, wq_ref[...]).astype(BF16)
-        k1_ref[rows, :] = dot(normed, wk_ref[...]).astype(BF16)
-        v1_ref[rows, :] = dot(normed, wv_ref[...]).astype(BF16)
-
-    row_blocks(length, 256, project_self)
+    count = SHARDS - 1 if plan else ATTENTION
+    shards, refs = refs[:count], refs[count:]
+    if plan:
+        gathered, refs = refs[:SHARDS], refs[SHARDS:]
+    else:
+        gathered = shards
+    (
+        gains_ref, q1_ref, k1_ref, v1_ref, mixed1_ref, lse1_ref, first_ref,
+        q2_ref, k2_ref, v2_ref, mixed2_ref, lse2_ref, second_ref,
+        bias_ref, causal_ref, two_ref, weights_ref, share_ref, tile_ref, load_sem, *gather_sems,
+    ) = refs
+    length, width = tokens_ref.shape
+    if plan:
+        sizes, pieces, (soon, later, feed) = plan
+        place = Place(sizes)
+        gather = Gather(place, pieces, (*shards, share_ref), gathered, *gather_sems)
+
+    def advance(*steps):
+        if plan:
+            for numbers, phase in steps:
+                gather.advance({"soon": soon, "later": later, "feed": feed}[numbers], phase)
+
+    def load(number):
+        return pltpu.make_async_copy(gathered[number].reshape(width, width), weights_ref.at[number], load_sem.at[number])
+
+    def load_tile():
+        return pltpu.make_async_copy(gathered[SHARDS - 1].reshape(tile_ref.shape), tile_ref, load_sem.at[ATTENTION])
+
+    gain_refs = (gain1_ref, gain2_ref, gain3_ref)
+    if plan:
+        share_ref[...] = jnp.zeros_like(share_ref)
+        for number, gain_ref in enumerate(gain_refs):
+            share_ref[number : number + 1, : gain_ref.shape[1]] = gain_ref[...].astype(F32)
+        place.meet()
+    advance(("soon", 0))
+    bias_ref[...] = bias_rows(table_ref, map_ref, band, "queries")
     lse1_ref[...] = jnp.zeros_like(lse1_ref)
     lse2_ref[...] = jnp.zeros_like(lse2_ref)
     mixed1_ref[...] = jnp.zeros_like(mixed1_ref)
     mixed2_ref[...] = jnp.zeros_like(mixed2_ref)
+    advance(("soon", 1), ("later", 0), ("feed", 0), ("soon", 2), ("soon", 3), ("later", 1), ("soon", 4))
+    for number in range(3):
+        load(number).start()
+    if plan:
+        load_tile().start()
+        load_tile().wait()
+        gains_ref[...] = gain_rows(tile_ref[...], width)
+    else:
+        gains_ref[...] = jnp.zeros_like(gains_ref)
+        for number, gain_ref in enumerate(gain_refs):
+            gains_ref[number : number + 1, :] = gain_ref[...].astype(F32)
+    for number in range(3):
+        load(number).wait()
+
+    def project_self(rows):
+        value = tokens_ref[rows, :].astype(F32)
+        normed = (value * rms(value) * gains_ref[0:1, :]).astype(BF16)
+        q1_ref[rows, :] = dot(normed, weights_ref[0]).astype(BF16)
+        k1_ref[rows, :] = dot(normed, weights_ref[1]).astype(BF16)
+        v1_ref[rows, :] = dot(normed, weights_ref[2]).astype(BF16)
+
+    row_blocks(length, 256, project_self)
+    advance(("later", 2))
 
     @pl.loop(0, heads)
     def _(head):
         fill_bands(head, bias_ref, band, causal_ref, two_ref)
         self_forward_head(head, limit_ref[0], q1_ref, k1_ref, v1_ref, causal_ref, two_ref, band, mixed1_ref, lse1_ref)
 
+        @pl.when(head == heads // 4)
+        def _():
+            advance(("feed", 1), ("later", 3))
+
+        @pl.when(head == heads // 2)
+        def _():
+            advance(("later", 4))
+            for number in range(3, ATTENTION):
+                load(number).start()
+            advance(("feed", 2))
+
+    for number in range(3, ATTENTION):
+        load(number).wait()
+
     def project_memory(rows):
-        k2_ref[rows, :] = dot(memory_ref[rows, :], ck_ref[...]).astype(BF16)
-        v2_ref[rows, :] = dot(memory_ref[rows, :], cv_ref[...]).astype(BF16)
+        k2_ref[rows, :] = dot(memory_ref[rows, :], weights_ref[5]).astype(BF16)
+        v2_ref[rows, :] = dot(memory_ref[rows, :], weights_ref[6]).astype(BF16)
 
     row_blocks(memory_ref.shape[0], 256, project_memory)
 
     def project_cross(rows):
-        value = tokens_ref[rows, :].astype(F32) + dot(mixed1_ref[rows, :], wo_ref[...])
+        value = tokens_ref[rows, :].astype(F32) + dot(mixed1_ref[rows, :], weights_ref[3])
         first_ref[rows, :] = value
         normed = (value * rms(value) * gains_ref[1:2, :]).astype(BF16)
-        q2_ref[rows, :] = dot(normed, cq_ref[...]).astype(BF16)
+        q2_ref[rows, :] = dot(normed, weights_ref[4]).astype(BF16)
 
     row_blocks(length, 256, project_cross)
+    advance(("feed", 3))
 
     @pl.loop(0, heads)
     def _(head):
         cross_forward_head(head, q2_ref, k2_ref, v2_ref, mixed2_ref, lse2_ref)
 
     def project_second(rows):
-        second_ref[rows, :] = first_ref[rows, :] + dot(mixed2_ref[rows, :], co_ref[...])
+        second_ref[rows, :] = first_ref[rows, :] + dot(mixed2_ref[rows, :], weights_ref[7])
 
     row_blocks(length, 256, project_second)
+    advance(("feed", 4))
 
 
 def norm_back_rows(value, gain, grad):
@@ -346,7 +544,7 @@
             at = band.key_zero - key + start
             bias = causal_ref[:, at : at + count]
             if first < reach:
-                at = band.key_zero_two - key
+                at = band.key_zero - key
                 two = two_ref[:, at : at + reach]
                 inside = (key + lax.broadcasted_iota(jnp.int32, (SUB, reach), 0) < limit) & (
                     lax.broadcasted_iota(jnp.int32, (SUB, reach), 1) < limit
@@ -365,7 +563,7 @@
                     lax.broadcasted_iota(jnp.int32, (SUB, reach), 1) < limit
                 )
                 head_part = part[:, :reach]
-                at_two = band.key_zero_two - key
+                at_two = band.key_zero - key
                 two_sum_ref[:, at_two : at_two + reach] += jnp.where(inside, head_part, 0.0)
                 causal_sum_ref[:, at : at + reach] += jnp.where(inside, 0.0, head_part)
                 causal_sum_ref[:, at + reach : at + count] += part[:, reach:]
@@ -461,7 +659,7 @@
 
 
 def self_backward_kernel(
-    limit_ref, tokens_ref, gains_ref, table_ref, buckets_ref, q_ref, k_ref, v_ref, mixed_ref, lse_ref, gm_ref, gfirst_ref,
+    limit_ref, tokens_ref, gains_ref, table_ref, map_ref, q_ref, k_ref, v_ref, mixed_ref, lse_ref, gm_ref, gfirst_ref,
     wq_ref, wk_ref, wv_ref,
     gtokens_ref, ggain_ref, gtable_ref, dwq_ref, dwk_ref, dwv_ref,
     bias_ref, causal_ref, two_ref, flipped_ref, lse_rows_ref, delta_ref, gq_ref, gk_ref, gv_ref, gqt_ref,
@@ -470,7 +668,7 @@
 ):
     length, width = tokens_ref.shape
     block = 256
-    bias_ref[...] = bias_rows(table_ref, buckets_ref)
+    bias_ref[...] = bias_rows(table_ref, map_ref, band, "keys")
     lse_rows_ref[...] = lse_ref[...].T
     gk_ref[...] = jnp.zeros_like(gk_ref)
     gv_ref[...] = jnp.zeros_like(gv_ref)
@@ -497,7 +695,7 @@
 
         gq_ref[:, cols] = gqt_ref[...].T.astype(BF16)
 
-    hot = jnp.where(one_hot(buckets_ref), 1.0, 0.0)
+    hot, unused = one_hot(map_ref, band, "keys")
     gtable_ref[...] = exact_dot(sums_ref[...], hot, 1, 1)
     ggain_ref[...] = jnp.zeros_like(ggain_ref)
 
@@ -528,10 +726,6 @@
 
 def params(**kw):
     return pltpu.CompilerParams(vmem_limit_bytes=60 * 1024 * 1024, **kw)
-
-
-def weight_block(number, width):
-    return pl.BlockSpec((width, width), lambda *_: (0, number))
 
 
 def per_device(
@@ -548,27 +742,26 @@
     tokens = inputs.reshape(length, width)
     memory = encoded.reshape(source, width)
     gout = out_grad.reshape(length, width)
-    lanes = 16
-    table = jnp.pad(bias_table.T, ((0, lanes - heads), (0, 0)))
-    query_buckets = lane_buckets(bucket_map, band, "queries")
-    key_buckets = lane_buckets(bucket_map, band, "keys")
-
-    attention = lax.all_gather(
-        jnp.concatenate(
-            [self_query, self_key, self_value, self_out, cross_query, cross_key, cross_value, cross_out], axis=1
-        ),
-        AXES, axis=0, tiled=True,
-    )
-    feed = lax.all_gather(jnp.concatenate([feed_gate, feed_up], axis=1), AXES, axis=0, tiled=True)
-    down = lax.all_gather(feed_down, AXES, axis=0, tiled=True)
-    gains = lax.all_gather(jnp.stack([norm_self, norm_cross, norm_feed]), AXES, axis=1, tiled=True)
-    gains = jnp.pad(gains.astype(F32), ((0, 5), (0, 0)))
-
-    whole = pl.BlockSpec(memory_space=pltpu.VMEM)
+    gains_in = [norm_self, norm_cross, norm_feed]
+    projections = [self_query, self_key, self_value, self_out, cross_query, cross_key, cross_value, cross_out]
+    feeds = [feed_gate, feed_up, feed_down]
+    sizes = dict(dp=lax.axis_size("dp"), fsdp=lax.axis_size("fsdp"))
+    devices = sizes["dp"] * sizes["fsdp"]
+    own = self_query.shape[0] % 8 == 0
+    if own:
+        pieces, groups = gather_pieces(self_query.shape[0], feed_down.shape[0])
+        plan = (sizes, pieces, groups)
+        copies = Gather.copies(sizes, pieces)
+        shards = projections + feeds
+    else:
+        plan = None
+        gains_in = [lax.all_gather(gain, AXES, axis=0, tiled=True) for gain in gains_in]
+        shards = [lax.all_gather(shard, AXES, axis=0, tiled=True) for shard in projections]
+        gate_full, up_full, down = [lax.all_gather(shard, AXES, axis=0, tiled=True) for shard in feeds]
+    gains_in = [gain.reshape(1, -1) for gain in gains_in]
+
+    remote = pl.BlockSpec(memory_space=pl.ANY)
     scalar = pl.BlockSpec(memory_space=pltpu.SMEM)
-
-    def weights(*numbers):
-        return [weight_block(number, width) for number in numbers]
 
     def full(shape):
         return pl.BlockSpec(shape, lambda *_: (0,) * len(shape))
@@ -580,19 +773,36 @@
     mem = like((source, width), BF16)
     act32 = like((length, width), F32)
     lse_shape = like((length, SUB), F32)
-    outs = [act, act, act, act, lse_shape, act32, act, mem, mem, act, lse_shape, act32]
-    q1, k1, v1, mixed1, lse1, first, q2, k2, v2, mixed2, lse2, second = pl.pallas_call(
-        functools.partial(forward_kernel, band=band, heads=heads),
-        out_shape=outs,
+    gain_shape = like((8, width), F32)
+    outs = [gain_shape, act, act, act, act, lse_shape, act32, act, mem, mem, act, lse_shape, act32]
+    gathered_shapes = []
+    if own:
+        chips, cores = grid_of(sizes)[:3], grid_of(sizes)[3]
+        gathered_shapes = [like(chips + (cores * shard.shape[0], shard.shape[1]), shard.dtype) for shard in shards]
+        gathered_shapes.append(like(chips + (cores * 8, SUB), F32))
+    forward_in = (tokens, memory, bias_table, bucket_map, *gains_in)
+    results = pl.pallas_call(
+        functools.partial(forward_kernel, band=band, heads=heads, plan=plan),
+        out_shape=gathered_shapes + outs,
         grid=(1,),
-        in_specs=[scalar] + [full(a.shape) for a in (tokens, memory, gains, table, query_buckets)] + weights(*range(8)),
-        out_specs=[full(o.shape) for o in outs],
+        in_specs=[scalar] + [full(a.shape) for a in forward_in] + [remote] * len(shards),
+        out_specs=[remote] * len(gathered_shapes) + [full(o.shape) for o in outs],
         scratch_shapes=vmem(
-            ((lanes, band.width), F32), ((SUB, band.causal), F32), ((SUB, band.two_way), F32)
-        ),
-        compiler_params=params(),
+            ((heads, band.width), F32), ((SUB, band.causal), F32), ((SUB, band.two_way), F32),
+            ((ATTENTION, width, width), BF16), ((8, SUB), F32), ((devices, 8, SUB), F32),
+        )
+        + [pltpu.SemaphoreType.DMA((ATTENTION + 1,))]
+        + ([pltpu.SemaphoreType.DMA((number,)) for number in (len(pieces), copies, copies)] if own else []),
+        compiler_params=params(collective_id=0, has_side_effects=True) if own else params(),
         name="forward",
-    )(prefix, tokens, memory, gains, table, query_buckets, *([attention] * 8))
+    )(prefix, *forward_in, *shards)
+    attention = shards
+    if own:
+        gathered, results = results[:SHARDS], results[SHARDS:]
+        attention = [part.reshape(width, width) for part in gathered[:ATTENTION]]
+        gate_full, up_full = gathered[8].reshape(width, ff), gathered[9].reshape(width, ff)
+        down = gathered[10].reshape(ff, width)
+    gains, q1, k1, v1, mixed1, lse1, first, q2, k2, v2, mixed2, lse2, second = results
 
     fblock = 256
     ggain_shape = like((8, width), F32)
@@ -606,7 +816,7 @@
         in_specs=[full(second.shape), full(gout.shape), full(gains.shape)]
         + [
             pl.BlockSpec((width, fblock), lambda i: (0, i)),
-            pl.BlockSpec((width, fblock), lambda i: (0, i + ff // fblock)),
+            pl.BlockSpec((width, fblock), lambda i: (0, i)),
             pl.BlockSpec((fblock, width), lambda i: (i, 0)),
         ],
         out_specs=[full(o.shape) for o in feed_out[:3]]
@@ -621,7 +831,7 @@
         ),
         compiler_params=params(),
         name="feed",
-    )(second, gout, gains, feed, feed, down)
+    )(second, gout, gains, gate_full, up_full, down)
 
     square = like((width, width), BF16)
     cross_out_shapes = [like((source, width), F32), act32, act, ggain_shape] + [square] * 5
@@ -630,7 +840,7 @@
         functools.partial(cross_backward_kernel, heads=heads),
         out_shape=cross_out_shapes,
         grid=(1,),
-        in_specs=[full(a.shape) for a in cross_in] + weights(3, 4, 5, 6, 7),
+        in_specs=[full(a.shape) for a in cross_in] + [full((width, width))] * 5,
         out_specs=[full(o.shape) for o in cross_out_shapes],
         scratch_shapes=vmem(
             ((length, width), BF16), ((length, width), BF16), ((width, length), BF16), ((SUB, length), F32),
@@ -639,27 +849,27 @@
         ),
         compiler_params=params(),
         name="cross_backward",
-    )(*cross_in, *([attention] * 5))
-
-    self_out_shapes = [act32, ggain_shape, like((lanes, NB), F32)] + [square] * 3
-    self_in = (tokens, gains, table, key_buckets, q1, k1, v1, mixed1, lse1, gm1, gfirst)
+    )(*cross_in, *attention[3:])
+
+    self_out_shapes = [act32, ggain_shape, like((heads, NB), F32)] + [square] * 3
+    self_in = (tokens, gains, bias_table, bucket_map, q1, k1, v1, mixed1, lse1, gm1, gfirst)
     gtokens, ggain_self, gtable, dwq, dwk, dwv = pl.pallas_call(
         functools.partial(self_backward_kernel, band=band, heads=heads),
         out_shape=self_out_shapes,
         grid=(1,),
-        in_specs=[scalar] + [full(a.shape) for a in self_in] + weights(0, 1, 2),
+        in_specs=[scalar] + [full(a.shape) for a in self_in] + [full((width, width))] * 3,
         out_specs=[full(o.shape) for o in self_out_shapes],
         scratch_shapes=vmem(
-            ((lanes, band.width), F32), ((SUB, band.causal), F32), ((SUB, band.two_way), F32), ((width, length), BF16),
+            ((heads, band.width), F32), ((SUB, band.causal), F32), ((SUB, band.two_way), F32), ((width, length), BF16),
             ((SUB, length), F32), ((8, length), F32), ((length, width), BF16), ((length, width), BF16),
             ((length, width), BF16), ((PAIR, length), F32), ((SUB, band.causal), F32), ((SUB, band.two_way), F32),
-            ((lanes, band.width), F32),
+            ((heads, band.width), F32),
         ),
         compiler_params=params(),
         name="self_backward",
-    )(prefix, *self_in, *([attention] * 3))
-
-    table_grad = lax.psum(gtable[:heads].T, AXES)
+    )(prefix, *self_in, *attention[:3])
+
+    table_grad = lax.psum(gtable.T, AXES)
     ggains = lax.psum_scatter(
         jnp.stack([ggain_self[0], ggain_cross[0], ggain_feed[0]]), AXES, scatter_dimension=1, tiled=True
     )

time: 665 us -> 574 us (0.86)
  waiting for transfers between devices: 278 us -> 196 us
  Pallas kernels: 232 us -> 296 us
  blocking collectives: 83.7 us -> 39.2 us
  local copies, waits for them, and re-layouts: 44.9 us -> 20.1 us
    all_gather x3 -> x0, waiting for transfers between devices: 88.2 us -> none  [the longest x1 63.7 us: per_device(): lax.all_gather(jnp.concatenate([feed_gate, feed_up], axis=1), AXES, axis=...]
    pallas_call x1, Pallas kernels: 68.5 us -> 132 us  [per_device(): pl.pallas_call(functools.partial(forward_kernel, band=band, heads=heads,...]
    all_gather x1 -> x0, blocking collectives: 43.4 us -> none  [per_device(): lax.all_gather(jnp.stack([norm_self, norm_cross, norm_feed]), AXES, axis=...]
    gather x3 -> x0, local copies, waits for them, and re-layouts: 16.2 us -> none  [the longest x2 11.7 us: lane_buckets(): one = bucket_map[0][np.clip(causal, 0, top)]]
    reduce_scatter x2, waiting for transfers between devices: 189 us -> 196 us  [scatter(): lax.psum_scatter(jnp.concatenate(parts, axis=1), AXES, scatter_dimension=...]
    unnamed x56 -> x27, local copies, waits for them, and re-layouts: 17.9 us -> 12.8 us
  transfers between devices with their start and end apart: 6 -> 3, of which waited for: 4 -> 2; matrix products, arithmetic and copies ran while one was open for 7% -> 4% of each run, Pallas kernels for 26% -> 18%
where the time goes in v2:
time: 574 us; the launch traced here: 573 us
  Pallas kernels  296 us (52%)
  waiting for transfers between devices  196 us (34%)
  blocking collectives  39.2 us (7%)
  local copies, waits for them, and re-layouts  20.1 us (4%)
  between operations  14.5 us (3%)
  other arithmetic  6.85 us (1%)
    reduce_scatter x2, waiting for transfers between devices, scatter(): lax.psum_scatter(jnp.concatenate(parts, axis=1), AXES, scatter_dimension=...  196 us
    pallas_call x1, Pallas kernels, per_device(): pl.pallas_call(functools.partial(forward_kernel, band=band, heads=heads,...  132 us
    pallas_call x1, Pallas kernels, per_device(): pl.pallas_call(feed_kernel, out_shape=feed_out, grid=(ff // fblock,), in_...  62.4 us
    pallas_call x1, Pallas kernels, per_device(): pl.pallas_call(functools.partial(self_backward_kernel, band=band, heads=h...  54.3 us
    pallas_call x1, Pallas kernels, per_device(): pl.pallas_call(functools.partial(cross_backward_kernel, heads=heads), out...  47 us
    psum x1, blocking collectives, per_device(): table_grad = lax.psum(gtable.T, AXES)  39.2 us
    unnamed x27, local copies, waits for them, and re-layouts  12.8 us
  transfers between devices with their start and end apart: 3, of which 2 were waited for; matrix products, arithmetic and copies ran while one was open for 4% of the time, Pallas kernels for 18%

profile of v2, /device:TPU:0, one launch (start us, length us, event | category | flops | bytes accessed | tf_op | source)
XLA Modules:
  0.0 573.3 jit_solution(17647074563863714782)
XLA Ops:
  7.2 0.0 reduce-scatter.9.cloned.1.call-start
  7.2 1.4 copy.40.table_ref
  9.3 132.3 %forward.1 = (bf16[4,2,2,48,768]{4,3,2,1,0:T(8,128)(2,1)}, bf16[4,2,2,48,768]{4,3,2,1,0:T(8,128)(2,1)}, bf16[4,2,2,48,768]{4,3,2,1,0:T(8,128)(2,1)}, bf16[4,2,2,...) custom-call(s32[1]{0:T(128)S(6)} %copy.51.limit_ref, ...), custom_call_target="tpu_custom_call" | custom-call | tf_op jit(solution)/shard_map/forward/pallas_call | solution.py:784
  141.6 62.4 %feed.1 = (bf16[1024,768]{1,0:T(8,128)(2,1)}, f32[1024,768]{1,0:T(8,128)}, f32[8,768]{1,0:T(8,128)}, bf16[768,2048]{1,0:T(8,128)(2,1)}, bf16[768,2048]{1,0:T(8,128)(2,1)}, /*index=5*/bf16[2048,768]{1,0:T(8,128)(2,1)}) custom-call(f32[1024,768]{1,0:T(8,128)} %get-tuple-element.63.second_ref, bf16[1024,768]{1,0:T(8,128)(2,1)} %bitcast.36, ...), custom_call_target="tpu_custom_call" | custom-call | tf_op jit(solution)/shard_map/feed/pallas_call | solution.py:812
  203.9 0.0 copy-start
  203.9 0.0 reduce-scatter.9.cloned.1.call-update
  204.0 0.2 reduce-scatter.7.cloned.1.call-start
  204.2 1.6 copy-done
  205.8 5.3 pad_maximum_fusion
  211.1 0.0 reduce-scatter.7.cloned.1.call-update
  211.1 0.0 reduce-scatter.5.cloned.1.call-start
  211.2 47.0 %cross_backward.1 = (f32[512,768]{1,0:T(8,128)}, f32[1024,768]{1,0:T(8,128)}, bf16[1024,768]{1,0:T(8,128)(2,1)}, f32[8,768]{1,0:T(8,128)}, bf16[768,768]{1,0:T(8...) custom-call(f32[1024,768]{1,0:T(8,128)} %get-tuple-element.74.gsecon, ...), custom_call_target="tpu_custom_call" | custom-call | tf_op jit(solution)/shard_map/cross_backward/pallas_call | solution.py:839
  258.1 54.3 %self_backward.1 = (f32[1024,768]{1,0:T(8,128)}, f32[8,768]{1,0:T(8,128)}, f32[12,32]{1,0:T(8,128)}, bf16[768,768]{1,0:T(8,128)(2,1)}, bf16[768,768]{1,0:T(8,128)(2,1)}, /*index=5*/bf16[768,768]{1,0:T(8,128)(2,1)}) custom-call(s32[1]{0:T(128)S(6)} %copy.51.limit_ref, bf16[1024,768]{1,0:T(8,128)(2,1)} %bitcast.30, f32[8,768]{1,0:T(8,128)} %get-tuple-element.64.gains_ref, ...), custom_call_target="tpu_custom_call" | custom-call | tf_op jit(solution)/shard_map/self_backward/pallas_call | solution.py:856
  312.4 0.0 copy-start.7
  312.4 0.0 copy-start.6
  312.4 0.0 copy-start.5
  312.5 2.7 constant_dynamic-update-slice_fusion.7
  315.2 0.0 copy-done.7
  315.2 0.0 copy-start.4
  315.2 1.1 constant_dynamic-update-slice_fusion.6
  316.3 0.0 copy-done.6
  316.3 0.0 copy-start.3
  316.3 1.1 constant_dynamic-update-slice_fusion.5
  317.5 0.0 copy-done.5
  317.5 0.0 copy-start.2
  317.5 1.2 constant_dynamic-update-slice_fusion.4
  318.6 0.0 copy-done.4
  318.6 0.0 copy-start.1
  318.6 1.2 constant_dynamic-update-slice_fusion.3
  319.8 0.0 copy-done.3
  319.8 1.2 constant_dynamic-update-slice_fusion.2
  321.0 0.0 copy-done.2
  321.0 1.1 constant_dynamic-update-slice_fusion.1
  322.1 0.0 copy-done.1
  322.1 1.2 constant_dynamic-update-slice_fusion
  323.3 0.0 reduce-scatter.5.cloned.1.call-update
  323.4 0.7 slice.48
  324.1 0.8 slice.49
  324.8 0.7 slice.50
  325.6 0.0 copy-done.8
  325.6 39.2 %all-reduce.1 = (f32[32,12]{0,1:T(8,128)}, f32[3,768]{1,0:T(4,128)S(1)}) all-reduce(f32[32,12]{0,1:T(8,128)S(1)} %bitcast.45, f32[3,768]{1,0:T(4,128)S(1)} %pad_maximum_fusion.1), channel_id=1, replica_groups=mesh['dp'=8,'fsdp'=4] {'dp','fsdp'}, use_global_device_ids=true, to_apply=%region_0.0 | all-reduce | flops 2688 | bytes 21504 | tf_op jit(solution)/shard_map/psum | solution.py:872
  364.8 0.1 constant_dynamic-slice_fusion
  364.9 0.5 slice_bitcast_fusion
  365.4 1.6 convert_element_type.11
  367.0 56.2 %reduce-scatter.7.cloned.1.call-done = bf16[24,4096]{1,0:T(8,128)(2,1)} async-done(((bf16[768,4096]{1,0:T(8,128)(2,1)}), bf16[24,4096]{1,0:T(8,128)(2,1)}) %reduce-scatter.7.cloned.1.call-update) | async-done | bytes 196624 | tf_op jit(solution)/shard_map/reduce_scatter | solution.py:878
  423.2 1.7 fusion.1
  424.9 140.1 %reduce-scatter.5.cloned.1.call-done = bf16[24,6144]{1,0:T(8,128)(2,1)} async-done(((bf16[768,6144]{1,0:T(8,128)(2,1)}), bf16[24,6144]{1,0:T(8,128)(2,1)}) %reduce-scatter.5.cloned.1.call-update) | async-done | bytes 294928 | tf_op jit(solution)/shard_map/reduce_scatter | solution.py:878
  565.0 1.7 fusion
  (3 shorter events, 0.0 us)
Async XLA Ops:
  7.2 358.3 %reduce-scatter.9.cloned.1.call-start = ((), (), s32[]{:S(2)}) async-start(), calls=%async_computation.5 | async-start | bytes 3244032 | tf_op jit(solution)/shard_map/reduce_scatter | solution.py:881
  203.9 1.9 copy-start
  204.0 219.2 %reduce-scatter.7.cloned.1.call-start = ((), (), s32[]{:S(2)}) async-start(), calls=%async_computation.4 | async-start | bytes 6488064 | tf_op jit(solution)/shard_map/reduce_scatter | solution.py:878
  211.1 353.9 %reduce-scatter.5.cloned.1.call-start = ((), (), s32[]{:S(2)}) async-start(), calls=%async_computation.3 | async-start | bytes 9732096 | tf_op jit(solution)/shard_map/reduce_scatter | solution.py:878
  312.4 2.8 copy-start.7
  312.4 3.9 copy-start.6
  312.4 5.0 copy-start.5
  315.2 3.4 copy-start.4
  316.3 3.5 copy-start.3
  317.5 3.5 copy-start.2
  318.6 3.5 copy-start.1
  323.3 2.3 copy-start.8
Sparse Core Ops, SparseCore 0:
  204.1 99.3 reduce-scatter.8
  309.1 114.0 reduce-scatter.6
  430.1 134.8 reduce-scatter.4

commit v3 on v2

--- a/solution.py
+++ b/solution.py
@@ -138,6 +138,122 @@
             if phase > 0:
                 for copy in self.phase(number, phase - 1):
                     copy.wait()
+            if phase < self.PHASES:
+                for copy in self.phase(number, phase):
+                    copy.start()
+
+
+class Scatter:
+    PHASES = 4
+
+    def __init__(self, place, pieces, sources, kept, outs, buffers, load_sem, send_sem, recv_sem):
+        self.place, self.pieces, self.sources, self.kept, self.outs = place, pieces, sources, kept, outs
+        self.buffers, self.load_sem, self.send_sem, self.recv_sem = buffers, load_sem, send_sem, recv_sem
+
+    @staticmethod
+    def copies(sizes, pieces):
+        return len(pieces) * sum(size - 1 for size in grid_of(sizes))
+
+    @staticmethod
+    def scratch(sizes, pieces, shapes, kept):
+        deep, high, wide, cores = grid_of(sizes)
+        buffers = []
+        for source, first, columns, order in pieces:
+            rows, dtype = shapes[source]
+            near, far = (wide, high) if order == "xy" else (high, wide)
+            block = (rows, columns)
+            shapes_here = [(deep, high, wide) + block, (near - 1, deep, far) + block, (far - 1, deep) + block, (deep,) + block]
+            if not kept[source]:
+                shapes_here.append((deep, high, wide) + block)
+            buffers += [pltpu.VMEM(shape, dtype) for shape in shapes_here]
+        return buffers
+
+    def buffer(self, number, which):
+        place = sum(4 if self.kept[piece[0]] else 5 for piece in self.pieces[:number])
+        return self.buffers[place + which]
+
+    def half(self, number, core):
+        source, first, columns, order = self.pieces[number]
+        return self.sources[source].at[:, :, :, core, :, pl.ds(first, columns)]
+
+    def load(self, number):
+        return pltpu.make_async_copy(self.half(number, self.place.at["c"]), self.buffer(number, 4), self.load_sem.at[number])
+
+    def phase(self, number, phase):
+        place = self.place
+        at = place.at
+        deep, high, wide, cores = place.sizes
+        order = self.pieces[number][3]
+        base = number * sum(size - 1 for size in place.sizes)
+        axis = ("c" + order + "z")[phase]
+        skip = sum(place.size(before) - 1 for before in ("c" + order + "z")[:phase])
+        sums = self.buffer(number, 0)
+        copies = []
+        for step, other in enumerate(place.others(axis)):
+            if phase == 0:
+                source, target = self.half(number, other), sums
+            elif phase == 3:
+                source, target = sums.at[other, at["y"], at["x"]], self.buffer(number, 3).at[at["z"]]
+            else:
+                target = self.buffer(number, phase).at[step]
+                y, x = (other, EVERY) if axis == "y" else (EVERY, other)
+                if phase == 2:
+                    y, x = (other, at["x"]) if axis == "y" else (at["y"], other)
+                source = sums.at[:, y, x]
+            slot = base + skip + step
+            copies.append(
+                pltpu.make_async_remote_copy(
+                    source,
+                    target,
+                    self.send_sem.at[slot],
+                    self.recv_sem.at[slot],
+                    device_id=place.device(**{axis: other}),
+                    device_id_type=MESH,
+                )
+            )
+        return copies
+
+    def absorb(self, number, phase):
+        source, first, columns, order = self.pieces[number]
+        at = self.place.at
+        deep = self.place.sizes[0]
+        sums = self.buffer(number, 0)
+        if phase == 3:
+            slots = self.buffer(number, 3)
+            slots[at["z"]] = sums[at["z"], at["y"], at["x"]]
+            total = slots[0].astype(F32)
+            for slot in range(1, deep):
+                total += slots[slot].astype(F32)
+            self.outs[source][:, first : first + columns] = total
+            return
+
+        @pl.loop(0, deep)
+        def _(z):
+            if phase == 0:
+                own = self.sources[source].at[z, :, :, at["c"], :, pl.ds(first, columns)] if self.kept[source] else self.buffer(number, 4).at[z]
+                view, parts = sums.at[z], [own[...]]
+            else:
+                came = self.buffer(number, phase)
+                parts = [came[step, z] for step in range(came.shape[0])]
+                if phase == 1:
+                    view = sums.at[z, :, at["x"]] if order[0] == "x" else sums.at[z, at["y"]]
+                else:
+                    view = sums.at[z, at["y"], at["x"]]
+            total = view[...].astype(F32)
+            for part in parts:
+                total += part.astype(F32)
+            view[...] = total.astype(view.dtype)
+
+    def advance(self, numbers, phase):
+        for number in numbers:
+            if phase > 0:
+                for copy in self.phase(number, phase - 1):
+                    copy.wait()
+                if phase == 1 and not self.kept[self.pieces[number][0]]:
+                    self.load(number).wait()
+                self.absorb(number, phase - 1)
+            elif not self.kept[self.pieces[number][0]]:
+                self.load(number).start()
             if phase < self.PHASES:
                 for copy in self.phase(number, phase):
                     copy.start()
@@ -571,13 +687,26 @@
                 causal_sum_ref[:, at : at + count] += part
 
 
+def split_columns(number, columns):
+    half = columns // 2
+    return [(number, 0, half, "xy"), (number, half, half, "yx")]
+
+
 def cross_backward_kernel(
     gsecond_ref, first_ref, memory_ref, gains_ref, q_ref, k_ref, v_ref, mixed1_ref, mixed2_ref, lse_ref,
-    wo_ref, cq_ref, ck_ref, cv_ref, co_ref,
-    gmem_ref, gfirst_ref, gm1_ref, ggain_ref, dwo_ref, dcq_ref, dck_ref, dcv_ref, dco_ref,
-    gm_ref, branch_ref, flipped_ref, lse_rows_ref, delta_ref, gq_ref, gk_ref, gv_ref, gqt_ref,
-    *, heads,
+    wo_ref, cq_ref, ck_ref, cv_ref, co_ref, *refs, heads, plan,
 ):
+    count = 2 if plan else 0
+    sources, refs = refs[:count], refs[count:]
+    gmem_ref, gfirst_ref, gm1_ref, ggain_ref, dwo_ref, dcq_ref, dck_ref, dcv_ref, dco_ref, *refs = refs
+    outs, refs = refs[:count], refs[count:]
+    gm_ref, branch_ref, flipped_ref, lse_rows_ref, delta_ref, gq_ref, gk_ref, gv_ref, gqt_ref, *refs = refs
+    if plan:
+        sizes, pieces = plan
+        scatter = Scatter(Place(sizes), pieces, sources, [False] * count, outs, refs[:-3], *refs[-3:])
+        everything = range(len(pieces))
+        scatter.place.meet()
+        scatter.advance(everything, 0)
     length, width = first_ref.shape
     source = memory_ref.shape[0]
     block = 256
@@ -597,9 +726,17 @@
     lse_rows_ref[...] = lse_ref[...].T
     gk_ref[...] = jnp.zeros_like(gk_ref)
     gv_ref[...] = jnp.zeros_like(gv_ref)
-
-    @pl.loop(0, heads // 2)
+    groups = heads // 2
+
+    @pl.loop(0, groups)
     def _(group):
+        if plan:
+            for when, phase in ((1, 1), (groups - 2, 2), (groups - 1, 3)):
+
+                @pl.when(group == when)
+                def _(phase=phase):
+                    scatter.advance(everything, phase)
+
         cols = pl.ds(pl.multiple_of(group * PAIR, PAIR), PAIR)
         backward_head_prepare(cols, gm_ref, mixed2_ref, delta_ref)
         gqt_ref[...] = jnp.zeros_like(gqt_ref)
@@ -656,26 +793,102 @@
         dwo_ref[rows, :] = dot(flipped_ref[rows, :], branch_ref[...]).astype(BF16)
 
     row_blocks(width, block, out_weights)
+    if plan:
+        scatter.advance(everything, 4)
+
+
+def store_shares(ref, cols, value, start):
+    if len(ref.shape) == 2:
+        ref[pl.ds(start, value.shape[0]), cols] = value.astype(BF16)
+    else:
+        deep, high, wide, cores, rows, columns = ref.shape
+        chunk = high * wide * cores * rows
+        ref[start // chunk, :, :, :, :, cols] = value.reshape(high, wide, cores, rows, value.shape[1]).astype(BF16)
+
+
+TILE = 16
+
+
+def fill_tiles(tiles_ref, gtable, ggains):
+    deep, high, wide, cores, rows, lanes = tiles_ref.shape
+    devices = deep * high * wide * cores
+    width = ggains[0].shape[1]
+    share = width // devices
+    lane = lax.broadcasted_iota(jnp.int32, (SUB, width), 1)
+    select = jnp.where(lax.rem(lane, share) == lax.broadcasted_iota(jnp.int32, (SUB, width), 0), 1.0, 0.0)
+    first = share * lax.broadcasted_iota(jnp.int32, (devices, width), 0)
+    lane = lax.broadcasted_iota(jnp.int32, (devices, width), 1)
+    own = (lane >= first) & (lane < first + share)
+    parts = [exact_dot(jnp.where(own, ggain, 0.0), select, 1, 1) for ggain in ggains]
+    tiles_ref[...] = jnp.zeros_like(tiles_ref)
+    heads, buckets = gtable.shape
+    for device in range(devices):
+        at = tuple(int(part) for part in (device // (high * wide * cores), device // (wide * cores) % high, device // cores % wide, device % cores))
+        tiles_ref[(*at, slice(0, heads), slice(0, buckets))] = gtable
+        for number, part in enumerate(parts):
+            row = TILE - len(parts) + number
+            tiles_ref[(*at, slice(row, row + 1), EVERY)] = part[device : device + 1]
+
+
+REST = 6
+
+
+def self_pieces(down_columns, columns):
+    first = split_columns(0, down_columns) + [(1, 0, columns, "xy"), (2, 0, columns, "yx")]
+    rest = [(3, 0, columns, "xy"), (4, 0, columns, "yx")] + split_columns(5, columns)
+    half = columns // 2
+    early = [(REST, 0, half, "xy"), (REST + 1, 0, half, "yx"), (REST + 2, 0, half, "xy")]
+    late = [(REST, half, half, "yx"), (REST + 1, half, half, "xy"), (REST + 2, half, half, "yx"), (REST + 3, 0, SUB, "xy")]
+    pieces, groups = [], []
+    for group in (first, rest, early, late):
+        groups.append(range(len(pieces), len(pieces) + len(group)))
+        pieces += group
+    return pieces, groups
 
 
 def self_backward_kernel(
     limit_ref, tokens_ref, gains_ref, table_ref, map_ref, q_ref, k_ref, v_ref, mixed_ref, lse_ref, gm_ref, gfirst_ref,
-    wq_ref, wk_ref, wv_ref,
-    gtokens_ref, ggain_ref, gtable_ref, dwq_ref, dwk_ref, dwv_ref,
-    bias_ref, causal_ref, two_ref, flipped_ref, lse_rows_ref, delta_ref, gq_ref, gk_ref, gv_ref, gqt_ref,
-    causal_sum_ref, two_sum_ref, sums_ref,
-    *, band, heads,
+    ggain2_ref, ggain3_ref, wq_ref, wk_ref, wv_ref, *refs, band, heads, plan,
 ):
+    count = REST if plan else 0
+    sources, refs = refs[:count], refs[count:]
+    gtokens_ref, refs = refs[0], refs[1:]
+    if plan:
+        outs, refs = refs[: REST + 3], refs[REST + 3 :]
+        gtable_ref, *ggain_refs = refs[:4]
+        refs = refs[4:]
+    else:
+        ggain_ref, gtable_ref, dwq_ref, dwk_ref, dwv_ref, *refs = refs
+    (
+        bias_ref, causal_ref, two_ref, flipped_ref, lse_rows_ref, delta_ref, gq_ref, gk_ref, gv_ref, gqt_ref,
+        causal_sum_ref, two_sum_ref, sums_ref, *refs,
+    ) = refs
     length, width = tokens_ref.shape
     block = 256
+    groups = heads // 2
+    if plan:
+        sizes, pieces, (first, rest, early, late) = plan
+        dwq_ref, dwk_ref, dwv_ref, tiles_ref, tile_ref, ggain_ref, *refs = refs
+        scatter = Scatter(
+            Place(sizes), pieces, (*sources, dwq_ref, dwk_ref, dwv_ref, tiles_ref), [False] * REST + [True] * 4,
+            (*outs, tile_ref), refs[:-3], *refs[-3:],
+        )
+        scatter.place.meet()
+        scatter.advance(first, 0)
+        scatter.advance(rest, 0)
     bias_ref[...] = bias_rows(table_ref, map_ref, band, "keys")
     lse_rows_ref[...] = lse_ref[...].T
     gk_ref[...] = jnp.zeros_like(gk_ref)
     gv_ref[...] = jnp.zeros_like(gv_ref)
     sums_ref[...] = jnp.zeros_like(sums_ref)
 
-    @pl.loop(0, heads // 2)
-    def _(group):
+    def flip_normed(rows):
+        value = tokens_ref[rows, :].astype(F32)
+        flipped_ref[:, rows] = (value * rms(value) * gains_ref[0:1, :]).astype(BF16).T
+
+    row_blocks(length, block, flip_normed)
+
+    def group_step(group):
         cols = pl.ds(pl.multiple_of(group * PAIR, PAIR), PAIR)
         backward_head_prepare(cols, gm_ref, mixed_ref, delta_ref)
         gqt_ref[...] = jnp.zeros_like(gqt_ref)
@@ -695,13 +908,61 @@
 
         gq_ref[:, cols] = gqt_ref[...].T.astype(BF16)
 
+    rows_each = width // (sizes["dp"] // (sizes["fsdp"] // 2)) if plan else block
+
+    def weights(cols):
+        @pl.loop(0, width // rows_each)
+        def _(index):
+            start = pl.multiple_of(index * rows_each, 64)
+            flipped = flipped_ref[pl.ds(start, rows_each), :]
+            for target, grad in ((dwq_ref, gq_ref), (dwk_ref, gk_ref), (dwv_ref, gv_ref)):
+                store_shares(target, cols, dot(flipped, grad[:, cols]), start)
+
+    half_groups = groups // 2
+    low, high = pl.ds(0, width // 2), pl.ds(width // 2, width // 2)
+
+    @pl.loop(0, groups)
+    def _(group):
+        if plan:
+
+            @pl.when(group == 1)
+            def _():
+                scatter.advance(first, 1)
+
+            @pl.when(group == half_groups)
+            def _():
+                weights(low)
+                scatter.advance(early, 0)
+                scatter.advance(first, 2)
+                scatter.advance(rest, 1)
+
+            @pl.when(group == half_groups + 1)
+            def _():
+                scatter.advance(first, 3)
+                scatter.advance(early, 1)
+
+            @pl.when(group == groups - 1)
+            def _():
+                scatter.advance(rest, 2)
+                scatter.advance(early, 2)
+
+        group_step(group)
+
+    if plan:
+        scatter.advance(first, 4)
+        scatter.advance(rest, 3)
+        weights(high)
+        scatter.advance(early, 3)
+        scatter.advance(late[:3], 0)
+    else:
+        weights(low)
+        weights(high)
     hot, unused = one_hot(map_ref, band, "keys")
-    gtable_ref[...] = exact_dot(sums_ref[...], hot, 1, 1)
+    gtable = exact_dot(sums_ref[...], hot, 1, 1)
     ggain_ref[...] = jnp.zeros_like(ggain_ref)
 
     def tokens_grad(rows):
         value = tokens_ref[rows, :].astype(F32)
-        flipped_ref[:, rows] = (value * rms(value) * gains_ref[0:1, :]).astype(BF16).T
         grad = dot(gq_ref[rows, :], wq_ref[...], 1, 1)
         grad += dot(gk_ref[rows, :], wk_ref[...], 1, 1)
         grad += dot(gv_ref[rows, :], wv_ref[...], 1, 1)
@@ -709,15 +970,27 @@
         ggain_ref[0:1, :] += ggain
         gtokens_ref[rows, :] = back + gfirst_ref[rows, :]
 
-    row_blocks(length, block, tokens_grad)
-
-    def weights(rows):
-        flipped = flipped_ref[rows, :]
-        dwq_ref[rows, :] = dot(flipped, gq_ref[...]).astype(BF16)
-        dwk_ref[rows, :] = dot(flipped, gk_ref[...]).astype(BF16)
-        dwv_ref[rows, :] = dot(flipped, gv_ref[...]).astype(BF16)
-
-    row_blocks(width, block, weights)
+    if plan:
+        scatter.advance(late[:3], 1)
+        row_blocks(length, block, tokens_grad)
+        fill_tiles(tiles_ref, gtable, [ggain_ref[0:1, :], ggain2_ref[0:1, :], ggain3_ref[0:1, :]])
+        scatter.advance(late[3:], 0)
+        scatter.advance(late[:3], 2)
+        scatter.advance(late[3:], 1)
+        scatter.advance(rest, 4)
+        scatter.advance(late[:3], 3)
+        scatter.advance(late[3:], 2)
+        scatter.advance(early, 4)
+        scatter.advance(late[3:], 3)
+        scatter.advance(late, 4)
+        tile = tile_ref[...]
+        gtable_ref[...] = tile.T[:NB, :heads]
+        for number, ref in enumerate(ggain_refs):
+            row = TILE - len(ggain_refs) + number
+            ref[...] = tile[row : row + 1, : ref.shape[1]]
+    else:
+        row_blocks(length, block, tokens_grad)
+        gtable_ref[...] = gtable.T
 
 
 def vmem(*shapes):
@@ -834,61 +1107,100 @@
     )(second, gout, gains, gate_full, up_full, down)
 
     square = like((width, width), BF16)
-    cross_out_shapes = [like((source, width), F32), act32, act, ggain_shape] + [square] * 5
+    cross_shapes = [like((source, width), F32), act32, act, ggain_shape] + [square] * 5
     cross_in = (gsecond, first, memory, gains, q2, k2, v2, mixed1, mixed2, lse2)
-    gmem, gfirst, gm1, ggain_cross, dwo, dcq, dck, dcv, dco = pl.pallas_call(
-        functools.partial(cross_backward_kernel, heads=heads),
-        out_shape=cross_out_shapes,
+    cross_scratch = vmem(
+        ((length, width), BF16), ((length, width), BF16), ((width, length), BF16), ((SUB, length), F32),
+        ((8, length), F32), ((length, width), BF16), ((source, width), BF16), ((source, width), BF16),
+        ((PAIR, length), F32),
+    )
+    grid = grid_of(sizes)
+
+    def shares(grads):
+        return [grad.reshape(grid + (grad.shape[0] // devices, grad.shape[1])) for grad in grads]
+
+    def scatter_scratch(pieces, shapes, kept):
+        count = Scatter.copies(sizes, pieces)
+        return Scatter.scratch(sizes, pieces, shapes, kept) + [
+            pltpu.SemaphoreType.DMA((number,)) for number in (len(pieces), count, count)
+        ]
+
+    plan, sources, gate_shapes, scratch = None, [], [], []
+    if own:
+        sources = shares([dgate, dup])
+        pieces = [(0, 0, ff, "xy"), (1, 0, ff, "yx")]
+        plan = (sizes, pieces)
+        gate_shapes = [like(part.shape[-2:], F32) for part in sources]
+        scratch = scatter_scratch(pieces, [(part.shape[-2], BF16) for part in sources], [False, False])
+    cross_shapes += gate_shapes
+    gmem, gfirst, gm1, ggain_cross, dwo, dcq, dck, dcv, dco, *feed_grads = pl.pallas_call(
+        functools.partial(cross_backward_kernel, heads=heads, plan=plan),
+        out_shape=cross_shapes,
         grid=(1,),
-        in_specs=[full(a.shape) for a in cross_in] + [full((width, width))] * 5,
-        out_specs=[full(o.shape) for o in cross_out_shapes],
-        scratch_shapes=vmem(
-            ((length, width), BF16), ((length, width), BF16), ((width, length), BF16), ((SUB, length), F32),
-            ((8, length), F32), ((length, width), BF16), ((source, width), BF16), ((source, width), BF16),
-            ((PAIR, length), F32),
-        ),
-        compiler_params=params(),
+        in_specs=[full(a.shape) for a in cross_in] + [full((width, width))] * 5 + [remote] * len(sources),
+        out_specs=[full(o.shape) for o in cross_shapes],
+        scratch_shapes=cross_scratch + scratch,
+        compiler_params=params(collective_id=1, has_side_effects=True) if own else params(),
         name="cross_backward",
-    )(*cross_in, *attention[3:])
-
-    self_out_shapes = [act32, ggain_shape, like((heads, NB), F32)] + [square] * 3
-    self_in = (tokens, gains, bias_table, bucket_map, q1, k1, v1, mixed1, lse1, gm1, gfirst)
-    gtokens, ggain_self, gtable, dwq, dwk, dwv = pl.pallas_call(
-        functools.partial(self_backward_kernel, band=band, heads=heads),
-        out_shape=self_out_shapes,
+    )(*cross_in, *attention[3:], *sources)
+
+    self_in = (tokens, gains, bias_table, bucket_map, q1, k1, v1, mixed1, lse1, gm1, gfirst, ggain_cross, ggain_feed)
+    self_scratch = vmem(
+        ((heads, band.width), F32), ((SUB, band.causal), F32), ((SUB, band.two_way), F32), ((width, length), BF16),
+        ((SUB, length), F32), ((8, length), F32), ((length, width), BF16), ((length, width), BF16),
+        ((length, width), BF16), ((PAIR, length), F32), ((SUB, band.causal), F32), ((SUB, band.two_way), F32),
+        ((heads, band.width), F32),
+    )
+    plan, sources, scratch = None, [], []
+    table_shape = like((NB, heads), F32)
+    if own:
+        sources = shares([ddown, dco, dwo, dcq, dck, dcv])
+        pieces, groups = self_pieces(width, width)
+        plan = (sizes, pieces, groups)
+        share = width // devices
+        kept = [False] * REST + [True] * 4
+        shapes = [(part.shape[-2], BF16) for part in sources] + [(share, BF16)] * 3 + [(TILE, F32)]
+        self_shapes = [act32] + [like(part.shape[-2:], F32) for part in sources] + [like((share, width), F32)] * 3
+        self_shapes += [table_shape] + [like((1, share), F32)] * 3
+        scratch = vmem(*[(grid + (share, width), BF16)] * 3, (grid + (TILE, SUB), F32), ((TILE, SUB), F32), ((8, width), F32))
+        scratch += scatter_scratch(pieces, shapes, kept)
+    else:
+        self_shapes = [act32, ggain_shape, table_shape] + [square] * 3
+    gtokens, *grads = pl.pallas_call(
+        functools.partial(self_backward_kernel, band=band, heads=heads, plan=plan),
+        out_shape=self_shapes,
         grid=(1,),
-        in_specs=[scalar] + [full(a.shape) for a in self_in] + [full((width, width))] * 3,
-        out_specs=[full(o.shape) for o in self_out_shapes],
-        scratch_shapes=vmem(
-            ((heads, band.width), F32), ((SUB, band.causal), F32), ((SUB, band.two_way), F32), ((width, length), BF16),
-            ((SUB, length), F32), ((8, length), F32), ((length, width), BF16), ((length, width), BF16),
-            ((length, width), BF16), ((PAIR, length), F32), ((SUB, band.causal), F32), ((SUB, band.two_way), F32),
-            ((heads, band.width), F32),
-        ),
-        compiler_params=params(),
+        in_specs=[scalar] + [full(a.shape) for a in self_in] + [full((width, width))] * 3 + [remote] * len(sources),
+        out_specs=[full(o.shape) for o in self_shapes],
+        scratch_shapes=self_scratch + scratch,
+        compiler_params=params(collective_id=2, has_side_effects=True) if own else params(),
         name="self_backward",
-    )(prefix, *self_in, *attention[:3])
-
-    table_grad = lax.psum(gtable.T, AXES)
-    ggains = lax.psum_scatter(
-        jnp.stack([ggain_self[0], ggain_cross[0], ggain_feed[0]]), AXES, scatter_dimension=1, tiled=True
-    )
-
-    def scatter(parts):
-        return lax.psum_scatter(jnp.concatenate(parts, axis=1), AXES, scatter_dimension=0, tiled=True).astype(F32)
-
-    feed_grads = scatter([dgate, dup])
-    down_grad = lax.psum_scatter(ddown, AXES, scatter_dimension=0, tiled=True).astype(F32)
-    squares = scatter([dwq, dwk, dwv, dwo, dcq, dck, dcv, dco])
-    pieces = [squares[:, i * width : (i + 1) * width] for i in range(8)]
+    )(prefix, *self_in, *attention[:3], *sources)
+
+    if own:
+        ddown, dco, dwo, dcq, dck, dcv, dwq, dwk, dwv, table_grad, *ggains = grads
+        ggains = [ggain.reshape(-1) for ggain in ggains]
+        dgate, dup = feed_grads
+    else:
+        ggain_self, gtable, dwq, dwk, dwv = grads
+        table_grad = lax.psum(gtable, AXES)
+
+        def scatter(parts, axis):
+            return lax.psum_scatter(jnp.concatenate(parts, axis=1 - axis), AXES, scatter_dimension=axis, tiled=True)
+
+        ggains = scatter([ggain_self[:1], ggain_cross[:1], ggain_feed[:1]], 1)
+        dgate, dup = jnp.split(scatter([dgate, dup], 0).astype(F32), 2, axis=1)
+        ddown = scatter([ddown], 0).astype(F32)
+        squares = scatter([dwq, dwk, dwv, dwo, dcq, dck, dcv, dco], 0).astype(F32)
+        dwq, dwk, dwv, dwo, dcq, dck, dcv, dco = jnp.split(squares, 8, axis=1)
     return (
         output.reshape(inputs.shape),
         gtokens.reshape(inputs.shape),
         gmem.reshape(encoded.shape),
         table_grad,
-        ggains[0], pieces[0], pieces[1], pieces[2], pieces[3],
-        ggains[1], pieces[4], pieces[5], pieces[6], pieces[7],
-        ggains[2], feed_grads[:, :ff], feed_grads[:, ff:], down_grad,
+        ggains[0], dwq, dwk, dwv, dwo,
+        ggains[1], dcq, dck, dcv, dco,
+        ggains[2], dgate, dup, ddown,
     )
 
 

time: 574 us -> 371 us (0.65)
  waiting for transfers between devices: 196 us -> 0 us
  Pallas kernels: 296 us -> 353 us
  blocking collectives: 39.2 us -> 0 us
  between operations: 14.5 us -> 1.42 us
  other arithmetic: 6.85 us -> 0 us
    reduce_scatter x3 -> x0, waiting for transfers between devices: 196 us -> none  [the longest x2 196 us: scatter(): lax.psum_scatter(jnp.concatenate(parts, axis=1), AXES, scatter_dimension=...]
    pallas_call x1, Pallas kernels: 54.3 us -> 94.3 us  [per_device(): pl.pallas_call(functools.partial(self_backward_kernel, band=band, heads=h...]
    psum x1 -> x0, blocking collectives: 39.2 us -> none  [per_device(): table_grad = lax.psum(gtable.T, AXES)]
    pallas_call x1, Pallas kernels: 47 us -> 63.9 us  [per_device(): pl.pallas_call(functools.partial(cross_backward_kernel, heads=heads, plan...]
    unnamed x27 -> x48, local copies, waits for them, and re-layouts: 12.8 us -> 16.5 us
  transfers between devices with their start and end apart: 3 -> 0, of which waited for: 2 -> 0; matrix products, arithmetic and copies ran while one was open for 4% -> 0% of each run, Pallas kernels for 18% -> 0%
where the time goes in v3:
time: 371 us; the launch traced here: 370 us
  Pallas kernels  353 us (95%)
  local copies, waits for them, and re-layouts  16.5 us (4%)
    pallas_call x1, Pallas kernels, per_device(): pl.pallas_call(functools.partial(forward_kernel, band=band, heads=heads,...  132 us
    pallas_call x1, Pallas kernels, per_device(): pl.pallas_call(functools.partial(self_backward_kernel, band=band, heads=h...  94.3 us
    pallas_call x1, Pallas kernels, per_device(): pl.pallas_call(functools.partial(cross_backward_kernel, heads=heads, plan...  63.9 us
    pallas_call x1, Pallas kernels, per_device(): pl.pallas_call(feed_kernel, out_shape=feed_out, grid=(ff // fblock,), in_...  62.4 us
    unnamed x48, local copies, waits for them, and re-layouts  16.5 us

profile of v3, /device:TPU:0, one launch (start us, length us, event | category | flops | bytes accessed | tf_op | source)
XLA Modules:
  0.0 370.5 jit_solution(16395220419728365508)
XLA Ops:
  1.3 1.4 copy.38.table_ref
  2.7 132.1 %forward.1 = (bf16[4,2,2,48,768]{4,3,2,1,0:T(8,128)(2,1)}, bf16[4,2,2,48,768]{4,3,2,1,0:T(8,128)(2,1)}, bf16[4,2,2,48,768]{4,3,2,1,0:T(8,128)(2,1)}, bf16[4,2,2,...) custom-call(s32[1]{0:T(128)S(6)} %copy.57.limit_ref, ...), custom_call_target="tpu_custom_call" | custom-call | tf_op jit(solution)/shard_map/forward/pallas_call | solution.py:1057
  134.8 62.4 %feed.1 = (bf16[1024,768]{1,0:T(8,128)(2,1)}, f32[1024,768]{1,0:T(8,128)}, f32[8,768]{1,0:T(8,128)}, bf16[768,2048]{1,0:T(8,128)(2,1)}, bf16[768,2048]{1,0:T(8,128)(2,1)}, /*index=5*/bf16[2048,768]{1,0:T(8,128)(2,1)}) custom-call(f32[1024,768]{1,0:T(8,128)} %get-tuple-element.73.second_ref, bf16[1024,768]{1,0:T(8,128)(2,1)} %bitcast.43, ...), custom_call_target="tpu_custom_call" | custom-call | tf_op jit(solution)/shard_map/feed/pallas_call | solution.py:1085
  197.1 63.9 %cross_backward.1 = (f32[512,768]{1,0:T(8,128)}, f32[1024,768]{1,0:T(8,128)}, bf16[1024,768]{1,0:T(8,128)(2,1)}, f32[8,768]{1,0:T(8,128)}, bf16[768,768]{1,0:T(8...) custom-call(f32[1024,768]{1,0:T(8,128)} %get-tuple-element.84.gsecon, ...), custom_call_target="tpu_custom_call" | custom-call | tf_op jit(solution)/shard_map/cross_backward/pallas_call | solution.py:1136
  261.0 94.3 %self_backward.1 = (f32[1024,768]{1,0:T(8,128)}, f32[64,768]{1,0:T(8,128)}, f32[24,768]{1,0:T(8,128)}, f32[24,768]{1,0:T(8,128)}, f32[24,768]{1,0:T(8,128)}, /*i...) custom-call(s32[1]{0:T(128)S(6)} %copy.57.limit_ref, ...), custom_call_target="tpu_custom_call" | custom-call | tf_op jit(solution)/shard_map/self_backward/pallas_call | solution.py:1169
  355.3 1.4 copy.40
  356.7 0.0 copy-start
  356.7 3.9 %copy.58 = f32[1,1024,768]{2,1,0:T(8,128)} copy(f32[1,1024,768]{2,1,0:T(8,128)} %bitcast.34) | data formatting | bytes 6291456
  360.5 0.0 copy-done
  360.5 0.0 copy-start.14
  360.6 0.0 copy-start.9
  360.6 0.0 copy-start.8
  360.6 0.0 copy-start.13
  360.6 0.0 copy-start.7
  360.6 0.0 copy-start.6
  360.6 0.0 copy-start.5
  360.6 0.0 copy-start.4
  360.6 0.0 copy-start.12
  360.6 0.0 copy-start.2
  360.6 1.1 copy.59
  361.8 0.0 copy-done.14
  361.8 0.5 copy.60
  362.3 0.0 copy-done.11
  362.3 0.6 copy.61
  362.9 0.0 copy-done.10
  362.9 0.6 copy.62
  363.6 0.0 copy-done.9
  363.6 0.6 copy.63
  364.2 0.0 copy-done.8
  364.2 0.6 copy.64
  364.8 0.0 copy-done.13
  364.9 0.5 copy.65
  365.4 0.0 copy-done.7
  365.4 0.6 copy.66
  366.0 0.0 copy-done.6
  366.0 0.6 copy.67
  366.6 0.0 copy-done.5
  366.6 0.6 copy.68
  367.3 0.0 copy-done.4
  367.3 0.6 copy.69
  367.9 0.0 copy-done.12
  367.9 0.5 copy.70
  368.4 0.0 copy-done.2
  368.4 0.7 copy.71
  369.1 0.0 copy-done.1
  369.1 0.7 copy.72
  369.8 0.0 copy-done.3
  369.8 0.7 copy.73
  (4 shorter events, 0.0 us)
Async XLA Ops:
  356.7 3.9 %copy-start = (f32[512,768]{1,0:T(8,128)S(1)}, f32[512,768]{1,0:T(8,128)}, u32[]{:S(2)}) copy-start(f32[512,768]{1,0:T(8,128)} %get-tuple-element.112) | copy-start | bytes 4718596
  360.5 1.2 copy-start.14
  360.5 1.8 copy-start.11
  360.5 2.4 copy-start.10
  360.6 3.0 copy-start.9
  360.6 3.7 copy-start.8
  360.6 4.3 %copy-start.13 = (f32[1,24]{1,0:T(1,128)S(1)}, f32[1,24]{1,0:T(1,128)}, u32[]{:S(2)}) copy-start(f32[1,24]{1,0:T(1,128)} %get-tuple-element.119) | copy-start | bytes 292
  360.6 4.8 %copy-start.7 = (f32[24,768]{1,0:T(8,128)S(1)}, f32[24,768]{1,0:T(8,128)}, u32[]{:S(2)}) copy-start(f32[24,768]{1,0:T(8,128)} %get-tuple-element.174) | copy-start | bytes 221188
  360.6 5.4 %copy-start.6 = (f32[24,768]{1,0:T(8,128)S(1)}, f32[24,768]{1,0:T(8,128)}, u32[]{:S(2)}) copy-start(f32[24,768]{1,0:T(8,128)} %get-tuple-element.175) | copy-start | bytes 221188
  360.6 6.0 %copy-start.5 = (f32[24,768]{1,0:T(8,128)S(1)}, f32[24,768]{1,0:T(8,128)}, u32[]{:S(2)}) copy-start(f32[24,768]{1,0:T(8,128)} %get-tuple-element.176) | copy-start | bytes 221188
  360.6 6.7 %copy-start.4 = (f32[24,768]{1,0:T(8,128)S(1)}, f32[24,768]{1,0:T(8,128)}, u32[]{:S(2)}) copy-start(f32[24,768]{1,0:T(8,128)} %get-tuple-element.177) | copy-start | bytes 221188
  360.6 7.3 %copy-start.12 = (f32[1,24]{1,0:T(1,128)S(1)}, f32[1,24]{1,0:T(1,128)}, u32[]{:S(2)}) copy-start(f32[1,24]{1,0:T(1,128)} %get-tuple-element.124) | copy-start | bytes 292
  360.6 7.8 %copy-start.2 = (f32[24,2048]{1,0:T(8,128)S(1)}, f32[24,2048]{1,0:T(8,128)}, u32[]{:S(2)}) copy-start(f32[24,2048]{1,0:T(8,128)} %get-tuple-element.179) | copy-start | bytes 589828
  361.8 7.3 %copy-start.1 = (f32[24,2048]{1,0:T(8,128)S(1)}, f32[24,2048]{1,0:T(8,128)}, u32[]{:S(2)}) copy-start(f32[24,2048]{1,0:T(8,128)} %get-tuple-element.180) | copy-start | bytes 589828
  361.8 8.0 %copy-start.3 = (f32[64,768]{1,0:T(8,128)S(1)}, f32[64,768]{1,0:T(8,128)}, u32[]{:S(2)}) copy-start(f32[64,768]{1,0:T(8,128)} %get-tuple-element.181) | copy-start | bytes 589828

commit v4 on v3

--- a/solution.py
+++ b/solution.py
@@ -41,6 +41,7 @@
 
 class Place:
     def __init__(self, sizes):
+        self.grid = sizes
         self.sizes = grid_of(sizes)
         across, inner = lax.axis_index("dp"), lax.axis_index("fsdp")
         deep, high, wide, cores = self.sizes
@@ -84,63 +85,76 @@
         self.local_sem, self.send_sem, self.recv_sem = local_sem, send_sem, recv_sem
 
     @staticmethod
+    def each(sizes):
+        grid = grid_of(sizes)
+        return sum(size - 1 for size in grid[:3]) + max(grid[:3])
+
+    @staticmethod
     def copies(sizes, pieces):
-        return len(pieces) * sum(size - 1 for size in grid_of(sizes))
-
-    def view(self, piece, *index):
+        return len(pieces) * Gather.each(sizes)
+
+    def view(self, piece, held):
         array, first, rows, order = piece
         start = self.place.at["c"] * self.shards[array].shape[0] + first
-        return self.outs[array].at[(*index, pl.ds(pl.multiple_of(start, 8), rows), EVERY)]
-
-    def phase(self, number, phase):
+        where = [held.get(axis, EVERY) for axis in "zyx"]
+        return self.outs[array].at[(*where, pl.ds(pl.multiple_of(start, 8), rows), EVERY)]
+
+    def phase(self, number, phase, core):
         piece = self.pieces[number]
-        place = self.place
-        at = place.at
-        deep, high, wide, cores = place.sizes
+        place, at = self.place, self.place.at
         array, first, rows, order = piece
-        base = number * sum(size - 1 for size in place.sizes)
-        if phase == 0:
-            axis, skip = "z", 0
-            source = self.shards[array].at[pl.ds(first, rows), :]
-            target = self.view(piece, at["z"], at["y"], at["x"])
-        elif phase == 3:
-            axis, skip = "c", deep + high + wide - 3
-            source = target = self.view(piece, EVERY, EVERY, EVERY)
-        else:
-            axis = order[phase - 1]
-            skip = deep - 1 + (phase - 1) * (high - 1)
-            if phase == 1:
-                source = self.view(piece, EVERY, at["y"], at["x"])
-            elif axis == "y":
-                source = self.view(piece, EVERY, at["y"], EVERY)
-            else:
-                source = self.view(piece, EVERY, EVERY, at["x"])
-            target = source
+        slot = number * self.each(place.grid) + sum(place.size(axis) - 1 for axis in order[:phase])
         copies = []
-        for step, other in enumerate(place.others(axis)):
-            slot = base + skip + step
+
+        def send(source, target, **moved):
             copies.append(
                 pltpu.make_async_remote_copy(
                     source,
                     target,
-                    self.send_sem.at[slot],
-                    self.recv_sem.at[slot],
-                    device_id=place.device(**{axis: other}),
+                    self.send_sem.at[slot + len(copies)],
+                    self.recv_sem.at[slot + len(copies)],
+                    device_id=place.device(**moved),
                     device_id_type=MESH,
                 )
             )
+
+        other_core = place.others("c")[0]
+        last = order[2]
+        if core:
+            slot = number * self.each(place.grid) + sum(place.size(axis) - 1 for axis in order)
+            if phase == 2:
+                part = self.view(piece, {last: at[last]})
+                send(part, part, c=other_core)
+            else:
+                slot += 1
+                for other in place.others(last):
+                    part = self.view(piece, {last: other})
+                    send(part, part, c=other_core)
+            return copies
+        axis = order[phase]
+        target = self.view(piece, {later: at[later] for later in order[phase:]})
+        source = self.shards[array].at[pl.ds(first, rows), :] if phase == 0 else target
+        for other in place.others(axis):
+            send(source, target, **{axis: other})
         if phase == 0:
             copies.append(pltpu.make_async_copy(source, target, self.local_sem.at[number]))
         return copies
 
     def advance(self, numbers, phase):
         for number in numbers:
-            if phase > 0:
-                for copy in self.phase(number, phase - 1):
-                    copy.wait()
-            if phase < self.PHASES:
-                for copy in self.phase(number, phase):
-                    copy.start()
+            waits, starts = [], []
+            if 0 < phase < 4:
+                waits = self.phase(number, phase - 1, False)
+            if phase < 3:
+                starts = self.phase(number, phase, False)
+            if phase in (2, 3):
+                starts += self.phase(number, phase, True)
+            if phase == 4:
+                waits = self.phase(number, 2, True) + self.phase(number, 3, True)
+            for copy in waits:
+                copy.wait()
+            for copy in starts:
+                copy.start()
 
 
 class Scatter:
@@ -421,14 +435,19 @@
 
 def gather_pieces(rows, down_rows):
     head, tail = rows // 3 // 8 * 8, rows - rows // 3 // 8 * 8
-    first = [(0, 0, rows, "xy"), (1, 0, rows, "yx"), (2, 0, head, "xy"), (2, head, tail, "yx"), (11, 0, 8, "xy")]
-    rest = [(3, 0, rows, "xy"), (4, 0, rows, "yx"), (5, 0, rows, "xy"), (6, 0, rows, "yx")]
-    rest += [(7, 0, tail, "xy"), (7, tail, head, "yx")]
-    feed = [(8, 0, rows, "xy"), (9, 0, rows, "yx")]
-    feed += [(10, 0, down_rows // 2, "xy"), (10, down_rows // 2, down_rows // 2, "yx")]
-    pieces = first + rest + feed
-    numbers = list(range(len(pieces)))
-    groups = numbers[: len(first)], numbers[len(first) : len(first) + len(rest)], numbers[len(first) + len(rest) :]
+    half = down_rows // 2
+    table = {
+        "qk": [(0, 0, rows, "zxy"), (1, 0, rows, "zyx"), (11, 0, 8, "zxy")],
+        "v": [(2, 0, head, "xzy"), (2, head, tail, "yzx")],
+        "out": [(3, 0, rows, "zxy"), (4, 0, rows, "zyx"), (7, 0, tail, "zxy"), (7, tail, head, "zyx")],
+        "memory": [(5, 0, rows, "xzy"), (6, 0, rows, "yzx")],
+        "gate": [(8, 0, rows, "zxy"), (9, 0, rows, "zyx")],
+        "down": [(10, 0, half, "xzy"), (10, half, half, "yzx")],
+    }
+    pieces, groups = [], {}
+    for name, group in table.items():
+        groups[name] = range(len(pieces), len(pieces) + len(group))
+        pieces += group
     return pieces, groups
 
 
@@ -448,14 +467,14 @@
     ) = refs
     length, width = tokens_ref.shape
     if plan:
-        sizes, pieces, (soon, later, feed) = plan
+        sizes, pieces, groups = plan
         place = Place(sizes)
         gather = Gather(place, pieces, (*shards, share_ref), gathered, *gather_sems)
 
     def advance(*steps):
         if plan:
             for numbers, phase in steps:
-                gather.advance({"soon": soon, "later": later, "feed": feed}[numbers], phase)
+                gather.advance(groups[numbers], phase)
 
     def load(number):
         return pltpu.make_async_copy(gathered[number].reshape(width, width), weights_ref.at[number], load_sem.at[number])
@@ -469,13 +488,14 @@
         for number, gain_ref in enumerate(gain_refs):
             share_ref[number : number + 1, : gain_ref.shape[1]] = gain_ref[...].astype(F32)
         place.meet()
-    advance(("soon", 0))
+    advance(("qk", 0), ("v", 0), ("memory", 0))
     bias_ref[...] = bias_rows(table_ref, map_ref, band, "queries")
     lse1_ref[...] = jnp.zeros_like(lse1_ref)
     lse2_ref[...] = jnp.zeros_like(lse2_ref)
     mixed1_ref[...] = jnp.zeros_like(mixed1_ref)
     mixed2_ref[...] = jnp.zeros_like(mixed2_ref)
-    advance(("soon", 1), ("later", 0), ("feed", 0), ("soon", 2), ("soon", 3), ("later", 1), ("soon", 4))
+    advance(("v", 1), ("out", 0), ("memory", 1), ("qk", 1), ("gate", 0), ("down", 0), ("qk", 2), ("v", 2))
+    advance(("qk", 3), ("v", 3), ("out", 1), ("qk", 4), ("v", 4))
     for number in range(3):
         load(number).start()
     if plan:
@@ -496,25 +516,30 @@
         k1_ref[rows, :] = dot(normed, weights_ref[1]).astype(BF16)
         v1_ref[rows, :] = dot(normed, weights_ref[2]).astype(BF16)
 
-    row_blocks(length, 256, project_self)
-    advance(("later", 2))
+    for start in range(0, length, length // 2):
+        project_self(pl.ds(start, length // 2))
+        if start == 0:
+            advance(("out", 2))
 
     @pl.loop(0, heads)
     def _(head):
         fill_bands(head, bias_ref, band, causal_ref, two_ref)
         self_forward_head(head, limit_ref[0], q1_ref, k1_ref, v1_ref, causal_ref, two_ref, band, mixed1_ref, lse1_ref)
 
-        @pl.when(head == heads // 4)
-        def _():
-            advance(("feed", 1), ("later", 3))
-
-        @pl.when(head == heads // 2)
-        def _():
-            advance(("later", 4))
-            for number in range(3, ATTENTION):
-                load(number).start()
-            advance(("feed", 2))
-
+        for when, steps in (
+            (1, (("out", 3), ("memory", 2))),
+            (4, (("out", 4), ("down", 1))),
+            (6, (("memory", 3),)),
+            (8, (("memory", 4), ("gate", 1))),
+        ):
+
+            @pl.when(head == when * heads // 12)
+            def _(when=when, steps=steps):
+                advance(*steps)
+                for number in {4: (3, 4, 7), 8: (5, 6)}.get(when, ()):
+                    load(number).start()
+
+    advance(("gate", 2))
     for number in range(3, ATTENTION):
         load(number).wait()
 
@@ -522,7 +547,7 @@
         k2_ref[rows, :] = dot(memory_ref[rows, :], weights_ref[5]).astype(BF16)
         v2_ref[rows, :] = dot(memory_ref[rows, :], weights_ref[6]).astype(BF16)
 
-    row_blocks(memory_ref.shape[0], 256, project_memory)
+    row_blocks(memory_ref.shape[0], 512, project_memory)
 
     def project_cross(rows):
         value = tokens_ref[rows, :].astype(F32) + dot(mixed1_ref[rows, :], weights_ref[3])
@@ -530,18 +555,27 @@
         normed = (value * rms(value) * gains_ref[1:2, :]).astype(BF16)
         q2_ref[rows, :] = dot(normed, weights_ref[4]).astype(BF16)
 
-    row_blocks(length, 256, project_cross)
-    advance(("feed", 3))
+    row_blocks(length, 512, project_cross)
 
     @pl.loop(0, heads)
     def _(head):
         cross_forward_head(head, q2_ref, k2_ref, v2_ref, mixed2_ref, lse2_ref)
 
+        @pl.when(head == heads // 4)
+        def _():
+            advance(("down", 2))
+
+        @pl.when(head == heads * 2 // 3)
+        def _():
+            advance(("gate", 3))
+
+    advance(("down", 3))
+
     def project_second(rows):
         second_ref[rows, :] = first_ref[rows, :] + dot(mixed2_ref[rows, :], weights_ref[7])
 
-    row_blocks(length, 256, project_second)
-    advance(("feed", 4))
+    row_blocks(length, 512, project_second)
+    advance(("gate", 4), ("down", 4))
 
 
 def norm_back_rows(value, gain, grad):
@@ -596,7 +630,7 @@
         gup_ref[rows, :] = gup
         back_ref[rows, :] += dot(ggate, gate_ref[...], 1, 1) + dot(gup, up_ref[...], 1, 1)
 
-    row_blocks(length, block, rows_step)
+    row_blocks(length, 512, rows_step)
     ddown_ref[...] = dot(hidden_ref[...].T, gout_ref[...]).astype(BF16)
     dgate_ref[...] = dot(flipped_ref[...], ggate_ref[...]).astype(BF16)
     dup_ref[...] = dot(flipped_ref[...], gup_ref[...]).astype(BF16)
@@ -704,9 +738,10 @@
     if plan:
         sizes, pieces = plan
         scatter = Scatter(Place(sizes), pieces, sources, [False] * count, outs, refs[:-3], *refs[-3:])
-        everything = range(len(pieces))
+        soon, later = range(len(pieces) // 2), range(len(pieces) // 2, len(pieces))
         scatter.place.meet()
-        scatter.advance(everything, 0)
+        scatter.advance(soon, 0)
+        scatter.advance(later, 0)
     length, width = first_ref.shape
     source = memory_ref.shape[0]
     block = 256
@@ -717,12 +752,14 @@
         gm_ref[rows, :] = dot(branch, co_ref[...], 1, 1).astype(BF16)
         flipped_ref[:, rows] = mixed2_ref[rows, :].T
 
-    row_blocks(length, block, prepare)
+    row_blocks(length, 512, prepare)
 
     def out_grad(rows):
         dco_ref[rows, :] = dot(flipped_ref[rows, :], branch_ref[...]).astype(BF16)
 
-    row_blocks(width, block, out_grad)
+    row_blocks(width, 384, out_grad)
+    if plan:
+        scatter.advance(soon, 1)
     lse_rows_ref[...] = lse_ref[...].T
     gk_ref[...] = jnp.zeros_like(gk_ref)
     gv_ref[...] = jnp.zeros_like(gv_ref)
@@ -731,11 +768,15 @@
     @pl.loop(0, groups)
     def _(group):
         if plan:
-            for when, phase in ((1, 1), (groups - 2, 2), (groups - 1, 3)):
-
-                @pl.when(group == when)
-                def _(phase=phase):
-                    scatter.advance(everything, phase)
+
+            @pl.when(group == groups // 3)
+            def _():
+                scatter.advance(soon, 2)
+                scatter.advance(later, 1)
+
+            @pl.when(group == groups - 2)
+            def _():
+                scatter.advance(soon, 3)
 
         cols = pl.ds(pl.multiple_of(group * PAIR, PAIR), PAIR)
         backward_head_prepare(cols, gm_ref, mixed2_ref, delta_ref)
@@ -752,18 +793,24 @@
 
         gq_ref[:, cols] = gqt_ref[...].T.astype(BF16)
 
+    if plan:
+        scatter.advance(later, 2)
+
     def memory_grad(rows):
         gmem_ref[rows, :] = dot(gk_ref[rows, :], ck_ref[...], 1, 1) + dot(gv_ref[rows, :], cv_ref[...], 1, 1)
         flipped_ref[:, rows] = memory_ref[rows, :].T
 
-    row_blocks(source, block, memory_grad)
+    row_blocks(source, 512, memory_grad)
 
     def memory_weights(rows):
         flipped = flipped_ref[rows, :source]
         dck_ref[rows, :] = dot(flipped, gk_ref[...]).astype(BF16)
         dcv_ref[rows, :] = dot(flipped, gv_ref[...]).astype(BF16)
 
-    row_blocks(width, block, memory_weights)
+    row_blocks(width, 384, memory_weights)
+    if plan:
+        scatter.advance(later, 3)
+        scatter.advance(soon, 4)
     ggain_ref[...] = jnp.zeros_like(ggain_ref)
 
     def first_grad(rows):
@@ -777,12 +824,12 @@
         branch_ref[rows, :] = branch
         gm1_ref[rows, :] = dot(branch, wo_ref[...], 1, 1).astype(BF16)
 
-    row_blocks(length, block, first_grad)
+    row_blocks(length, 512, first_grad)
 
     def query_weights(rows):
         dcq_ref[rows, :] = dot(flipped_ref[rows, :], gq_ref[...]).astype(BF16)
 
-    row_blocks(width, block, query_weights)
+    row_blocks(width, 384, query_weights)
 
     def flip_mixed(rows):
         flipped_ref[:, rows] = mixed1_ref[rows, :].T
@@ -792,9 +839,9 @@
     def out_weights(rows):
         dwo_ref[rows, :] = dot(flipped_ref[rows, :], branch_ref[...]).astype(BF16)
 
-    row_blocks(width, block, out_weights)
+    row_blocks(width, 384, out_weights)
     if plan:
-        scatter.advance(everything, 4)
+        scatter.advance(later, 4)
 
 
 def store_shares(ref, cols, value, start):
@@ -944,16 +991,14 @@
             @pl.when(group == groups - 1)
             def _():
                 scatter.advance(rest, 2)
-                scatter.advance(early, 2)
 
         group_step(group)
 
     if plan:
-        scatter.advance(first, 4)
+        weights(high)
+        scatter.advance(late[:3], 0)
+        scatter.advance(early, 2)
         scatter.advance(rest, 3)
-        weights(high)
-        scatter.advance(early, 3)
-        scatter.advance(late[:3], 0)
     else:
         weights(low)
         weights(high)
@@ -972,15 +1017,17 @@
 
     if plan:
         scatter.advance(late[:3], 1)
-        row_blocks(length, block, tokens_grad)
+        steps = (first, 4), (early, 3), (late[:3], 2), (rest, 4)
+        for number, step in enumerate(steps):
+            for start in range(number * length // 4, (number + 1) * length // 4, block):
+                tokens_grad(pl.ds(start, block))
+            scatter.advance(*step)
         fill_tiles(tiles_ref, gtable, [ggain_ref[0:1, :], ggain2_ref[0:1, :], ggain3_ref[0:1, :]])
         scatter.advance(late[3:], 0)
-        scatter.advance(late[:3], 2)
+        scatter.advance(late[:3], 3)
         scatter.advance(late[3:], 1)
-        scatter.advance(rest, 4)
-        scatter.advance(late[:3], 3)
+        scatter.advance(early, 4)
         scatter.advance(late[3:], 2)
-        scatter.advance(early, 4)
         scatter.advance(late[3:], 3)
         scatter.advance(late, 4)
         tile = tile_ref[...]
@@ -991,6 +1038,33 @@
     else:
         row_blocks(length, block, tokens_grad)
         gtable_ref[...] = gtable.T
+
+
+def hand_on_kernel(*refs):
+    count = (len(refs) - 2) // 3
+    ins, outs, held, (in_sem, out_sem) = refs[:count], refs[count : 2 * count], refs[2 * count : 3 * count], refs[3 * count :]
+    loads = [pltpu.make_async_copy(ins[i], held[i], in_sem.at[i]) for i in range(count)]
+    stores = [pltpu.make_async_copy(held[i], outs[i], out_sem.at[i]) for i in range(count)]
+    for load in loads:
+        load.start()
+    for load, store in zip(loads, stores):
+        load.wait()
+        store.start()
+    for store in stores:
+        store.wait()
+
+
+def hand_on(arrays):
+    spec = pl.BlockSpec(memory_space=pl.ANY)
+    return pl.pallas_call(
+        hand_on_kernel,
+        out_shape=[jax.ShapeDtypeStruct(a.shape, a.dtype) for a in arrays],
+        in_specs=[spec] * len(arrays),
+        out_specs=[spec] * len(arrays),
+        scratch_shapes=[pltpu.VMEM(a.shape, a.dtype) for a in arrays] + [pltpu.SemaphoreType.DMA((len(arrays),))] * 2,
+        compiler_params=params(),
+        name="hand_on",
+    )(*arrays)
 
 
 def vmem(*shapes):
@@ -1058,7 +1132,8 @@
         functools.partial(forward_kernel, band=band, heads=heads, plan=plan),
         out_shape=gathered_shapes + outs,
         grid=(1,),
-        in_specs=[scalar] + [full(a.shape) for a in forward_in] + [remote] * len(shards),
+        in_specs=[scalar] + [full(a.shape) for a in forward_in]
+        + ([full(a.shape) for a in shards] if own else [remote] * len(shards)),
         out_specs=[remote] * len(gathered_shapes) + [full(o.shape) for o in outs],
         scratch_shapes=vmem(
             ((heads, band.width), F32), ((SUB, band.causal), F32), ((SUB, band.two_way), F32),
@@ -1077,7 +1152,7 @@
         down = gathered[10].reshape(ff, width)
     gains, q1, k1, v1, mixed1, lse1, first, q2, k2, v2, mixed2, lse2, second = results
 
-    fblock = 256
+    fblock = min(1024, ff)
     ggain_shape = like((8, width), F32)
     feed_out = [
         act, act32, ggain_shape, like((width, ff), BF16), like((width, ff), BF16), like((ff, width), BF16)
@@ -1128,7 +1203,8 @@
     plan, sources, gate_shapes, scratch = None, [], [], []
     if own:
         sources = shares([dgate, dup])
-        pieces = [(0, 0, ff, "xy"), (1, 0, ff, "yx")]
+        half = ff // 2
+        pieces = [(0, 0, half, "xy"), (1, 0, half, "yx"), (0, half, half, "xy"), (1, half, half, "yx")]
         plan = (sizes, pieces)
         gate_shapes = [like(part.shape[-2:], F32) for part in sources]
         scratch = scatter_scratch(pieces, [(part.shape[-2], BF16) for part in sources], [False, False])
@@ -1178,9 +1254,9 @@
     )(prefix, *self_in, *attention[:3], *sources)
 
     if own:
+        gtokens, gmem, dgate, dup, *grads = hand_on([gtokens, gmem, *feed_grads, *grads])
         ddown, dco, dwo, dcq, dck, dcv, dwq, dwk, dwv, table_grad, *ggains = grads
         ggains = [ggain.reshape(-1) for ggain in ggains]
-        dgate, dup = feed_grads
     else:
         ggain_self, gtable, dwq, dwk, dwv = grads
         table_grad = lax.psum(gtable, AXES)

time: 371 us -> 329 us (0.89); the launches traced: 370 us -> 324 us
  Pallas kernels: 353 us -> 320 us
  local copies, waits for them, and re-layouts: 16.5 us -> 2.76 us
    pallas_call x1, Pallas kernels: 62.4 us -> 45.3 us  [per_device(): pl.pallas_call(feed_kernel, out_shape=feed_out, grid=(ff // fblock,), in_...]
    unnamed x48 -> x2, local copies, waits for them, and re-layouts: 16.5 us -> 2.76 us
    pallas_call x1, Pallas kernels: 63.9 us -> 55.9 us  [per_device(): pl.pallas_call(functools.partial(cross_backward_kernel, heads=heads, plan...]
    pallas_call x1, Pallas kernels: 132 us -> 124 us  [per_device(): pl.pallas_call(functools.partial(forward_kernel, band=band, heads=heads,...]
    pallas_call x0 -> x1, Pallas kernels: none -> 4.75 us  [hand_on(): pl.pallas_call(hand_on_kernel, out_shape=[jax.ShapeDtypeStruct(a.shape, a...]
    pallas_call x1, Pallas kernels: 94.3 us -> 89.7 us  [per_device(): pl.pallas_call(functools.partial(self_backward_kernel, band=band, heads=h...]
where the time goes in v4:
time: 329 us; the launch traced here: 324 us
  Pallas kernels  320 us (97%)
    pallas_call x1, Pallas kernels, per_device(): pl.pallas_call(functools.partial(forward_kernel, band=band, heads=heads,...  124 us
    pallas_call x1, Pallas kernels, per_device(): pl.pallas_call(functools.partial(self_backward_kernel, band=band, heads=h...  89.7 us
    pallas_call x1, Pallas kernels, per_device(): pl.pallas_call(functools.partial(cross_backward_kernel, heads=heads, plan...  55.9 us
    pallas_call x1, Pallas kernels, per_device(): pl.pallas_call(feed_kernel, out_shape=feed_out, grid=(ff // fblock,), in_...  45.3 us

profile of v4, /device:TPU:0, one launch (start us, length us, event | category | flops | bytes accessed | tf_op | source)
XLA Modules:
  0.0 324.1 jit_solution(15351115804756724917)
XLA Ops:
  1.3 1.4 copy.38.table_ref
  2.7 124.2 %forward.1 = (bf16[4,2,2,48,768]{4,3,2,1,0:T(8,128)(2,1)}, bf16[4,2,2,48,768]{4,3,2,1,0:T(8,128)(2,1)}, bf16[4,2,2,48,768]{4,3,2,1,0:T(8,128)(2,1)}, bf16[4,2,2,...) custom-call(s32[1]{0:T(128)S(6)} %copy.41.limit_ref, ...), custom_call_target="tpu_custom_call" | custom-call | tf_op jit(solution)/shard_map/forward/pallas_call | solution.py:1131
  126.9 45.3 %feed.1 = (bf16[1024,768]{1,0:T(8,128)(2,1)}, f32[1024,768]{1,0:T(8,128)}, f32[8,768]{1,0:T(8,128)}, bf16[768,2048]{1,0:T(8,128)(2,1)}, bf16[768,2048]{1,0:T(8,128)(2,1)}, /*index=5*/bf16[2048,768]{1,0:T(8,128)(2,1)}) custom-call(f32[1024,768]{1,0:T(8,128)} %get-tuple-element.90.second_ref, bf16[1024,768]{1,0:T(8,128)(2,1)} %bitcast.41, ...), custom_call_target="tpu_custom_call" | custom-call | tf_op jit(solution)/shard_map/feed/pallas_call | solution.py:1160
  172.2 55.9 %cross_backward.1 = (f32[512,768]{1,0:T(8,128)}, f32[1024,768]{1,0:T(8,128)}, bf16[1024,768]{1,0:T(8,128)(2,1)}, f32[8,768]{1,0:T(8,128)}, bf16[768,768]{1,0:T(8...) custom-call(f32[1024,768]{1,0:T(8,128)} %get-tuple-element.101.gseco, ...), custom_call_target="tpu_custom_call" | custom-call | tf_op jit(solution)/shard_map/cross_backward/pallas_call | solution.py:1212
  228.1 89.7 %self_backward.1 = (f32[1024,768]{1,0:T(8,128)}, f32[64,768]{1,0:T(8,128)}, f32[24,768]{1,0:T(8,128)}, f32[24,768]{1,0:T(8,128)}, f32[24,768]{1,0:T(8,128)}, /*i...) custom-call(s32[1]{0:T(128)S(6)} %copy.41.limit_ref, ...), custom_call_target="tpu_custom_call" | custom-call | tf_op jit(solution)/shard_map/self_backward/pallas_call | solution.py:1245
  317.8 4.7 %hand_on.1 = (f32[1024,768]{1,0:T(8,128)}, f32[512,768]{1,0:T(8,128)}, f32[24,2048]{1,0:T(8,128)}, f32[24,2048]{1,0:T(8,128)}, f32[64,768]{1,0:T(8,128)}, /*inde...) custom-call(f32[1024,768]{1,0:T(8,128)} %get-tuple-element.128.refs_, ...), custom_call_target="tpu_custom_call" | custom-call | tf_op jit(solution)/shard_map/hand_on/pallas_call | solution.py:1059
  322.5 1.4 copy.40

commit v5 on v4

--- a/solution.py
+++ b/solution.py
@@ -64,17 +64,56 @@
         size = self.size(axis)
         return [lax.rem(self.at[axis] + step, size) for step in range(1, size)]
 
+    def greet(self):
+        barrier = pltpu.get_barrier_semaphore()
+        for peer in self.peers():
+            pl.semaphore_signal(barrier, inc=1, device_id=peer, device_id_type=MESH)
+
     def meet(self):
-        barrier = pltpu.get_barrier_semaphore()
-        peers = [self.device(**{axis: other}) for axis in "zyxc" for other in self.others(axis)]
-        for peer in peers:
-            pl.semaphore_signal(barrier, inc=1, device_id=peer, device_id_type=MESH)
-        pl.semaphore_wait(barrier, len(peers))
+        pl.semaphore_wait(pltpu.get_barrier_semaphore(), len(self.peers()))
+
+    def peers(self):
+        return [self.device(**{axis: other}) for axis in "zyxc" for other in self.others(axis)]
 
 
 def grid_of(sizes):
     wide = sizes["fsdp"] // 2
     return (sizes["dp"] // wide, wide, wide, 2)
+
+
+class Moves:
+    def __init__(self, ins, outs, refs):
+        count = len(ins) + len(outs)
+        self.ins, self.outs = ins, outs
+        self.held, self.sem, self.rest = refs[:count], refs[count], refs[count + 1 :]
+        self.held_ins, self.held_outs = self.held[: len(ins)], self.held[len(ins) :]
+        self.stored = []
+
+    @staticmethod
+    def scratch(arrays):
+        return [pltpu.VMEM(a.shape, a.dtype) for a in arrays] + [pltpu.SemaphoreType.DMA((len(arrays),))]
+
+    def copy(self, number):
+        if number < len(self.ins):
+            return pltpu.make_async_copy(self.ins[number], self.held[number], self.sem.at[number])
+        return pltpu.make_async_copy(self.held[number], self.outs[number - len(self.ins)], self.sem.at[number])
+
+    def load(self, *numbers):
+        for number in numbers:
+            self.copy(number).start()
+
+    def need(self, *numbers):
+        for number in numbers:
+            self.copy(number).wait()
+
+    def store(self, *numbers):
+        for number in numbers:
+            self.copy(len(self.ins) + number).start()
+            self.stored.append(len(self.ins) + number)
+
+    def finish(self):
+        for number in self.stored:
+            self.copy(number).wait()
 
 
 class Gather:
@@ -95,7 +134,7 @@
 
     def view(self, piece, held):
         array, first, rows, order = piece
-        start = self.place.at["c"] * self.shards[array].shape[0] + first
+        start = self.place.at["c"] * (self.outs[array].shape[3] // 2) + first
         where = [held.get(axis, EVERY) for axis in "zyx"]
         return self.outs[array].at[(*where, pl.ds(pl.multiple_of(start, 8), rows), EVERY)]
 
@@ -154,6 +193,16 @@
             for copy in waits:
                 copy.wait()
             for copy in starts:
+                copy.start()
+
+    def settle(self, numbers):
+        for number in numbers:
+            for copy in self.phase(number, 0, False):
+                copy.wait()
+
+    def resume(self, numbers):
+        for number in numbers:
+            for copy in self.phase(number, 1, False):
                 copy.start()
 
 
@@ -430,19 +479,20 @@
 
 
 ATTENTION = 8
-SHARDS = 12
+SHARDS = 14
 
 
 def gather_pieces(rows, down_rows):
     head, tail = rows // 3 // 8 * 8, rows - rows // 3 // 8 * 8
     half = down_rows // 2
     table = {
-        "qk": [(0, 0, rows, "zxy"), (1, 0, rows, "zyx"), (11, 0, 8, "zxy")],
+        "qk": [(0, 0, rows, "zxy"), (1, 0, rows, "zyx"), (13, 0, 8, "zxy")],
         "v": [(2, 0, head, "xzy"), (2, head, tail, "yzx")],
         "out": [(3, 0, rows, "zxy"), (4, 0, rows, "zyx"), (7, 0, tail, "zxy"), (7, tail, head, "zyx")],
         "memory": [(5, 0, rows, "xzy"), (6, 0, rows, "yzx")],
         "gate": [(8, 0, rows, "zxy"), (9, 0, rows, "zyx")],
         "down": [(10, 0, half, "xzy"), (10, half, half, "yzx")],
+        "upper": [(11, 0, rows, "zxy"), (12, 0, rows, "zyx")],
     }
     pieces, groups = [], {}
     for name, group in table.items():
@@ -451,25 +501,32 @@
     return pieces, groups
 
 
+FORWARD_OUTS = 13
+
+
 def forward_kernel(
     limit_ref, tokens_ref, memory_ref, table_ref, map_ref, gain1_ref, gain2_ref, gain3_ref, *refs, band, heads, plan,
 ):
-    count = SHARDS - 1 if plan else ATTENTION
+    count = ATTENTION + 3 if plan else ATTENTION
     shards, refs = refs[:count], refs[count:]
     if plan:
         gathered, refs = refs[:SHARDS], refs[SHARDS:]
     else:
         gathered = shards
+    moves = Moves((), refs[:FORWARD_OUTS], refs[FORWARD_OUTS:])
     (
         gains_ref, q1_ref, k1_ref, v1_ref, mixed1_ref, lse1_ref, first_ref,
         q2_ref, k2_ref, v2_ref, mixed2_ref, lse2_ref, second_ref,
-        bias_ref, causal_ref, two_ref, weights_ref, share_ref, tile_ref, load_sem, *gather_sems,
-    ) = refs
+    ) = moves.held_outs
+    bias_ref, causal_ref, two_ref, weights_ref, share_ref, tile_ref, load_sem, *gather_sems = moves.rest
     length, width = tokens_ref.shape
     if plan:
         sizes, pieces, groups = plan
         place = Place(sizes)
-        gather = Gather(place, pieces, (*shards, share_ref), gathered, *gather_sems)
+        columns = gathered[8].shape[-1]
+        halves = [[ref.at[:, start : start + columns] for ref in shards[8:10]] for start in (0, columns)]
+        parts = (*shards[:8], *halves[0], shards[10], *halves[1], share_ref)
+        gather = Gather(place, pieces, parts, gathered, *gather_sems)
 
     def advance(*steps):
         if plan:
@@ -487,15 +544,17 @@
         share_ref[...] = jnp.zeros_like(share_ref)
         for number, gain_ref in enumerate(gain_refs):
             share_ref[number : number + 1, : gain_ref.shape[1]] = gain_ref[...].astype(F32)
-        place.meet()
-    advance(("qk", 0), ("v", 0), ("memory", 0))
+        place.greet()
     bias_ref[...] = bias_rows(table_ref, map_ref, band, "queries")
     lse1_ref[...] = jnp.zeros_like(lse1_ref)
     lse2_ref[...] = jnp.zeros_like(lse2_ref)
     mixed1_ref[...] = jnp.zeros_like(mixed1_ref)
     mixed2_ref[...] = jnp.zeros_like(mixed2_ref)
-    advance(("v", 1), ("out", 0), ("memory", 1), ("qk", 1), ("gate", 0), ("down", 0), ("qk", 2), ("v", 2))
-    advance(("qk", 3), ("v", 3), ("out", 1), ("qk", 4), ("v", 4))
+    if plan:
+        place.meet()
+    advance(("qk", 0), ("v", 0), ("memory", 0))
+    advance(("v", 1), ("qk", 1), ("qk", 2), ("v", 2), ("out", 0))
+    advance(("qk", 3), ("v", 3), ("qk", 4), ("v", 4), ("memory", 1), ("out", 1), ("gate", 0), ("down", 0), ("upper", 0))
     for number in range(3):
         load(number).start()
     if plan:
@@ -520,6 +579,7 @@
         project_self(pl.ds(start, length // 2))
         if start == 0:
             advance(("out", 2))
+    moves.store(0, 1, 2, 3)
 
     @pl.loop(0, heads)
     def _(head):
@@ -540,6 +600,7 @@
                     load(number).start()
 
     advance(("gate", 2))
+    moves.store(4, 5)
     for number in range(3, ATTENTION):
         load(number).wait()
 
@@ -556,6 +617,7 @@
         q2_ref[rows, :] = dot(normed, weights_ref[4]).astype(BF16)
 
     row_blocks(length, 512, project_cross)
+    moves.store(6, 7, 8, 9)
 
     @pl.loop(0, heads)
     def _(head):
@@ -570,29 +632,55 @@
             advance(("gate", 3))
 
     advance(("down", 3))
+    moves.store(10, 11)
 
     def project_second(rows):
         second_ref[rows, :] = first_ref[rows, :] + dot(mixed2_ref[rows, :], weights_ref[7])
 
     row_blocks(length, 512, project_second)
+    moves.store(12)
     advance(("gate", 4), ("down", 4))
+    if plan:
+        gather.settle(groups["upper"])
+    moves.finish()
 
 
 def norm_back_rows(value, gain, grad):
     scale = rms(value)
     unit = value * scale
     scaled = grad * gain
-    back = scale * (scaled - unit * jnp.mean(scaled * unit, axis=-1, keepdims=True))
-    return back, jnp.sum(grad * unit, axis=0, keepdims=True)
+    return scale * (scaled - unit * jnp.mean(scaled * unit, axis=-1, keepdims=True))
 
 
 GELU_A = 0.7978845608028654
 GELU_B = 0.044715
 
 
+def feed_rows(
+    rows, gate_ref, up_ref, down_ref, gout_ref, normed_ref, out_ref, back_ref, hidden_ref, ggate_ref, gup_ref
+):
+    normed = normed_ref[rows, :]
+    gate = dot(normed, gate_ref[...])
+    upward = dot(normed, up_ref[...])
+    square = gate * gate
+    bend = jnp.tanh(GELU_A * gate * (1.0 + GELU_B * square))
+    half = 0.5 * (1.0 + bend)
+    active = gate * half
+    hidden = (active * upward).astype(BF16)
+    hidden_ref[rows, :] = hidden
+    out_ref[rows, :] += dot(hidden, down_ref[...])
+    ghidden = dot(gout_ref[rows, :], down_ref[...], 1, 1)
+    slope = half + 0.5 * gate * (1.0 - bend * bend) * (GELU_A * (1.0 + 3.0 * GELU_B * square))
+    ggate = (ghidden * upward * slope).astype(BF16)
+    gup = (ghidden * active).astype(BF16)
+    ggate_ref[rows, :] = ggate
+    gup_ref[rows, :] = gup
+    back_ref[rows, :] += dot(ggate, gate_ref[...], 1, 1) + dot(gup, up_ref[...], 1, 1)
+
+
 def feed_kernel(
     second_ref, gout_ref, gains_ref, gate_ref, up_ref, down_ref,
-    output_ref, gsecond_ref, ggain_ref, dgate_ref, dup_ref, ddown_ref,
+    output_ref, gsecond_ref, dgate_ref, dup_ref, ddown_ref,
     normed_ref, flipped_ref, out_ref, back_ref, hidden_ref, ggate_ref, gup_ref,
 ):
     step = pl.program_id(0)
@@ -612,23 +700,9 @@
         row_blocks(length, block, prepare)
 
     def rows_step(rows):
-        normed = normed_ref[rows, :]
-        gate = dot(normed, gate_ref[...])
-        upward = dot(normed, up_ref[...])
-        square = gate * gate
-        bend = jnp.tanh(GELU_A * gate * (1.0 + GELU_B * square))
-        half = 0.5 * (1.0 + bend)
-        active = gate * half
-        hidden = (active * upward).astype(BF16)
-        hidden_ref[rows, :] = hidden
-        out_ref[rows, :] += dot(hidden, down_ref[...])
-        ghidden = dot(gout_ref[rows, :], down_ref[...], 1, 1)
-        slope = half + 0.5 * gate * (1.0 - bend * bend) * (GELU_A * (1.0 + 3.0 * GELU_B * square))
-        ggate = (ghidden * upward * slope).astype(BF16)
-        gup = (ghidden * active).astype(BF16)
-        ggate_ref[rows, :] = ggate
-        gup_ref[rows, :] = gup
-        back_ref[rows, :] += dot(ggate, gate_ref[...], 1, 1) + dot(gup, up_ref[...], 1, 1)
+        feed_rows(
+            rows, gate_ref, up_ref, down_ref, gout_ref, normed_ref, out_ref, back_ref, hidden_ref, ggate_ref, gup_ref
+        )
 
     row_blocks(length, 512, rows_step)
     ddown_ref[...] = dot(hidden_ref[...].T, gout_ref[...]).astype(BF16)
@@ -637,15 +711,131 @@
 
     @pl.when(step == pl.num_programs(0) - 1)
     def _():
-        ggain_ref[...] = jnp.zeros_like(ggain_ref)
-
         def finish(rows):
             output_ref[rows, :] = out_ref[rows, :].astype(BF16)
-            back, ggain = norm_back_rows(second_ref[rows, :], gains_ref[2:3, :], back_ref[rows, :])
+            back = norm_back_rows(second_ref[rows, :], gains_ref[2:3, :], back_ref[rows, :])
             gsecond_ref[rows, :] = back + gout_ref[rows, :].astype(F32)
-            ggain_ref[0:1, :] += ggain
 
         row_blocks(length, block, finish)
+
+
+FEED_INS, FEED_OUTS = 6, 3
+
+
+def feed_exchange_kernel(*refs, plan):
+    ins, refs = refs[:FEED_INS], refs[FEED_INS + 2 :]
+    results, refs = refs[:FEED_OUTS], refs[FEED_OUTS:]
+    shares, outs, gathered, refs = refs[:2], refs[2:4], refs[4:6], refs[6:]
+    moves = Moves(ins, results, refs)
+    second_ref, gout_ref, gains_ref, gate_low_ref, up_low_ref, down_ref = moves.held_ins
+    output_ref, gsecond_ref, ddown_ref = moves.held_outs
+    (
+        normed_ref, flipped_ref, out_ref, back_ref, hidden_ref, ggate_ref, gup_ref, gate_ref, up_ref,
+        dgate_ref, dup_ref, load_sem, share_sem, *refs,
+    ) = moves.rest
+    sizes, gather_plan, scatter_plan = plan
+    place = Place(sizes)
+    gather = Gather(place, gather_plan, (), gathered, *refs[:3])
+    lower = [dgate_ref.at[0], dup_ref.at[0]]
+    scatter = Scatter(place, scatter_plan, lower, [True, True], outs, refs[3:-3], *refs[-3:])
+    upper, every = range(len(gather_plan)), range(len(scatter_plan))
+    length, width = second_ref.shape
+    columns = gate_low_ref.shape[1]
+    block = 256
+
+    def load(number):
+        target = (gate_ref, up_ref)[number].at[1]
+        return pltpu.make_async_copy(gathered[number].reshape(width, columns), target, load_sem.at[number])
+
+    def low(number):
+        target = (gate_ref, up_ref)[number].at[0]
+        return pltpu.make_async_copy((ins[3], ins[4])[number], target, load_sem.at[2 + number])
+
+    place.greet()
+    moves.load(0, 2, 1)
+    for number in (0, 1):
+        low(number).start()
+    moves.load(5)
+    place.meet()
+    gather.resume(upper)
+    moves.need(0, 2)
+
+    def prepare(rows):
+        value = second_ref[rows, :]
+        normed = (value * rms(value) * gains_ref[2:3, :]).astype(BF16)
+        normed_ref[rows, :] = normed
+        flipped_ref[:, rows] = normed.T
+        out_ref[rows, :] = value
+        back_ref[rows, :] = jnp.zeros_like(value)
+
+    row_blocks(length, block, prepare)
+    moves.need(1, 5)
+    for number in (0, 1):
+        low(number).wait()
+
+    @pl.loop(0, 2)
+    def _(half):
+        units = pl.ds(pl.multiple_of(half * columns, columns), columns)
+        gate, up, down = gate_ref.at[half], up_ref.at[half], down_ref.at[units]
+
+        @pl.loop(0, 2)
+        def _(index):
+            rows = pl.ds(pl.multiple_of(index * (length // 2), length // 2), length // 2)
+            feed_rows(rows, gate, up, down, gout_ref, normed_ref, out_ref, back_ref, hidden_ref, ggate_ref, gup_ref)
+
+            @pl.when((half == 0) & (index == 0))
+            def _():
+                gather.advance(upper, 2)
+
+            @pl.when((half == 1) & (index == 0))
+            def _():
+                scatter.advance(every, 2)
+
+            @pl.when((half == 1) & (index == 1))
+            def _():
+                scatter.advance(every, 3)
+
+        rows_each = width // place.sizes[0]
+
+        @pl.loop(0, place.sizes[0])
+        def _(index):
+            start = pl.multiple_of(index * rows_each, 64)
+            flipped = flipped_ref[pl.ds(start, rows_each), :]
+            for target, grad in ((dgate_ref, ggate_ref), (dup_ref, gup_ref)):
+                store_shares(target.at[half], EVERY, dot(flipped, grad[...]), start)
+
+        @pl.when(half == 0)
+        def _():
+            scatter.advance(every, 0)
+            gather.advance(upper, 3)
+
+        ddown_ref[units, :] = dot(hidden_ref[...].T, gout_ref[...]).astype(BF16)
+
+        @pl.when(half == 0)
+        def _():
+            gather.advance(upper, 4)
+            for number in upper:
+                load(number).start()
+            scatter.advance(every, 1)
+            for number in upper:
+                load(number).wait()
+
+    share = [pltpu.make_async_copy(ref.at[1], shares[i], share_sem.at[i]) for i, ref in enumerate((dgate_ref, dup_ref))]
+    for copy in share:
+        copy.start()
+    moves.store(2)
+
+    def finish(rows):
+        output_ref[rows, :] = out_ref[rows, :].astype(BF16)
+        back = norm_back_rows(second_ref[rows, :], gains_ref[2:3, :], back_ref[rows, :])
+        gsecond_ref[rows, :] = back + gout_ref[rows, :].astype(F32)
+
+    row_blocks(length, block, finish)
+    moves.store(0, 1)
+    scatter.advance(every, 4)
+    for copy in share:
+        copy.wait()
+    moves.finish()
 
 
 def backward_head_prepare(group_cols, gm_ref, mixed_ref, delta_ref):
@@ -726,19 +916,29 @@
     return [(number, 0, half, "xy"), (number, half, half, "yx")]
 
 
-def cross_backward_kernel(
-    gsecond_ref, first_ref, memory_ref, gains_ref, q_ref, k_ref, v_ref, mixed1_ref, mixed2_ref, lse_ref,
-    wo_ref, cq_ref, ck_ref, cv_ref, co_ref, *refs, heads, plan,
-):
-    count = 2 if plan else 0
+CROSS_INS, CROSS_OUTS = 15, 8
+
+
+def cross_backward_kernel(*refs, heads, plan):
+    count = 3 if plan else 0
+    ins, refs = refs[:CROSS_INS], refs[CROSS_INS:]
     sources, refs = refs[:count], refs[count:]
-    gmem_ref, gfirst_ref, gm1_ref, ggain_ref, dwo_ref, dcq_ref, dck_ref, dcv_ref, dco_ref, *refs = refs
+    results, refs = refs[:CROSS_OUTS], refs[CROSS_OUTS:]
     outs, refs = refs[:count], refs[count:]
-    gm_ref, branch_ref, flipped_ref, lse_rows_ref, delta_ref, gq_ref, gk_ref, gv_ref, gqt_ref, *refs = refs
+    moves = Moves(ins, results, refs)
+    (
+        gsecond_ref, first_ref, memory_ref, gains_ref, q_ref, k_ref, v_ref, mixed1_ref, mixed2_ref, lse_ref,
+        wo_ref, cq_ref, ck_ref, cv_ref, co_ref,
+    ) = moves.held_ins
+    gmem_ref, gfirst_ref, gm1_ref, dwo_ref, dcq_ref, dck_ref, dcv_ref, dco_ref = moves.held_outs
+    gm_ref, branch_ref, flipped_ref, lse_rows_ref, delta_ref, gq_ref, gk_ref, gv_ref, gqt_ref, *refs = moves.rest
     if plan:
         sizes, pieces = plan
         scatter = Scatter(Place(sizes), pieces, sources, [False] * count, outs, refs[:-3], *refs[-3:])
         soon, later = range(len(pieces) // 2), range(len(pieces) // 2, len(pieces))
+        scatter.place.greet()
+    moves.load(0, 14, 8, 4, 5, 6, 9, 2, 12, 13, 1, 3, 11, 10, 7)
+    if plan:
         scatter.place.meet()
         scatter.advance(soon, 0)
         scatter.advance(later, 0)
@@ -752,12 +952,15 @@
         gm_ref[rows, :] = dot(branch, co_ref[...], 1, 1).astype(BF16)
         flipped_ref[:, rows] = mixed2_ref[rows, :].T
 
+    moves.need(0, 14, 8)
     row_blocks(length, 512, prepare)
 
     def out_grad(rows):
         dco_ref[rows, :] = dot(flipped_ref[rows, :], branch_ref[...]).astype(BF16)
 
     row_blocks(width, 384, out_grad)
+    moves.store(7)
+    moves.need(4, 5, 6, 9)
     if plan:
         scatter.advance(soon, 1)
     lse_rows_ref[...] = lse_ref[...].T
@@ -800,7 +1003,9 @@
         gmem_ref[rows, :] = dot(gk_ref[rows, :], ck_ref[...], 1, 1) + dot(gv_ref[rows, :], cv_ref[...], 1, 1)
         flipped_ref[:, rows] = memory_ref[rows, :].T
 
+    moves.need(2, 12, 13)
     row_blocks(source, 512, memory_grad)
+    moves.store(0)
 
     def memory_weights(rows):
         flipped = flipped_ref[rows, :source]
@@ -808,16 +1013,16 @@
         dcv_ref[rows, :] = dot(flipped, gv_ref[...]).astype(BF16)
 
     row_blocks(width, 384, memory_weights)
+    moves.store(5, 6)
+    moves.need(1, 3, 11, 10, 7)
     if plan:
         scatter.advance(later, 3)
         scatter.advance(soon, 4)
-    ggain_ref[...] = jnp.zeros_like(ggain_ref)
 
     def first_grad(rows):
         value = first_ref[rows, :]
         flipped_ref[:, rows] = (value * rms(value) * gains_ref[1:2, :]).astype(BF16).T
-        back, ggain = norm_back_rows(value, gains_ref[1:2, :], dot(gq_ref[rows, :], cq_ref[...], 1, 1))
-        ggain_ref[0:1, :] += ggain
+        back = norm_back_rows(value, gains_ref[1:2, :], dot(gq_ref[rows, :], cq_ref[...], 1, 1))
         gfirst = back + gsecond_ref[rows, :]
         gfirst_ref[rows, :] = gfirst
         branch = gfirst.astype(BF16)
@@ -825,11 +1030,13 @@
         gm1_ref[rows, :] = dot(branch, wo_ref[...], 1, 1).astype(BF16)
 
     row_blocks(length, 512, first_grad)
+    moves.store(1, 2)
 
     def query_weights(rows):
         dcq_ref[rows, :] = dot(flipped_ref[rows, :], gq_ref[...]).astype(BF16)
 
     row_blocks(width, 384, query_weights)
+    moves.store(4)
 
     def flip_mixed(rows):
         flipped_ref[:, rows] = mixed1_ref[rows, :].T
@@ -840,8 +1047,10 @@
         dwo_ref[rows, :] = dot(flipped_ref[rows, :], branch_ref[...]).astype(BF16)
 
     row_blocks(width, 384, out_weights)
+    moves.store(3)
     if plan:
         scatter.advance(later, 4)
+    moves.finish()
 
 
 def store_shares(ref, cols, value, start):
@@ -850,62 +1059,63 @@
     else:
         deep, high, wide, cores, rows, columns = ref.shape
         chunk = high * wide * cores * rows
-        ref[start // chunk, :, :, :, :, cols] = value.reshape(high, wide, cores, rows, value.shape[1]).astype(BF16)
+        ref[lax.div(start, chunk), :, :, :, :, cols] = value.reshape(high, wide, cores, rows, value.shape[1]).astype(BF16)
 
 
 TILE = 16
 
 
-def fill_tiles(tiles_ref, gtable, ggains):
+def fill_tiles(tiles_ref, gtable):
     deep, high, wide, cores, rows, lanes = tiles_ref.shape
-    devices = deep * high * wide * cores
-    width = ggains[0].shape[1]
-    share = width // devices
-    lane = lax.broadcasted_iota(jnp.int32, (SUB, width), 1)
-    select = jnp.where(lax.rem(lane, share) == lax.broadcasted_iota(jnp.int32, (SUB, width), 0), 1.0, 0.0)
-    first = share * lax.broadcasted_iota(jnp.int32, (devices, width), 0)
-    lane = lax.broadcasted_iota(jnp.int32, (devices, width), 1)
-    own = (lane >= first) & (lane < first + share)
-    parts = [exact_dot(jnp.where(own, ggain, 0.0), select, 1, 1) for ggain in ggains]
+    heads, buckets = gtable.shape
     tiles_ref[...] = jnp.zeros_like(tiles_ref)
-    heads, buckets = gtable.shape
-    for device in range(devices):
-        at = tuple(int(part) for part in (device // (high * wide * cores), device // (wide * cores) % high, device // cores % wide, device % cores))
-        tiles_ref[(*at, slice(0, heads), slice(0, buckets))] = gtable
-        for number, part in enumerate(parts):
-            row = TILE - len(parts) + number
-            tiles_ref[(*at, slice(row, row + 1), EVERY)] = part[device : device + 1]
-
-
-REST = 6
-
-
-def self_pieces(down_columns, columns):
-    first = split_columns(0, down_columns) + [(1, 0, columns, "xy"), (2, 0, columns, "yx")]
-    rest = [(3, 0, columns, "xy"), (4, 0, columns, "yx")] + split_columns(5, columns)
-    half = columns // 2
-    early = [(REST, 0, half, "xy"), (REST + 1, 0, half, "yx"), (REST + 2, 0, half, "xy")]
-    late = [(REST, half, half, "yx"), (REST + 1, half, half, "xy"), (REST + 2, half, half, "yx"), (REST + 3, 0, SUB, "xy")]
+
+    @pl.loop(0, deep)
+    def _(z):
+        shape = (high, wide, cores, heads, buckets)
+        tiles_ref[z, :, :, :, :heads, :buckets] = jnp.broadcast_to(gtable, shape)
+
+
+REST = 5
+
+
+def self_parts(columns):
+    half, third = columns // 2, columns // 3
+    return (0, half), (half, third), (half + third, columns - half - third)
+
+
+def self_pieces(columns):
+    first = [(0, 0, columns, "xy"), (1, 0, columns, "yx")]
+    rest = [(2, 0, columns, "xy"), (3, 0, columns, "yx")] + split_columns(4, columns)
+    parts = []
+    for number, (start, count) in enumerate(self_parts(columns)):
+        orders = ("xy", "yx", "xy") if number % 2 else ("yx", "xy", "yx")
+        parts.append([(REST + array, start, count, orders[array]) for array in range(3)])
     pieces, groups = [], []
-    for group in (first, rest, early, late):
+    for group in (first, rest, *parts, [(REST + 3, 0, SUB, "xy")]):
         groups.append(range(len(pieces), len(pieces) + len(group)))
         pieces += group
     return pieces, groups
 
 
-def self_backward_kernel(
-    limit_ref, tokens_ref, gains_ref, table_ref, map_ref, q_ref, k_ref, v_ref, mixed_ref, lse_ref, gm_ref, gfirst_ref,
-    ggain2_ref, ggain3_ref, wq_ref, wk_ref, wv_ref, *refs, band, heads, plan,
-):
+SELF_INS = 12
+
+
+def self_backward_kernel(limit_ref, table_ref, map_ref, *refs, band, heads, plan):
     count = REST if plan else 0
+    ins, refs = refs[:SELF_INS], refs[SELF_INS:]
     sources, refs = refs[:count], refs[count:]
     gtokens_ref, refs = refs[0], refs[1:]
     if plan:
         outs, refs = refs[: REST + 3], refs[REST + 3 :]
-        gtable_ref, *ggain_refs = refs[:4]
-        refs = refs[4:]
+        gtable_ref, refs = refs[0], refs[1:]
     else:
-        ggain_ref, gtable_ref, dwq_ref, dwk_ref, dwv_ref, *refs = refs
+        gtable_ref, dwq_ref, dwk_ref, dwv_ref, *refs = refs
+    moves = Moves(ins, (), refs)
+    (
+        tokens_ref, gains_ref, lse_ref, q_ref, k_ref, v_ref, mixed_ref, gm_ref, gfirst_ref, wq_ref, wk_ref, wv_ref,
+    ) = moves.held_ins
+    refs = moves.rest
     (
         bias_ref, causal_ref, two_ref, flipped_ref, lse_rows_ref, delta_ref, gq_ref, gk_ref, gv_ref, gqt_ref,
         causal_sum_ref, two_sum_ref, sums_ref, *refs,
@@ -914,16 +1124,20 @@
     block = 256
     groups = heads // 2
     if plan:
-        sizes, pieces, (first, rest, early, late) = plan
-        dwq_ref, dwk_ref, dwv_ref, tiles_ref, tile_ref, ggain_ref, *refs = refs
+        sizes, pieces, (first, rest, early, middle, late, table) = plan
+        dwq_ref, dwk_ref, dwv_ref, tiles_ref, tile_ref, *refs = refs
         scatter = Scatter(
             Place(sizes), pieces, (*sources, dwq_ref, dwk_ref, dwv_ref, tiles_ref), [False] * REST + [True] * 4,
             (*outs, tile_ref), refs[:-3], *refs[-3:],
         )
+        scatter.place.greet()
+    moves.load(*range(SELF_INS))
+    bias_ref[...] = bias_rows(table_ref, map_ref, band, "keys")
+    if plan:
         scatter.place.meet()
         scatter.advance(first, 0)
         scatter.advance(rest, 0)
-    bias_ref[...] = bias_rows(table_ref, map_ref, band, "keys")
+    moves.need(0, 1, 2)
     lse_rows_ref[...] = lse_ref[...].T
     gk_ref[...] = jnp.zeros_like(gk_ref)
     gv_ref[...] = jnp.zeros_like(gv_ref)
@@ -934,6 +1148,7 @@
         flipped_ref[:, rows] = (value * rms(value) * gains_ref[0:1, :]).astype(BF16).T
 
     row_blocks(length, block, flip_normed)
+    moves.need(*range(3, SELF_INS))
 
     def group_step(group):
         cols = pl.ds(pl.multiple_of(group * PAIR, PAIR), PAIR)
@@ -943,6 +1158,13 @@
         @pl.loop(0, 2)
         def _(half):
             head = group * 2 + half
+            if plan:
+                for when, numbers, phase in ((1, first, 1), (4, rest, 1), (5, first, 2), (8, first, 3), (9, early, 1), (11, rest, 2)):
+
+                    @pl.when(head == when * heads // 12)
+                    def _(numbers=numbers, phase=phase):
+                        scatter.advance(numbers, phase)
+
             fill_bands(head, bias_ref, band, causal_ref, two_ref)
             causal_sum_ref[...] = jnp.zeros_like(causal_sum_ref)
             two_sum_ref[...] = jnp.zeros_like(two_sum_ref)
@@ -965,106 +1187,141 @@
             for target, grad in ((dwq_ref, gq_ref), (dwk_ref, gk_ref), (dwv_ref, gv_ref)):
                 store_shares(target, cols, dot(flipped, grad[:, cols]), start)
 
-    half_groups = groups // 2
-    low, high = pl.ds(0, width // 2), pl.ds(width // 2, width // 2)
+    parts = [pl.ds(start, count) for start, count in self_parts(width)]
 
     @pl.loop(0, groups)
     def _(group):
         if plan:
 
-            @pl.when(group == 1)
+            @pl.when(group == groups // 2)
             def _():
-                scatter.advance(first, 1)
-
-            @pl.when(group == half_groups)
-            def _():
-                weights(low)
+                weights(parts[0])
                 scatter.advance(early, 0)
-                scatter.advance(first, 2)
-                scatter.advance(rest, 1)
-
-            @pl.when(group == half_groups + 1)
-            def _():
-                scatter.advance(first, 3)
-                scatter.advance(early, 1)
 
             @pl.when(group == groups - 1)
             def _():
-                scatter.advance(rest, 2)
+                weights(parts[1])
+                scatter.advance(middle, 0)
 
         group_step(group)
 
     if plan:
-        weights(high)
-        scatter.advance(late[:3], 0)
+        weights(parts[2])
+        scatter.advance(late, 0)
         scatter.advance(early, 2)
         scatter.advance(rest, 3)
     else:
-        weights(low)
-        weights(high)
+        for part in parts:
+            weights(part)
     hot, unused = one_hot(map_ref, band, "keys")
     gtable = exact_dot(sums_ref[...], hot, 1, 1)
-    ggain_ref[...] = jnp.zeros_like(ggain_ref)
+    if plan:
+        fill_tiles(tiles_ref, gtable)
+        scatter.advance(table, 0)
+        scatter.advance(middle, 1)
+        scatter.advance(late, 1)
 
     def tokens_grad(rows):
         value = tokens_ref[rows, :].astype(F32)
         grad = dot(gq_ref[rows, :], wq_ref[...], 1, 1)
         grad += dot(gk_ref[rows, :], wk_ref[...], 1, 1)
         grad += dot(gv_ref[rows, :], wv_ref[...], 1, 1)
-        back, ggain = norm_back_rows(value, gains_ref[0:1, :], grad)
-        ggain_ref[0:1, :] += ggain
-        gtokens_ref[rows, :] = back + gfirst_ref[rows, :]
-
-    if plan:
-        scatter.advance(late[:3], 1)
-        steps = (first, 4), (early, 3), (late[:3], 2), (rest, 4)
-        for number, step in enumerate(steps):
-            for start in range(number * length // 4, (number + 1) * length // 4, block):
-                tokens_grad(pl.ds(start, block))
-            scatter.advance(*step)
-        fill_tiles(tiles_ref, gtable, [ggain_ref[0:1, :], ggain2_ref[0:1, :], ggain3_ref[0:1, :]])
-        scatter.advance(late[3:], 0)
-        scatter.advance(late[:3], 3)
-        scatter.advance(late[3:], 1)
+        gtokens_ref[rows, :] = norm_back_rows(value, gains_ref[0:1, :], grad) + gfirst_ref[rows, :]
+
+    if plan:
+        steps = (
+            ((table, 1), (early, 3), (first, 4)),
+            ((middle, 2), (late, 2), (table, 2)),
+            ((middle, 3), (rest, 4)),
+            ((late, 3), (table, 3)),
+        )
+
+        @pl.loop(0, len(steps))
+        def _(step):
+            for start in range(0, length // len(steps), block):
+                start = step * (length // len(steps)) + start
+                tokens_grad(pl.ds(pl.multiple_of(start, block), block))
+            for number, advances in enumerate(steps):
+
+                @pl.when(step == number)
+                def _(advances=advances):
+                    for numbers, phase in advances:
+                        scatter.advance(numbers, phase)
+
         scatter.advance(early, 4)
-        scatter.advance(late[3:], 2)
-        scatter.advance(late[3:], 3)
+        scatter.advance(middle, 4)
         scatter.advance(late, 4)
-        tile = tile_ref[...]
-        gtable_ref[...] = tile.T[:NB, :heads]
-        for number, ref in enumerate(ggain_refs):
-            row = TILE - len(ggain_refs) + number
-            ref[...] = tile[row : row + 1, : ref.shape[1]]
+        scatter.advance(table, 4)
+        gtable_ref[...] = tile_ref[...].T[:NB, :heads]
     else:
         row_blocks(length, block, tokens_grad)
         gtable_ref[...] = gtable.T
 
 
-def hand_on_kernel(*refs):
-    count = (len(refs) - 2) // 3
-    ins, outs, held, (in_sem, out_sem) = refs[:count], refs[count : 2 * count], refs[2 * count : 3 * count], refs[3 * count :]
+def gain_grads(gains, weights, grads):
+    results = []
+    for gain, parts in zip(gains, ((0, 1, 2), (3,), (4, 5))):
+        total = 0.0
+        for part in parts:
+            product = weights[part][...].astype(F32) * grads[part][...]
+            total += exact_dot(jnp.ones((8, product.shape[1]), F32), product, 1, 1)
+        results.append(total[0:1] / gain[...].astype(F32))
+    return results
+
+
+def hand_on_kernel(*refs, places, norms):
+    count = len(places)
+    shards, refs = refs[: len(norms) + 3], refs[len(norms) + 3 :]
+    ins, (in_sem, out_sem) = refs[:count], refs[-2:]
+    refs = refs[count:-2]
+    held, outs, ggain_refs = refs[-count:], refs[: -count - 3], refs[-count - 3 : -count]
     loads = [pltpu.make_async_copy(ins[i], held[i], in_sem.at[i]) for i in range(count)]
-    stores = [pltpu.make_async_copy(held[i], outs[i], out_sem.at[i]) for i in range(count)]
+    stores = []
+    for i, (out, start) in enumerate(places):
+        target = outs[out] if start is None else outs[out].at[:, start : start + ins[i].shape[1]]
+        stores.append(pltpu.make_async_copy(held[i], target, out_sem.at[i]))
     for load in loads:
         load.start()
     for load, store in zip(loads, stores):
         load.wait()
         store.start()
+    grads = []
+    for number in norms:
+        parts = [held[i][...] for i, (out, start) in enumerate(places) if out == number]
+        grads.append(jnp.concatenate(parts, axis=1))
+    for ref, value in zip(ggain_refs, gain_grads(shards[:3], shards[3:], grads)):
+        ref[...] = value
     for store in stores:
         store.wait()
 
 
-def hand_on(arrays):
+def hand_on(results, norms, gains, weights):
+    arrays, places, shapes = [], [], []
+    for number, result in enumerate(results):
+        parts = result if isinstance(result, tuple) else (result,)
+        start = 0
+        for part in parts:
+            arrays.append(part)
+            places.append((number, start if len(parts) > 1 else None))
+            start += part.shape[-1]
+        shapes.append(jax.ShapeDtypeStruct(parts[0].shape[:-1] + (start,), parts[0].dtype))
     spec = pl.BlockSpec(memory_space=pl.ANY)
-    return pl.pallas_call(
-        hand_on_kernel,
-        out_shape=[jax.ShapeDtypeStruct(a.shape, a.dtype) for a in arrays],
-        in_specs=[spec] * len(arrays),
-        out_specs=[spec] * len(arrays),
+    here = pl.BlockSpec(memory_space=pltpu.VMEM)
+    shards = [*[gain.reshape(1, -1) for gain in gains], *weights]
+    *results, first, second, third = pl.pallas_call(
+        functools.partial(hand_on_kernel, places=places, norms=norms),
+        out_shape=shapes + [jax.ShapeDtypeStruct((1, gain.shape[0]), F32) for gain in gains],
+        in_specs=[here] * len(shards) + [spec] * len(arrays),
+        out_specs=[spec] * len(shapes) + [here] * 3,
         scratch_shapes=[pltpu.VMEM(a.shape, a.dtype) for a in arrays] + [pltpu.SemaphoreType.DMA((len(arrays),))] * 2,
         compiler_params=params(),
         name="hand_on",
-    )(*arrays)
+    )(*shards, *arrays)
+    return results, [ggain.reshape(-1) for ggain in (first, second, third)]
+
+
+def upper_shapes(arrays):
+    return [jax.ShapeDtypeStruct(a.shape, a.dtype) for a in arrays]
 
 
 def vmem(*shapes):
@@ -1125,7 +1382,9 @@
     gathered_shapes = []
     if own:
         chips, cores = grid_of(sizes)[:3], grid_of(sizes)[3]
-        gathered_shapes = [like(chips + (cores * shard.shape[0], shard.shape[1]), shard.dtype) for shard in shards]
+        shapes = [shard.shape for shard in projections]
+        shapes += [(feed_gate.shape[0], ff // 2)] * 2 + [feed_down.shape] + [(feed_gate.shape[0], ff // 2)] * 2
+        gathered_shapes = [like(chips + (cores * shape[0], shape[1]), BF16) for shape in shapes]
         gathered_shapes.append(like(chips + (cores * 8, SUB), F32))
     forward_in = (tokens, memory, bias_table, bucket_map, *gains_in)
     results = pl.pallas_call(
@@ -1134,8 +1393,9 @@
         grid=(1,),
         in_specs=[scalar] + [full(a.shape) for a in forward_in]
         + ([full(a.shape) for a in shards] if own else [remote] * len(shards)),
-        out_specs=[remote] * len(gathered_shapes) + [full(o.shape) for o in outs],
-        scratch_shapes=vmem(
+        out_specs=[remote] * (len(gathered_shapes) + len(outs)),
+        scratch_shapes=Moves.scratch(outs)
+        + vmem(
             ((heads, band.width), F32), ((SUB, band.causal), F32), ((SUB, band.two_way), F32),
             ((ATTENTION, width, width), BF16), ((8, SUB), F32), ((devices, 8, SUB), F32),
         )
@@ -1148,79 +1408,110 @@
     if own:
         gathered, results = results[:SHARDS], results[SHARDS:]
         attention = [part.reshape(width, width) for part in gathered[:ATTENTION]]
-        gate_full, up_full = gathered[8].reshape(width, ff), gathered[9].reshape(width, ff)
+        gate_low, up_low = gathered[8].reshape(width, ff // 2), gathered[9].reshape(width, ff // 2)
         down = gathered[10].reshape(ff, width)
     gains, q1, k1, v1, mixed1, lse1, first, q2, k2, v2, mixed2, lse2, second = results
 
-    fblock = min(1024, ff)
-    ggain_shape = like((8, width), F32)
-    feed_out = [
-        act, act32, ggain_shape, like((width, ff), BF16), like((width, ff), BF16), like((ff, width), BF16)
-    ]
-    output, gsecond, ggain_feed, dgate, dup, ddown = pl.pallas_call(
-        feed_kernel,
-        out_shape=feed_out,
-        grid=(ff // fblock,),
-        in_specs=[full(second.shape), full(gout.shape), full(gains.shape)]
-        + [
-            pl.BlockSpec((width, fblock), lambda i: (0, i)),
-            pl.BlockSpec((width, fblock), lambda i: (0, i)),
-            pl.BlockSpec((fblock, width), lambda i: (i, 0)),
-        ],
-        out_specs=[full(o.shape) for o in feed_out[:3]]
-        + [
-            pl.BlockSpec((width, fblock), lambda i: (0, i)),
-            pl.BlockSpec((width, fblock), lambda i: (0, i)),
-            pl.BlockSpec((fblock, width), lambda i: (i, 0)),
-        ],
-        scratch_shapes=vmem(
-            ((length, width), BF16), ((width, length), BF16), ((length, width), F32), ((length, width), F32),
-            ((length, fblock), BF16), ((length, fblock), BF16), ((length, fblock), BF16),
-        ),
-        compiler_params=params(),
-        name="feed",
-    )(second, gout, gains, gate_full, up_full, down)
+    grid = grid_of(sizes)
+
+    def shares(grads):
+        return [grad.reshape(grid + (grad.shape[0] // devices, grad.shape[1])) for grad in grads]
+
+    def scatter_scratch(pieces, shapes, kept):
+        count = Scatter.copies(sizes, pieces)
+        return Scatter.scratch(sizes, pieces, shapes, kept) + [
+            pltpu.SemaphoreType.DMA((number,)) for number in (len(pieces), count, count)
+        ]
+
+    if own:
+        half = ff // 2
+        share = feed_gate.shape[0]
+        upper = gathered[11:13]
+        gather_plan = [(0, 0, share, "zxy"), (1, 0, share, "zyx")]
+        scatter_plan = [(0, 0, half, "xy"), (1, 0, half, "yx")]
+        feed_in = (second, gout, gains, gate_low, up_low, down)
+        feed_out = [act, act32, like((ff, width), BF16)]
+        share_shapes = [like(grid + (share, half), BF16)] * 2
+        grad_shapes = [like((share, half), F32)] * 2
+        copies = Gather.copies(sizes, gather_plan)
+        output, gsecond, ddown, *halves = pl.pallas_call(
+            functools.partial(feed_exchange_kernel, plan=(sizes, gather_plan, scatter_plan)),
+            out_shape=feed_out + share_shapes + grad_shapes + upper_shapes(upper),
+            grid=(1,),
+            in_specs=[remote] * (FEED_INS + 2),
+            out_specs=[remote] * (FEED_OUTS + 2) + [full(o.shape) for o in grad_shapes] + [remote] * 2,
+            scratch_shapes=Moves.scratch([*feed_in, *feed_out])
+            + vmem(
+                ((length, width), BF16), ((width, length), BF16), ((length, width), F32), ((length, width), F32),
+                ((length, half), BF16), ((length, half), BF16), ((length, half), BF16),
+                ((2, width, half), BF16), ((2, width, half), BF16),
+                ((2,) + grid + (share, half), BF16), ((2,) + grid + (share, half), BF16),
+            )
+            + [pltpu.SemaphoreType.DMA((number,)) for number in (4, 2, len(gather_plan), copies, copies)]
+            + scatter_scratch(scatter_plan, [(share, BF16)] * 2, [True, True]),
+            input_output_aliases={FEED_INS: FEED_OUTS + 4, FEED_INS + 1: FEED_OUTS + 5},
+            compiler_params=params(collective_id=3, has_side_effects=True),
+            name="feed",
+        )(*feed_in, *upper)
+        high_shares, low_grads = halves[:2], halves[2:4]
+    else:
+        fblock = min(1024, ff)
+        feed_out = [
+            act, act32, like((width, ff), BF16), like((width, ff), BF16), like((ff, width), BF16)
+        ]
+        output, gsecond, dgate, dup, ddown = pl.pallas_call(
+            feed_kernel,
+            out_shape=feed_out,
+            grid=(ff // fblock,),
+            in_specs=[full(second.shape), full(gout.shape), full(gains.shape)]
+            + [
+                pl.BlockSpec((width, fblock), lambda i: (0, i)),
+                pl.BlockSpec((width, fblock), lambda i: (0, i)),
+                pl.BlockSpec((fblock, width), lambda i: (i, 0)),
+            ],
+            out_specs=[full(o.shape) for o in feed_out[:2]]
+            + [
+                pl.BlockSpec((width, fblock), lambda i: (0, i)),
+                pl.BlockSpec((width, fblock), lambda i: (0, i)),
+                pl.BlockSpec((fblock, width), lambda i: (i, 0)),
+            ],
+            scratch_shapes=vmem(
+                ((length, width), BF16), ((width, length), BF16), ((length, width), F32), ((length, width), F32),
+                ((length, fblock), BF16), ((length, fblock), BF16), ((length, fblock), BF16),
+            ),
+            compiler_params=params(),
+            name="feed",
+        )(second, gout, gains, gate_full, up_full, down)
 
     square = like((width, width), BF16)
-    cross_shapes = [like((source, width), F32), act32, act, ggain_shape] + [square] * 5
+    cross_shapes = [like((source, width), F32), act32, act] + [square] * 5
     cross_in = (gsecond, first, memory, gains, q2, k2, v2, mixed1, mixed2, lse2)
     cross_scratch = vmem(
         ((length, width), BF16), ((length, width), BF16), ((width, length), BF16), ((SUB, length), F32),
         ((8, length), F32), ((length, width), BF16), ((source, width), BF16), ((source, width), BF16),
         ((PAIR, length), F32),
     )
-    grid = grid_of(sizes)
-
-    def shares(grads):
-        return [grad.reshape(grid + (grad.shape[0] // devices, grad.shape[1])) for grad in grads]
-
-    def scatter_scratch(pieces, shapes, kept):
-        count = Scatter.copies(sizes, pieces)
-        return Scatter.scratch(sizes, pieces, shapes, kept) + [
-            pltpu.SemaphoreType.DMA((number,)) for number in (len(pieces), count, count)
-        ]
-
     plan, sources, gate_shapes, scratch = None, [], [], []
     if own:
-        sources = shares([dgate, dup])
-        half = ff // 2
-        pieces = [(0, 0, half, "xy"), (1, 0, half, "yx"), (0, half, half, "xy"), (1, half, half, "yx")]
+        sources = high_shares + shares([ddown])
+        pieces = [(0, 0, half, "xy"), (1, 0, half, "yx")] + split_columns(2, width)
         plan = (sizes, pieces)
         gate_shapes = [like(part.shape[-2:], F32) for part in sources]
-        scratch = scatter_scratch(pieces, [(part.shape[-2], BF16) for part in sources], [False, False])
-    cross_shapes += gate_shapes
-    gmem, gfirst, gm1, ggain_cross, dwo, dcq, dck, dcv, dco, *feed_grads = pl.pallas_call(
+        scratch = scatter_scratch(pieces, [(part.shape[-2], BF16) for part in sources], [False] * 3)
+    moved = Moves.scratch([*cross_in, *attention[3:], *cross_shapes])
+    gmem, gfirst, gm1, dwo, dcq, dck, dcv, dco, *feed_grads = pl.pallas_call(
         functools.partial(cross_backward_kernel, heads=heads, plan=plan),
-        out_shape=cross_shapes,
+        out_shape=cross_shapes + gate_shapes,
         grid=(1,),
-        in_specs=[full(a.shape) for a in cross_in] + [full((width, width))] * 5 + [remote] * len(sources),
-        out_specs=[full(o.shape) for o in cross_shapes],
-        scratch_shapes=cross_scratch + scratch,
+        in_specs=[remote] * (CROSS_INS + len(sources)),
+        out_specs=[remote] * CROSS_OUTS + [full(o.shape) for o in gate_shapes],
+        scratch_shapes=moved + cross_scratch + scratch,
         compiler_params=params(collective_id=1, has_side_effects=True) if own else params(),
         name="cross_backward",
     )(*cross_in, *attention[3:], *sources)
 
-    self_in = (tokens, gains, bias_table, bucket_map, q1, k1, v1, mixed1, lse1, gm1, gfirst, ggain_cross, ggain_feed)
+    self_in = (bias_table, bucket_map)
+    self_moved = (tokens, gains, lse1, q1, k1, v1, mixed1, gm1, gfirst, *attention[:3])
     self_scratch = vmem(
         ((heads, band.width), F32), ((SUB, band.causal), F32), ((SUB, band.two_way), F32), ((width, length), BF16),
         ((SUB, length), F32), ((8, length), F32), ((length, width), BF16), ((length, width), BF16),
@@ -1230,45 +1521,48 @@
     plan, sources, scratch = None, [], []
     table_shape = like((NB, heads), F32)
     if own:
-        sources = shares([ddown, dco, dwo, dcq, dck, dcv])
-        pieces, groups = self_pieces(width, width)
+        sources = shares([dco, dwo, dcq, dck, dcv])
+        pieces, groups = self_pieces(width)
         plan = (sizes, pieces, groups)
         share = width // devices
         kept = [False] * REST + [True] * 4
         shapes = [(part.shape[-2], BF16) for part in sources] + [(share, BF16)] * 3 + [(TILE, F32)]
         self_shapes = [act32] + [like(part.shape[-2:], F32) for part in sources] + [like((share, width), F32)] * 3
-        self_shapes += [table_shape] + [like((1, share), F32)] * 3
-        scratch = vmem(*[(grid + (share, width), BF16)] * 3, (grid + (TILE, SUB), F32), ((TILE, SUB), F32), ((8, width), F32))
+        self_shapes += [table_shape]
+        scratch = vmem(*[(grid + (share, width), BF16)] * 3, (grid + (TILE, SUB), F32), ((TILE, SUB), F32))
         scratch += scatter_scratch(pieces, shapes, kept)
     else:
-        self_shapes = [act32, ggain_shape, table_shape] + [square] * 3
+        self_shapes = [act32, table_shape] + [square] * 3
     gtokens, *grads = pl.pallas_call(
         functools.partial(self_backward_kernel, band=band, heads=heads, plan=plan),
         out_shape=self_shapes,
         grid=(1,),
-        in_specs=[scalar] + [full(a.shape) for a in self_in] + [full((width, width))] * 3 + [remote] * len(sources),
+        in_specs=[scalar] + [full(a.shape) for a in self_in] + [remote] * (SELF_INS + len(sources)),
         out_specs=[full(o.shape) for o in self_shapes],
-        scratch_shapes=self_scratch + scratch,
+        scratch_shapes=Moves.scratch(self_moved) + self_scratch + scratch,
         compiler_params=params(collective_id=2, has_side_effects=True) if own else params(),
         name="self_backward",
-    )(prefix, *self_in, *attention[:3], *sources)
-
+    )(prefix, *self_in, *self_moved, *sources)
+
+    gain_parts = (norm_self, norm_cross, norm_feed)
+    weight_parts = (self_query, self_key, self_value, cross_query, feed_gate, feed_up)
     if own:
-        gtokens, gmem, dgate, dup, *grads = hand_on([gtokens, gmem, *feed_grads, *grads])
-        ddown, dco, dwo, dcq, dck, dcv, dwq, dwk, dwv, table_grad, *ggains = grads
-        ggains = [ggain.reshape(-1) for ggain in ggains]
+        results = [gtokens, output, gmem, (low_grads[0], feed_grads[0]), (low_grads[1], feed_grads[1]), feed_grads[2]]
+        results, ggains = hand_on([*results, *grads], (11, 12, 13, 8, 3, 4), gain_parts, weight_parts)
+        gtokens, output, gmem, dgate, dup, ddown, dco, dwo, dcq, dck, dcv, dwq, dwk, dwv, table_grad = results
     else:
-        ggain_self, gtable, dwq, dwk, dwv = grads
+        gtable, dwq, dwk, dwv = grads
         table_grad = lax.psum(gtable, AXES)
 
-        def scatter(parts, axis):
-            return lax.psum_scatter(jnp.concatenate(parts, axis=1 - axis), AXES, scatter_dimension=axis, tiled=True)
-
-        ggains = scatter([ggain_self[:1], ggain_cross[:1], ggain_feed[:1]], 1)
-        dgate, dup = jnp.split(scatter([dgate, dup], 0).astype(F32), 2, axis=1)
-        ddown = scatter([ddown], 0).astype(F32)
-        squares = scatter([dwq, dwk, dwv, dwo, dcq, dck, dcv, dco], 0).astype(F32)
+        def scatter(parts):
+            return lax.psum_scatter(jnp.concatenate(parts, axis=1), AXES, scatter_dimension=0, tiled=True).astype(F32)
+
+        dgate, dup = jnp.split(scatter([dgate, dup]), 2, axis=1)
+        ddown = scatter([ddown])
+        squares = scatter([dwq, dwk, dwv, dwo, dcq, dck, dcv, dco])
         dwq, dwk, dwv, dwo, dcq, dck, dcv, dco = jnp.split(squares, 8, axis=1)
+        parts = gain_grads([gain.reshape(1, -1) for gain in gain_parts], weight_parts, (dwq, dwk, dwv, dcq, dgate, dup))
+        ggains = [part.reshape(-1) for part in parts]
     return (
         output.reshape(inputs.shape),
         gtokens.reshape(inputs.shape),

time: 329 us -> 307 us (0.933)
  Pallas kernels: 320 us -> 297 us
    pallas_call x1, Pallas kernels: 124 us -> 106 us  [per_device(): pl.pallas_call(functools.partial(forward_kernel, band=band, heads=heads,...]
    pallas_call x2, Pallas kernels: 50.1 us -> 65.9 us  [the longest x1 59 us: per_device(): pl.pallas_call(functools.partial(feed_exchange_kernel, plan=(sizes, gathe...]
    pallas_call x1, Pallas kernels: 89.7 us -> 75.9 us  [per_device(): pl.pallas_call(functools.partial(self_backward_kernel, band=band, heads=h...]
    pallas_call x1, Pallas kernels: 55.9 us -> 49.7 us  [per_device(): pl.pallas_call(functools.partial(cross_backward_kernel, heads=heads, plan...]
where the time goes in v5:
time: 307 us; the launch traced here: 302 us
  Pallas kernels  297 us (97%)
    pallas_call x1, Pallas kernels, per_device(): pl.pallas_call(functools.partial(forward_kernel, band=band, heads=heads,...  106 us
    pallas_call x1, Pallas kernels, per_device(): pl.pallas_call(functools.partial(self_backward_kernel, band=band, heads=h...  75.9 us
    pallas_call x1, Pallas kernels, per_device(): pl.pallas_call(functools.partial(feed_exchange_kernel, plan=(sizes, gathe...  59 us
    pallas_call x1, Pallas kernels, per_device(): pl.pallas_call(functools.partial(cross_backward_kernel, heads=heads, plan...  49.7 us
    pallas_call x1, Pallas kernels, hand_on(): pl.pallas_call(functools.partial(hand_on_kernel, places=places, norms=nor...  6.86 us

profile of v5, /device:TPU:0, one launch (start us, length us, event | category | flops | bytes accessed | tf_op | source)
XLA Modules:
  0.0 301.8 jit_solution(2259779650182764114)
XLA Ops:
  1.3 1.4 copy.41.table_ref
  2.7 105.7 %forward.1 = (bf16[4,2,2,48,768]{4,3,2,1,0:T(8,128)(2,1)}, bf16[4,2,2,48,768]{4,3,2,1,0:T(8,128)(2,1)}, bf16[4,2,2,48,768]{4,3,2,1,0:T(8,128)(2,1)}, bf16[4,2,2,...) custom-call(s32[1]{0:T(128)S(6)} %copy.45.limit_ref, ...), custom_call_target="tpu_custom_call" | custom-call | tf_op jit(solution)/shard_map/forward/pallas_call | solution.py:1390
  108.4 59.0 %feed.1 = (bf16[1024,768]{1,0:T(8,128)(2,1)}, f32[1024,768]{1,0:T(8,128)}, bf16[2048,768]{1,0:T(8,128)(2,1)}, bf16[4,2,2,2,24,1024]{5,4,3,2,1,0:T(8,128)(2,1)}, ...) custom-call(f32[1024,768]{1,0:T(8,128)} %get-tuple-element.96.refs_0, ...), custom_call_target="tpu_custom_call", output_to_operand_aliasing={{7}: (6, {}), {8}: (7, {})} | custom-call | tf_op jit(solution)/shard_map/feed/pallas_call | solution.py:1437
  167.4 49.7 %cross_backward.1 = (f32[512,768]{1,0:T(8,128)}, f32[1024,768]{1,0:T(8,128)}, bf16[1024,768]{1,0:T(8,128)(2,1)}, bf16[768,768]{1,0:T(8,128)(2,1)}, bf16[768,768]...) custom-call(f32[1024,768]{1,0:T(8,128)} %get-tuple-element.102.refs_, ...), custom_call_target="tpu_custom_call" | custom-call | tf_op jit(solution)/shard_map/cross_backward/pallas_call | solution.py:1502
  217.2 75.9 %self_backward.1 = (f32[1024,768]{1,0:T(8,128)}, f32[24,768]{1,0:T(8,128)}, f32[24,768]{1,0:T(8,128)}, f32[24,768]{1,0:T(8,128)}, f32[24,768]{1,0:T(8,128)}, /*i...) custom-call(s32[1]{0:T(128)S(6)} %copy.45.limit_ref, ...), custom_call_target="tpu_custom_call" | custom-call | tf_op jit(solution)/shard_map/self_backward/pallas_call | solution.py:1536
  293.1 6.9 %hand_on.1 = (f32[1024,768]{1,0:T(8,128)}, bf16[1024,768]{1,0:T(8,128)(2,1)}, f32[512,768]{1,0:T(8,128)}, f32[24,2048]{1,0:T(8,128)}, f32[24,2048]{1,0:T(8,128)}...) custom-call(bf16[1,24]{1,0:T(2,128)(2,1)} %bitcast.52, ...), custom_call_target="tpu_custom_call" | custom-call | tf_op jit(solution)/shard_map/hand_on/pallas_call | solution.py:1311
  300.0 1.4 copy.42

commit v6 on v5

--- a/solution.py
+++ b/solution.py
@@ -302,10 +302,13 @@
                     view = sums.at[z, :, at["x"]] if order[0] == "x" else sums.at[z, at["y"]]
                 else:
                     view = sums.at[z, at["y"], at["x"]]
-            total = view[...].astype(F32)
-            for part in parts:
-                total += part.astype(F32)
-            view[...] = total.astype(view.dtype)
+            if len(parts) == 1:
+                view[...] = view[...] + parts[0]
+            else:
+                total = view[...].astype(F32)
+                for part in parts:
+                    total += part.astype(F32)
+                view[...] = total.astype(view.dtype)
 
     def advance(self, numbers, phase):
         for number in numbers:
@@ -390,7 +393,7 @@
 
 def bias_rows(table_ref, map_ref, band, rows):
     hot, causal = one_hot(map_ref, band, rows)
-    bias = dot(table_ref[...], hot.astype(BF16), 0, 0)
+    bias = dot(table_ref[...], hot.astype(BF16))
     return jnp.concatenate([jnp.where(causal < 0, NEG, bias[:, : band.causal]), bias[:, band.causal :]], axis=1)
 
 
@@ -809,7 +812,12 @@
             scatter.advance(every, 0)
             gather.advance(upper, 3)
 
-        ddown_ref[units, :] = dot(hidden_ref[...].T, gout_ref[...]).astype(BF16)
+        @pl.loop(0, 2)
+        def _(index):
+            start = pl.multiple_of(index * (columns // 2), columns // 2)
+            flipped = hidden_ref[:, pl.ds(start, columns // 2)].T
+            into = pl.ds(pl.multiple_of(half * columns + start, columns // 2), columns // 2)
+            ddown_ref[into, :] = dot(flipped, gout_ref[...]).astype(BF16)
 
         @pl.when(half == 0)
         def _():
@@ -935,13 +943,18 @@
     if plan:
         sizes, pieces = plan
         scatter = Scatter(Place(sizes), pieces, sources, [False] * count, outs, refs[:-3], *refs[-3:])
-        soon, later = range(len(pieces) // 2), range(len(pieces) // 2, len(pieces))
+        waves = [range(number, number + 2) for number in range(0, len(pieces), 2)]
         scatter.place.greet()
+
+    def advance(*steps):
+        if plan:
+            for wave, phase in steps:
+                scatter.advance(waves[wave], phase)
+
     moves.load(0, 14, 8, 4, 5, 6, 9, 2, 12, 13, 1, 3, 11, 10, 7)
     if plan:
         scatter.place.meet()
-        scatter.advance(soon, 0)
-        scatter.advance(later, 0)
+    advance((0, 0), (1, 0), (2, 0), (3, 0))
     length, width = first_ref.shape
     source = memory_ref.shape[0]
     block = 256
@@ -953,16 +966,15 @@
         flipped_ref[:, rows] = mixed2_ref[rows, :].T
 
     moves.need(0, 14, 8)
-    row_blocks(length, 512, prepare)
+    row_blocks(length, 256, prepare)
 
     def out_grad(rows):
         dco_ref[rows, :] = dot(flipped_ref[rows, :], branch_ref[...]).astype(BF16)
 
-    row_blocks(width, 384, out_grad)
+    row_blocks(width, 192, out_grad)
     moves.store(7)
     moves.need(4, 5, 6, 9)
-    if plan:
-        scatter.advance(soon, 1)
+    advance((0, 1))
     lse_rows_ref[...] = lse_ref[...].T
     gk_ref[...] = jnp.zeros_like(gk_ref)
     gv_ref[...] = jnp.zeros_like(gv_ref)
@@ -970,17 +982,6 @@
 
     @pl.loop(0, groups)
     def _(group):
-        if plan:
-
-            @pl.when(group == groups // 3)
-            def _():
-                scatter.advance(soon, 2)
-                scatter.advance(later, 1)
-
-            @pl.when(group == groups - 2)
-            def _():
-                scatter.advance(soon, 3)
-
         cols = pl.ds(pl.multiple_of(group * PAIR, PAIR), PAIR)
         backward_head_prepare(cols, gm_ref, mixed2_ref, delta_ref)
         gqt_ref[...] = jnp.zeros_like(gqt_ref)
@@ -988,23 +989,29 @@
         @pl.loop(0, 2)
         def _(half):
             head = group * 2 + half
-            for first in range(0, source, block):
+            for when, steps in ((3, ((0, 2), (1, 1))), (7, ((0, 3), (1, 2), (2, 1)))):
+
+                @pl.when(head == when * heads // 12)
+                def _(steps=steps):
+                    advance(*steps)
+
+            @pl.loop(0, source // block)
+            def _(index):
                 backward_block(
-                    pl.ds(first, block), cols, half, 0, None, q_ref, k_ref, v_ref, gm_ref,
+                    pl.ds(pl.multiple_of(index * block, block), block), cols, half, 0, None, q_ref, k_ref, v_ref, gm_ref,
                     lse_rows_ref[pl.ds(head, 1), :], delta_ref[pl.ds(half, 1), :], gk_ref, gv_ref, gqt_ref,
                 )
 
         gq_ref[:, cols] = gqt_ref[...].T.astype(BF16)
 
-    if plan:
-        scatter.advance(later, 2)
+    advance((1, 3), (2, 2), (3, 1))
 
     def memory_grad(rows):
         gmem_ref[rows, :] = dot(gk_ref[rows, :], ck_ref[...], 1, 1) + dot(gv_ref[rows, :], cv_ref[...], 1, 1)
         flipped_ref[:, rows] = memory_ref[rows, :].T
 
     moves.need(2, 12, 13)
-    row_blocks(source, 512, memory_grad)
+    row_blocks(source, 256, memory_grad)
     moves.store(0)
 
     def memory_weights(rows):
@@ -1012,12 +1019,10 @@
         dck_ref[rows, :] = dot(flipped, gk_ref[...]).astype(BF16)
         dcv_ref[rows, :] = dot(flipped, gv_ref[...]).astype(BF16)
 
-    row_blocks(width, 384, memory_weights)
+    row_blocks(width, 192, memory_weights)
     moves.store(5, 6)
     moves.need(1, 3, 11, 10, 7)
-    if plan:
-        scatter.advance(later, 3)
-        scatter.advance(soon, 4)
+    advance((2, 3), (3, 2), (0, 4))
 
     def first_grad(rows):
         value = first_ref[rows, :]
@@ -1029,13 +1034,14 @@
         branch_ref[rows, :] = branch
         gm1_ref[rows, :] = dot(branch, wo_ref[...], 1, 1).astype(BF16)
 
-    row_blocks(length, 512, first_grad)
+    row_blocks(length, 256, first_grad)
     moves.store(1, 2)
+    advance((3, 3), (1, 4))
 
     def query_weights(rows):
         dcq_ref[rows, :] = dot(flipped_ref[rows, :], gq_ref[...]).astype(BF16)
 
-    row_blocks(width, 384, query_weights)
+    row_blocks(width, 192, query_weights)
     moves.store(4)
 
     def flip_mixed(rows):
@@ -1046,10 +1052,9 @@
     def out_weights(rows):
         dwo_ref[rows, :] = dot(flipped_ref[rows, :], branch_ref[...]).astype(BF16)
 
-    row_blocks(width, 384, out_weights)
+    row_blocks(width, 192, out_weights)
     moves.store(3)
-    if plan:
-        scatter.advance(later, 4)
+    advance((2, 4), (3, 4))
     moves.finish()
 
 
@@ -1252,10 +1257,10 @@
         scatter.advance(middle, 4)
         scatter.advance(late, 4)
         scatter.advance(table, 4)
-        gtable_ref[...] = tile_ref[...].T[:NB, :heads]
+        gtable_ref[...] = tile_ref[:heads, :NB]
     else:
         row_blocks(length, block, tokens_grad)
-        gtable_ref[...] = gtable.T
+        gtable_ref[...] = gtable
 
 
 def gain_grads(gains, weights, grads):
@@ -1344,6 +1349,7 @@
     ff = feed_gate.shape[1]
     band = Band(length, length // 2)
     tokens = inputs.reshape(length, width)
+    flipped_table = bias_table.T
     memory = encoded.reshape(source, width)
     gout = out_grad.reshape(length, width)
     gains_in = [norm_self, norm_cross, norm_feed]
@@ -1386,7 +1392,7 @@
         shapes += [(feed_gate.shape[0], ff // 2)] * 2 + [feed_down.shape] + [(feed_gate.shape[0], ff // 2)] * 2
         gathered_shapes = [like(chips + (cores * shape[0], shape[1]), BF16) for shape in shapes]
         gathered_shapes.append(like(chips + (cores * 8, SUB), F32))
-    forward_in = (tokens, memory, bias_table, bucket_map, *gains_in)
+    forward_in = (tokens, memory, flipped_table, bucket_map, *gains_in)
     results = pl.pallas_call(
         functools.partial(forward_kernel, band=band, heads=heads, plan=plan),
         out_shape=gathered_shapes + outs,
@@ -1494,7 +1500,10 @@
     plan, sources, gate_shapes, scratch = None, [], [], []
     if own:
         sources = high_shares + shares([ddown])
-        pieces = [(0, 0, half, "xy"), (1, 0, half, "yx")] + split_columns(2, width)
+        quarter, third = half // 2, width // 3
+        pieces = [(0, 0, quarter, "xy"), (1, 0, quarter, "yx"), (0, quarter, quarter, "xy"), (1, quarter, quarter, "yx")]
+        pieces += [(2, 0, third, "xy"), (2, third, third, "yx")]
+        pieces += [(2, 2 * third, third // 2, "xy"), (2, 2 * third + third // 2, third // 2, "yx")]
         plan = (sizes, pieces)
         gate_shapes = [like(part.shape[-2:], F32) for part in sources]
         scratch = scatter_scratch(pieces, [(part.shape[-2], BF16) for part in sources], [False] * 3)
@@ -1510,7 +1519,7 @@
         name="cross_backward",
     )(*cross_in, *attention[3:], *sources)
 
-    self_in = (bias_table, bucket_map)
+    self_in = (flipped_table, bucket_map)
     self_moved = (tokens, gains, lse1, q1, k1, v1, mixed1, gm1, gfirst, *attention[:3])
     self_scratch = vmem(
         ((heads, band.width), F32), ((SUB, band.causal), F32), ((SUB, band.two_way), F32), ((width, length), BF16),
@@ -1519,7 +1528,7 @@
         ((heads, band.width), F32),
     )
     plan, sources, scratch = None, [], []
-    table_shape = like((NB, heads), F32)
+    table_shape = like((heads, NB), F32)
     if own:
         sources = shares([dco, dwo, dcq, dck, dcv])
         pieces, groups = self_pieces(width)
@@ -1567,7 +1576,7 @@
         output.reshape(inputs.shape),
         gtokens.reshape(inputs.shape),
         gmem.reshape(encoded.shape),
-        table_grad,
+        table_grad.T,
         ggains[0], dwq, dwk, dwv, dwo,
         ggains[1], dcq, dck, dcv, dco,
         ggains[2], dgate, dup, ddown,

time: 307 us -> 301 us (0.980); the launches traced: 302 us -> 300 us
  no operation moved by 1% of the time
where the time goes in v6:
time: 301 us; the launch traced here: 300 us
  Pallas kernels  299 us (99%)
    pallas_call x1, Pallas kernels, per_device(): pl.pallas_call(functools.partial(forward_kernel, band=band, heads=heads,...  106 us
    pallas_call x1, Pallas kernels, per_device(): pl.pallas_call(functools.partial(self_backward_kernel, band=band, heads=h...  76 us
    pallas_call x1, Pallas kernels, per_device(): pl.pallas_call(functools.partial(feed_exchange_kernel, plan=(sizes, gathe...  59.1 us
    pallas_call x1, Pallas kernels, per_device(): pl.pallas_call(functools.partial(cross_backward_kernel, heads=heads, plan...  51.1 us
    pallas_call x1, Pallas kernels, hand_on(): pl.pallas_call(functools.partial(hand_on_kernel, places=places, norms=nor...  6.86 us

profile of v6, /device:TPU:0, one launch (start us, length us, event | category | flops | bytes accessed | tf_op | source)
XLA Modules:
  0.0 300.5 jit_solution(16789316536520627195)
XLA Ops:
  1.3 105.9 %forward.1 = (bf16[4,2,2,48,768]{4,3,2,1,0:T(8,128)(2,1)}, bf16[4,2,2,48,768]{4,3,2,1,0:T(8,128)(2,1)}, bf16[4,2,2,48,768]{4,3,2,1,0:T(8,128)(2,1)}, bf16[4,2,2,...) custom-call(s32[1]{0:T(128)S(6)} %copy.42.limit_ref, ...), custom_call_target="tpu_custom_call" | custom-call | tf_op jit(solution)/shard_map/forward/pallas_call | solution.py:1396
  107.2 59.1 %feed.1 = (bf16[1024,768]{1,0:T(8,128)(2,1)}, f32[1024,768]{1,0:T(8,128)}, bf16[2048,768]{1,0:T(8,128)(2,1)}, bf16[4,2,2,2,24,1024]{5,4,3,2,1,0:T(8,128)(2,1)}, ...) custom-call(f32[1024,768]{1,0:T(8,128)} %get-tuple-element.96.refs_0, ...), custom_call_target="tpu_custom_call", output_to_operand_aliasing={{7}: (6, {}), {8}: (7, {})} | custom-call | tf_op jit(solution)/shard_map/feed/pallas_call | solution.py:1443
  166.3 51.1 %cross_backward.1 = (f32[512,768]{1,0:T(8,128)}, f32[1024,768]{1,0:T(8,128)}, bf16[1024,768]{1,0:T(8,128)(2,1)}, bf16[768,768]{1,0:T(8,128)(2,1)}, bf16[768,768]...) custom-call(f32[1024,768]{1,0:T(8,128)} %get-tuple-element.102.refs_, ...), custom_call_target="tpu_custom_call" | custom-call | tf_op jit(solution)/shard_map/cross_backward/pallas_call | solution.py:1511
  217.4 76.0 %self_backward.1 = (f32[1024,768]{1,0:T(8,128)}, f32[24,768]{1,0:T(8,128)}, f32[24,768]{1,0:T(8,128)}, f32[24,768]{1,0:T(8,128)}, f32[24,768]{1,0:T(8,128)}, /*i...) custom-call(s32[1]{0:T(128)S(6)} %copy.42.limit_ref, ...), custom_call_target="tpu_custom_call" | custom-call | tf_op jit(solution)/shard_map/self_backward/pallas_call | solution.py:1545
  293.4 6.9 %hand_on.1 = (f32[1024,768]{1,0:T(8,128)}, bf16[1024,768]{1,0:T(8,128)(2,1)}, f32[512,768]{1,0:T(8,128)}, f32[24,2048]{1,0:T(8,128)}, f32[24,2048]{1,0:T(8,128)}...) custom-call(bf16[1,24]{1,0:T(2,128)(2,1)} %bitcast.56, ...), custom_call_target="tpu_custom_call" | custom-call | tf_op jit(solution)/shard_map/hand_on/pallas_call | solution.py:1316

commit v7 on v6

--- a/solution.py
+++ b/solution.py
@@ -557,7 +557,7 @@
         place.meet()
     advance(("qk", 0), ("v", 0), ("memory", 0))
     advance(("v", 1), ("qk", 1), ("qk", 2), ("v", 2), ("out", 0))
-    advance(("qk", 3), ("v", 3), ("qk", 4), ("v", 4), ("memory", 1), ("out", 1), ("gate", 0), ("down", 0), ("upper", 0))
+    advance(("qk", 3), ("v", 3), ("qk", 4), ("v", 4), ("memory", 1), ("out", 1), ("gate", 0), ("down", 0))
     for number in range(3):
         load(number).start()
     if plan:
@@ -590,10 +590,11 @@
         self_forward_head(head, limit_ref[0], q1_ref, k1_ref, v1_ref, causal_ref, two_ref, band, mixed1_ref, lse1_ref)
 
         for when, steps in (
-            (1, (("out", 3), ("memory", 2))),
+            (2, (("out", 3),)),
+            (3, (("memory", 2),)),
             (4, (("out", 4), ("down", 1))),
             (6, (("memory", 3),)),
-            (8, (("memory", 4), ("gate", 1))),
+            (8, (("memory", 4), ("gate", 1), ("upper", 0))),
         ):
 
             @pl.when(head == when * heads // 12)
@@ -1164,7 +1165,7 @@
         def _(half):
             head = group * 2 + half
             if plan:
-                for when, numbers, phase in ((1, first, 1), (4, rest, 1), (5, first, 2), (8, first, 3), (9, early, 1), (11, rest, 2)):
+                for when, numbers, phase in ((1, first, 1), (3, rest, 1), (5, first, 2), (8, first, 3), (9, rest, 2), (10, early, 1), (11, rest, 3)):
 
                     @pl.when(head == when * heads // 12)
                     def _(numbers=numbers, phase=phase):
@@ -1214,7 +1215,6 @@
         weights(parts[2])
         scatter.advance(late, 0)
         scatter.advance(early, 2)
-        scatter.advance(rest, 3)
     else:
         for part in parts:
             weights(part)

time: 301 us -> 292 us (0.970)
  Pallas kernels: 299 us -> 291 us
    pallas_call x1, Pallas kernels: 59.1 us -> 53.7 us  [per_device(): pl.pallas_call(functools.partial(feed_exchange_kernel, plan=(sizes, gathe...]
where the time goes in v7:
time: 292 us
  Pallas kernels  291 us (100%)
    pallas_call x1, Pallas kernels, per_device(): pl.pallas_call(functools.partial(forward_kernel, band=band, heads=heads,...  105 us
    pallas_call x1, Pallas kernels, per_device(): pl.pallas_call(functools.partial(self_backward_kernel, band=band, heads=h...  75.1 us
    pallas_call x1, Pallas kernels, per_device(): pl.pallas_call(functools.partial(feed_exchange_kernel, plan=(sizes, gathe...  53.7 us
    pallas_call x1, Pallas kernels, per_device(): pl.pallas_call(functools.partial(cross_backward_kernel, heads=heads, plan...  50.2 us
    pallas_call x1, Pallas kernels, hand_on(): pl.pallas_call(functools.partial(hand_on_kernel, places=places, norms=nor...  6.86 us

profile of v7, /device:TPU:0, one launch (start us, length us, event | category | flops | bytes accessed | tf_op | source)
XLA Modules:
  0.0 292.2 jit_solution(17971840812501790625)
XLA Ops:
  1.3 104.7 %forward.1 = (bf16[4,2,2,48,768]{4,3,2,1,0:T(8,128)(2,1)}, bf16[4,2,2,48,768]{4,3,2,1,0:T(8,128)(2,1)}, bf16[4,2,2,48,768]{4,3,2,1,0:T(8,128)(2,1)}, bf16[4,2,2,...) custom-call(s32[1]{0:T(128)S(6)} %copy.42.limit_ref, ...), custom_call_target="tpu_custom_call" | custom-call | tf_op jit(solution)/shard_map/forward/pallas_call | solution.py:1396
  106.0 53.7 %feed.1 = (bf16[1024,768]{1,0:T(8,128)(2,1)}, f32[1024,768]{1,0:T(8,128)}, bf16[2048,768]{1,0:T(8,128)(2,1)}, bf16[4,2,2,2,24,1024]{5,4,3,2,1,0:T(8,128)(2,1)}, ...) custom-call(f32[1024,768]{1,0:T(8,128)} %get-tuple-element.96.refs_0, ...), custom_call_target="tpu_custom_call", output_to_operand_aliasing={{7}: (6, {}), {8}: (7, {})} | custom-call | tf_op jit(solution)/shard_map/feed/pallas_call | solution.py:1443
  159.7 50.2 %cross_backward.1 = (f32[512,768]{1,0:T(8,128)}, f32[1024,768]{1,0:T(8,128)}, bf16[1024,768]{1,0:T(8,128)(2,1)}, bf16[768,768]{1,0:T(8,128)(2,1)}, bf16[768,768]...) custom-call(f32[1024,768]{1,0:T(8,128)} %get-tuple-element.102.refs_, ...), custom_call_target="tpu_custom_call" | custom-call | tf_op jit(solution)/shard_map/cross_backward/pallas_call | solution.py:1511
  209.9 75.1 %self_backward.1 = (f32[1024,768]{1,0:T(8,128)}, f32[24,768]{1,0:T(8,128)}, f32[24,768]{1,0:T(8,128)}, f32[24,768]{1,0:T(8,128)}, f32[24,768]{1,0:T(8,128)}, /*i...) custom-call(s32[1]{0:T(128)S(6)} %copy.42.limit_ref, ...), custom_call_target="tpu_custom_call" | custom-call | tf_op jit(solution)/shard_map/self_backward/pallas_call | solution.py:1545
  285.1 6.9 %hand_on.1 = (f32[1024,768]{1,0:T(8,128)}, bf16[1024,768]{1,0:T(8,128)(2,1)}, f32[512,768]{1,0:T(8,128)}, f32[24,2048]{1,0:T(8,128)}, f32[24,2048]{1,0:T(8,128)}...) custom-call(bf16[1,24]{1,0:T(2,128)(2,1)} %bitcast.56, ...), custom_call_target="tpu_custom_call" | custom-call | tf_op jit(solution)/shard_map/hand_on/pallas_call | solution.py:1316
